TPU v7x, 32 devices: a whole 2x2x4 slice. The times are simulated.
32 devices in a mesh: member: 2 (over y), tile: 4 (over z), day: 4 (over x, core).
Axes of the slice: x: 2, y: 2, z: 4, core: 2. Of those that a mesh axis runs over, the one named last changes fastest.
Arguments:
- fields: bfloat16 [64, 35, 16384], P(('member', 'day'), None, 'tile'), parts along dimension 0, may hold values from -6 to 6
- remap_tiles: bfloat16 [512, 128, 128], P('tile'), may hold values from 0 to 0.015625
- tile_source: int32 [512], P('tile'), may hold values from 0 to 31, as said below
- tile_band: int32 [512, 1], P('tile'), may hold values from 0 to 3, as said below
- tile_block: int32 [512], P('tile'), may hold values from 0 to 35, as said below
- patterns: bfloat16 [18432, 512], P('tile'), may hold values from -0.125 to 0.125
Outputs:
- scores: float32 [64, 35, 512], P(('member', 'day'), None, 'tile'), parts along dimension 0
There are 2 independent parts, one for each index of `member`. A program takes and returns all parts, laid end to end along the dimension named above; an argument that names none is the same for every part. Nothing has to cross between parts.
Inputs may be any that keep to these rules, and one draw needn't show every extreme that they name: `tile_source`: index of the source block, among the 32 blocks held by the tile's own device; each of those blocks is read by some tile of that device. `tile_band`: among the 128 tiles of one device, at most 64 go to one band, and in some device exactly 64 do. `tile_block`: every target block of every band is written by at least one tile.
All inputs are finite; a program needn't handle non-finite values.
Results may differ from a plain program's by a relative error of at most 0.0039.
Values may be sent and summed in bfloat16 or wider, within the bound.
No kernel may reach another device: no remote copies, remote signals or barrier semaphores. Data moves between devices by JAX's collectives and lax.ppermute only.
A program may use at most 128 MiB of HBM per device.

v0:
```python
import jax
import jax.numpy as jnp
from jax import lax
from jax.sharding import PartitionSpec as P


def on_device(fields, remap_tiles, tile_source, tile_band, tile_block, patterns):
    band_count = lax.axis_size("tile")
    day_count, var_count, source_cells = fields.shape
    tile_count, block_size, _ = remap_tiles.shape
    row_count = day_count * var_count
    source_blocks = source_cells // block_size
    target_blocks = patterns.shape[0] // block_size
    pattern_count = patterns.shape[1]
    pattern_share = pattern_count // band_count
    capacity = max(2, 2 * tile_count // band_count)
    slot_count = band_count * capacity
    blocked = fields.reshape(row_count, source_blocks, block_size)
    columns = jnp.take(blocked, tile_source, axis=1)
    owner = tile_band[:, 0]
    tile_order = jnp.arange(tile_count, dtype=jnp.int32)
    same_owner = owner[:, None] == owner[None, :]
    earlier = tile_order[:, None] > tile_order[None, :]
    rank_within = jnp.sum(jnp.logical_and(same_owner, earlier).astype(jnp.int32), axis=1)
    slot_index = owner * capacity + rank_within
    block_label = (
        jnp.full((slot_count,), -1.0, jnp.bfloat16)
        .at[slot_index]
        .set(tile_block.astype(jnp.bfloat16))
    )
    contrib = jnp.einsum(
        "rtk,tkj->trj", columns, remap_tiles, preferred_element_type=jnp.float32
    ).astype(jnp.bfloat16)
    send_values = (
        jnp.zeros((slot_count, row_count, block_size), jnp.bfloat16).at[slot_index].set(contrib)
    )
    received, label_recv = (
        lax.all_to_all(send_values, "tile", split_axis=0, concat_axis=0, tiled=True),
        lax.all_to_all(block_label, "tile", split_axis=0, concat_axis=0, tiled=True),
    )
    block_ids = jnp.arange(target_blocks, dtype=jnp.int32).astype(jnp.bfloat16)
    selector = (label_recv[None, :] == block_ids[:, None]).astype(jnp.bfloat16)
    remapped = jnp.einsum("bs,srk->rbk", selector, received, preferred_element_type=jnp.float32)
    remapped = remapped.astype(jnp.bfloat16).reshape(row_count, target_blocks * block_size)
    partial_scores = jnp.dot(remapped, patterns, preferred_element_type=jnp.float32)
    total_scores = lax.psum(partial_scores, "tile")
    own_scores = lax.dynamic_slice_in_dim(
        total_scores, lax.axis_index("tile") * pattern_share, pattern_share, 1
    )
    return own_scores.reshape(day_count, var_count, pattern_share)


def solution(mesh):
    return jax.shard_map(
        on_device,
        mesh=mesh,
        in_specs=(
            P(("member", "day"), None, "tile"),
            P("tile", None, None),
            P("tile"),
            P("tile", None),
            P("tile"),
            P("tile", None),
        ),
        out_specs=P(("member", "day"), None, "tile"),
        check_vma=False,
    )
```

profile of v0, /device:TPU:0, one launch (start us, length us, event | category | flops | bytes accessed | tf_op | source)
XLA Modules:
  0.0 542.5 jit_solution(3007958193052604485)
XLA Ops:
  6.5 0.9 convert_reduce_fusion
  7.4 0.7 fusion.21
  8.1 0.7 convert_element_type.25
  8.8 1.3 scatter_custom_fusion.1
  10.1 0.7 all_to_all.12
  10.8 6.3 %all-to-all-start.1 = ((bf16[4,64,1]{1,2,0:T(2,128)(2,1)}), bf16[4,64,1]{1,2,0:T(2,128)(2,1)S(1)}, u32[]{:S(2)}, u32[]{:S(2)}) async-start(bf16[4,64,1]{1,2,0:T(2,128)(2,1)} %all_to_all.12), calls=%async_computation.1 | async-start | bytes 4096 | tf_op jit(solution)/shard_map/all_to_all | solution.py:39
  17.1 0.7 compare_select_fusion
  17.8 0.7 compare_and_fusion
  18.4 2.9 copy.16
  21.4 2.6 reshape.24
  24.0 2.5 copy.17
  26.5 7.1 %gather_fusion = bf16[128,280,128]{2,1,0:T(8,128)(2,1)} fusion(bf16[280,32,128]{2,0,1:T(8,128)(2,1)S(1)} %copy.17, s32[1024]{0:T(1024)S(1)} %pad_clamp_fusion), kind=kCustom, calls=%fused_computation | custom fusion | bytes 18350592 | tf_op jit(solution)/shard_map/jit(_take)/gather | solution.py:19
  33.6 13.4 %fusion.6 = bf16[128,280,128]{2,1,0:T(8,128)(2,1)} fusion(bf16[128,128,128]{2,1,0:T(8,128)(2,1)} %param.7, bf16[128,280,128]{2,1,0:T(8,128)(2,1)} %gather_fusion, pred[128]{0:T(512)(128)(4,1)S(1)} %compare_and_fusion), kind=kOutput, calls=%fused_computation.9 | convolution fusion | flops 1183580160 | bytes 22544512 | tf_op jit(solution)/shard_map/rtk,tkj->trj/dot_general | solution.py:31
  46.9 6.6 %broadcast_in_dim.24 = bf16[256,280,128]{2,1,0:T(8,128)(2,1)} broadcast(bf16[]{:T(256)} %constant.12.clone.1), dimensions={} | broadcast | bytes 18350082 | tf_op jit(solution)/shard_map/broadcast_in_dim | solution.py:35
  53.5 24.2 %scatter_fusion = bf16[256,280,128]{2,1,0:T(8,128)(2,1)} fusion(bf16[256,280,128]{2,1,0:T(8,128)(2,1)} %broadcast_in_dim.24, s32[128]{0:T(128)S(1)} %fusion.21, bf16[128,280,128]{2,1,0:T(8,128)(2,1)} %fusion.6), kind=kCustom, calls=%fused_computation.1 | custom fusion | bytes 27525632 | tf_op jit(solution)/shard_map/scatter | solution.py:35
  77.7 0.0 all-to-all-done.1
  77.7 7.3 %all-to-all-start = ((bf16[256,280,128]{2,1,0:T(8,128)(2,1)}), bf16[256,280,128]{2,1,0:T(8,128)(2,1)}, u32[]{:S(2)}, u32[]{:S(2)}) async-start(bf16[256,280,128]{2,1,0:T(8,128)(2,1)} %scatter_fusion), calls=%async_computation | async-start | bytes 36700160 | tf_op jit(solution)/shard_map/all_to_all | solution.py:38
  85.0 0.2 all-reduce.2.cloned.1.call-start
  85.3 0.1 eq.34
  85.4 396.3 %all-to-all-done = bf16[256,280,128]{2,1,0:T(8,128)(2,1)} async-done(((bf16[256,280,128]{2,1,0:T(8,128)(2,1)}), bf16[256,280,128]{2,1,0:T(8,128)(2,1)}, u32[]{:S(2)}, u32[]{:S(2)}) %all-to-all-start) | async-done | bytes 18350112 | tf_op jit(solution)/shard_map/all_to_all | solution.py:38
  481.7 9.4 %fusion.13 = bf16[280,128,36]{1,2,0:T(8,128)(2,1)S(1)} fusion(bf16[256,280,128]{2,1,0:T(8,128)(2,1)} %all-to-all-done, bf16[256]{0:T(256)(128)(2,1)S(1)} %eq.34, bf16[36]{0:T(256)(128)(2,1)S(1)} %iota_convert_fusion), kind=kOutput, calls=%fused_computation.14 | convolution fusion | flops 661902336 | bytes 20931144 | tf_op jit(solution)/shard_map/bs,srk->rbk/dot_general | solution.py:43
  491.1 4.7 fusion.10
  495.8 0.0 all-reduce.2.cloned.1.call-update
  495.8 38.2 %all-reduce.2.cloned.1.call-done = f32[280,512]{1,0:T(8,128)} async-done(((f32[280,512]{1,0:T(8,128)}), f32[280,512]{1,0:T(8,128)}) %all-reduce.2.cloned.1.call-update) | async-done | bytes 573456 | tf_op jit(solution)/shard_map/psum | solution.py:46
  534.0 0.9 constant_dynamic-slice_fusion
  534.9 0.7 copy.20
  (4 shorter events, 0.0 us)
Async XLA Ops:
  10.8 67.0 %all-to-all-start.1 = ((bf16[4,64,1]{1,2,0:T(2,128)(2,1)}), bf16[4,64,1]{1,2,0:T(2,128)(2,1)S(1)}, u32[]{:S(2)}, u32[]{:S(2)}) async-start(bf16[4,64,1]{1,2,0:T(2,128)(2,1)} %all_to_all.12), calls=%async_computation.1 | async-start | bytes 4096 | tf_op jit(solution)/shard_map/all_to_all | solution.py:39
  77.7 404.0 %all-to-all-start = ((bf16[256,280,128]{2,1,0:T(8,128)(2,1)}), bf16[256,280,128]{2,1,0:T(8,128)(2,1)}, u32[]{:S(2)}, u32[]{:S(2)}) async-start(bf16[256,280,128]{2,1,0:T(8,128)(2,1)} %scatter_fusion), calls=%async_computation | async-start | bytes 36700160 | tf_op jit(solution)/shard_map/all_to_all | solution.py:38
  85.0 449.0 %all-reduce.2.cloned.1.call-start = ((), (), s32[]{:S(2)}) async-start(), calls=%async_computation.2 | async-start | bytes 1146880 | tf_op jit(solution)/shard_map/psum | solution.py:46
Sparse Core Ops, SparseCore 0:
  495.9 38.0 all-reduce.1
where the time goes:
time: 543 us; the launch traced here: 542 us
  waiting for transfers between devices  434 us (80%)
  local copies, waits for them, and re-layouts  49.6 us (9%)
  matrix products  27.5 us (5%)
  starting transfers between devices  13.8 us (3%)
  between operations  13.5 us (2%)
    all_to_all x1, waiting for transfers between devices, on_device(): lax.all_to_all(send_values, 'tile', split_axis=0, concat_axis=0, tiled=True)  396 us
    psum x1, waiting for transfers between devices, on_device(): total_scores = lax.psum(partial_scores, 'tile')  38.2 us
    scatter x1, local copies, waits for them, and re-layouts, on_device(): jnp.zeros((slot_count, row_count, block_size), jnp.bfloat16).at[slot_index]  24.2 us
    dot_general x1, matrix products, on_device(): jnp.einsum('rtk,tkj->trj', columns, remap_tiles, preferred_element_type=j...  13.4 us
  transfers between devices with their start and end apart: 3, of which 2 were waited for; matrix products, arithmetic and copies ran while one was open for 11% of the time, Pallas kernels for 0%

commit v1 on v0

v1 whole, which is shorter than its diff:
```python
import functools

import jax
import jax.numpy as jnp
from jax import lax
from jax.experimental import pallas as pl
from jax.experimental.pallas import tpu as pltpu
from jax.sharding import PartitionSpec as P

PLANE = ("member", "day")
VMEM_LIMIT = 56 * 2**20
LANES = 128


def pack_kernel(place, patterns, packed):
    half = packed.shape[0]
    width = LANES // 2
    offset = lax.rem(place[0], 2) * width
    lane = lax.broadcasted_iota(jnp.int32, (LANES, LANES), 1)

    @pl.loop(0, half)
    def _(j):
        first = patterns[pl.ds(pl.multiple_of(j * LANES, LANES), LANES), :]
        second = patterns[pl.ds(pl.multiple_of((j + half) * LANES, LANES), LANES), :]
        first, second = first.astype(jnp.float32), second.astype(jnp.float32)
        first = pltpu.roll(first, lax.rem(LANES - offset, LANES), 1)
        second = pltpu.roll(second, width - offset, 1)
        packed[j] = jnp.where(lane < width, first, second).astype(packed.dtype)


def pack(patterns, place):
    rows = patterns.shape[0]
    half = rows // LANES // 2
    return pl.pallas_call(
        pack_kernel,
        grid_spec=pltpu.PrefetchScalarGridSpec(
            num_scalar_prefetch=1,
            grid=(1,),
            in_specs=[pl.BlockSpec((rows, LANES), lambda i, place: (0, place[0] // 2))],
            out_specs=pl.BlockSpec((half, LANES, LANES), lambda i, place: (0, 0, 0)),
        ),
        out_shape=jax.ShapeDtypeStruct((half, LANES, LANES), patterns.dtype),
        compiler_params=pltpu.CompilerParams(vmem_limit_bytes=VMEM_LIMIT),
        name="pack",
    )(place, patterns)


def operator_kernel(slots, unroll, place, source, slot, block, weights, *rest):
    bands, packed, held, total, sems = rest[:-4], rest[-4], rest[-3], rest[-2], rest[-1]
    half = held.shape[1]
    width = LANES // 2
    copies = [
        pltpu.make_async_copy(band, held.at[pl.ds(i * slots, slots)], sems.at[i])
        for i, band in enumerate(bands)
    ]
    for copy in copies:
        copy.start()
    total[...] = jnp.zeros_like(total)
    for copy in copies:
        copy.wait()
    lane = lax.broadcasted_iota(jnp.int32, (LANES, LANES), 1)
    tiles = weights.shape[0]

    @pl.loop(0, tiles // unroll)
    def _(step):
        products = []
        for u in range(unroll):
            t = step * unroll + u
            g = block[t]
            side = g // half
            rhs = held[slot[t], g - side * half]
            keep = (lane // width) == side
            rhs = jnp.where(keep, rhs, jnp.zeros_like(rhs))
            products.append(
                jnp.dot(weights[t], rhs, preferred_element_type=jnp.float32)
            )
        for u in range(unroll):
            s = source[step * unroll + u]
            total[s] += products[u]

    blocks = total.shape[0] // 2
    swap = lax.rem(place[0], 2)

    @pl.loop(0, blocks)
    def _(j):
        first, second = total[j], total[j + blocks]
        first = first + pltpu.roll(first, width, 1)
        second = second + pltpu.roll(second, width, 1)
        packed[j] = jnp.where((lane // width) == swap, first, second).astype(packed.dtype)


def operator(weights, bands, place, source, slot, block, source_blocks, out_dtype):
    tiles = weights.shape[0]
    slots = bands[0].shape[0]
    half = bands[0].shape[1]
    scalar = pl.BlockSpec(memory_space=pltpu.SMEM)
    return pl.pallas_call(
        functools.partial(operator_kernel, slots, 4),
        in_specs=[scalar] * 4
        + [pl.BlockSpec(memory_space=pltpu.VMEM)]
        + [pl.BlockSpec(memory_space=pl.ANY)] * len(bands),
        out_specs=pl.BlockSpec(memory_space=pltpu.VMEM),
        out_shape=jax.ShapeDtypeStruct((source_blocks // 2, LANES, LANES), out_dtype),
        scratch_shapes=[
            pltpu.VMEM((slots * len(bands), half, LANES, LANES), bands[0].dtype),
            pltpu.VMEM((source_blocks, LANES, LANES), jnp.float32),
            pltpu.SemaphoreType.DMA((len(bands),)),
        ],
        compiler_params=pltpu.CompilerParams(vmem_limit_bytes=VMEM_LIMIT),
        name="operator",
    )(place, source, slot, block, weights, *bands)


def score_kernel(place, fields, *rest):
    pieces, outs = rest[:10], rest[10:]
    p, z = place[0], place[1]
    core, chip = lax.rem(p, 2), p // 2
    width = LANES // 2
    depth = fields.shape[1] // 2
    mine = pl.ds(pl.multiple_of(core * depth, depth), depth)
    other = pl.ds(pl.multiple_of((1 - core) * depth, depth), depth)
    own, far, x_own, x_far, y_own, y_far, d0_own, d0_far, d1_own, d1_far = pieces
    rows = depth // LANES
    lane = lax.broadcasted_iota(jnp.int32, (depth, LANES), 1)

    def whole(*parts):
        parts = [part[...].reshape(-1, LANES) for part in parts]
        return parts[0] if len(parts) == 1 else jnp.concatenate(parts, 0)

    sets = [
        (whole(own), whole(far)),
        (whole(x_own), whole(x_far)),
        (whole(y_own), whole(y_far)),
        (whole(d0_own, d1_own), whole(d0_far, d1_far)),
    ]
    for relative, (a, b) in enumerate(sets):
        left = jnp.where(lane < width, a, b)
        right = jnp.where(lane < width, b, a)
        r1 = jnp.dot(fields[:, mine], left, preferred_element_type=jnp.float32)
        r2 = jnp.dot(fields[:, other], right, preferred_element_type=jnp.float32)
        straight = jnp.where(core == 0, r1, r2)
        crossed = jnp.where(core == 0, r2, r1)
        value = straight + pltpu.roll(crossed, width, 1)
        chip_of = chip ^ relative
        if len(outs) == 1:
            outs[0][chip_of] = value.astype(outs[0].dtype)
        else:
            hop = lax.rem(chip_of - z + 4, 4)
            for k, out in enumerate(outs):

                @pl.when(hop == k)
                def _(out=out, value=value):
                    out[...] = value.astype(out.dtype)


def scores(fields, pieces, place, split):
    rows = fields.shape[0]
    vmem = pl.BlockSpec(memory_space=pltpu.VMEM)
    if split:
        out_shape = [jax.ShapeDtypeStruct((rows, LANES), jnp.float32)] + [
            jax.ShapeDtypeStruct((rows, LANES), jnp.bfloat16)
        ] * 3
    else:
        out_shape = [jax.ShapeDtypeStruct((4, rows, LANES), jnp.float32)]
    return pl.pallas_call(
        score_kernel,
        in_specs=[pl.BlockSpec(memory_space=pltpu.SMEM)] + [vmem] * (1 + len(pieces)),
        out_specs=[vmem] * len(out_shape),
        out_shape=out_shape,
        compiler_params=pltpu.CompilerParams(vmem_limit_bytes=VMEM_LIMIT),
        name="scores",
    )(place, fields, *pieces)


def plane_permute(x, to):
    pairs = []
    for m in range(2):
        for a in range(2):
            for c in range(2):
                tm, ta, tc = to(m, a, c)
                pairs.append((m * 4 + a * 2 + c, tm * 4 + ta * 2 + tc))
    return lax.ppermute(x, PLANE, pairs)


def over_core(x):
    return plane_permute(x, lambda m, a, c: (m, a, 1 - c))


def over_x(x):
    return plane_permute(x, lambda m, a, c: (m, 1 - a, c))


def over_y(x):
    return plane_permute(x, lambda m, a, c: (1 - m, a, c))


def on_device(fields, remap_tiles, tile_source, tile_band, tile_block, patterns):
    band_count = lax.axis_size("tile")
    day_count, var_count, source_cells = fields.shape
    row_count = day_count * var_count
    source_blocks = source_cells // LANES
    pattern_count = patterns.shape[1]
    z = lax.axis_index("tile")
    p = lax.axis_index("member") * 4 + lax.axis_index("day")
    place = jnp.stack([p, z]).astype(jnp.int32)
    owner = tile_band[:, 0]
    own = pack(patterns, place)
    if band_count == 4:
        from_left = lax.ppermute(own, "tile", [(i, (i + 1) % 4) for i in range(4)])
        from_right = lax.ppermute(own, "tile", [(i, (i + 3) % 4) for i in range(4)])
        far_right = lax.ppermute(from_right, "tile", [(1, 0), (2, 1)])
        far_left = lax.ppermute(from_left, "tile", [(1, 2), (2, 3)])
        bands = [x[None] for x in (own, from_right, far_right, far_left, from_left)]
        hop = jnp.remainder(owner - z, 4)
        slot = jnp.where(hop == 3, 4, jnp.where((hop == 2) & (z >= 2), 3, hop))
    else:
        bands = [lax.all_gather(own, "tile", axis=0)]
        slot = owner
    piece = operator(
        remap_tiles, bands, place, tile_source, slot.astype(jnp.int32), tile_block,
        source_blocks, patterns.dtype,
    )
    far = over_core(piece)
    x_own, y_own = over_x(piece), over_y(piece)
    cut = piece.shape[0] // 2
    d0_own, d1_own = over_y(x_own[:cut]), over_x(y_own[cut:])
    pieces = [piece, far]
    for part in (x_own, y_own, d0_own, d1_own):
        pieces += [part, over_core(part)]
    rows = fields.reshape(row_count, source_cells)
    parts = scores(rows, pieces, place, band_count == 4)
    if band_count == 4:
        result = parts[0]
        for k in (1, 2, 3):
            moved = lax.ppermute(parts[k], "tile", [(i, (i + k) % 4) for i in range(4)])
            result = result + moved.astype(jnp.float32)
    else:
        partial = parts[0].transpose(1, 0, 2).reshape(row_count, pattern_count)
        result = lax.psum_scatter(partial, "tile", scatter_dimension=1, tiled=True)
    return result.reshape(day_count, var_count, pattern_count // band_count)


def solution(mesh):
    return jax.shard_map(
        on_device,
        mesh=mesh,
        in_specs=(
            P(("member", "day"), None, "tile"),
            P("tile", None, None),
            P("tile"),
            P("tile", None),
            P("tile"),
            P("tile", None),
        ),
        out_specs=P(("member", "day"), None, "tile"),
        check_vma=False,
    )
```

time: 543 us -> 111 us (0.20)
  waiting for transfers between devices: 434 us -> 59.5 us
  local copies, waits for them, and re-layouts: 49.6 us -> 6.15 us
  matrix products: 27.5 us -> 0 us
  Pallas kernels: 0 us -> 24.8 us
  between operations: 13.5 us -> 0.13 us
    all_to_all x2 -> x0, waiting for transfers between devices: 396 us -> none  [the longest x1 396 us: on_device(): lax.all_to_all(send_values, 'tile', split_axis=0, concat_axis=0, tiled=True)]
    ppermute x0 -> x16, waiting for transfers between devices: none -> 59.5 us  [the longest x9 16.3 us: plane_permute(): return lax.ppermute(x, PLANE, pairs)]
    psum x1 -> x0, waiting for transfers between devices: 38.2 us -> none  [on_device(): total_scores = lax.psum(partial_scores, 'tile')]
    dot_general x3 -> x0, matrix products: 27.5 us -> none  [the longest x1 13.4 us: on_device(): jnp.einsum('rtk,tkj->trj', columns, remap_tiles, preferred_element_type=j...]
    scatter x2 -> x0, local copies, waits for them, and re-layouts: 25.6 us -> none  [the longest x1 24.2 us: on_device(): jnp.zeros((slot_count, row_count, block_size), jnp.bfloat16).at[slot_index]]
    pallas_call x0 -> x3, Pallas kernels: none -> 24.8 us  [the longest x1 13 us: operator(): pl.pallas_call(functools.partial(operator_kernel, slots, 4), in_specs=[sc...]
    ppermute x0 -> x16, starting transfers between devices: none -> 17.9 us  [the longest x9 6.73 us: plane_permute(): return lax.ppermute(x, PLANE, pairs)]
    all_to_all x2 -> x0, starting transfers between devices: 13.6 us -> none  [the longest x1 7.3 us: on_device(): lax.all_to_all(send_values, 'tile', split_axis=0, concat_axis=0, tiled=True)]
  transfers between devices with their start and end apart: 3 -> 16, of which waited for: 2 -> 8; matrix products, arithmetic and copies ran while one was open for 11% -> 5% of each run, Pallas kernels for 0% -> 0%
where the time goes in v1:
time: 111 us
  waiting for transfers between devices  59.5 us (54%)
  Pallas kernels  24.8 us (22%)
  starting transfers between devices  17.9 us (16%)
  local copies, waits for them, and re-layouts  6.15 us (6%)
  other arithmetic  2.13 us (2%)
    ppermute x9, waiting for transfers between devices, plane_permute(): return lax.ppermute(x, PLANE, pairs)  16.3 us
    ppermute x1, waiting for transfers between devices, on_device(): from_right = lax.ppermute(own, 'tile', [(i, (i + 3) % 4) for i in range(4)])  14 us
    pallas_call x1, Pallas kernels, operator(): pl.pallas_call(functools.partial(operator_kernel, slots, 4), in_specs=[sc...  13 us
    ppermute x1, waiting for transfers between devices, on_device(): far_right = lax.ppermute(from_right, 'tile', [(1, 0), (2, 1)])  11.2 us
    ppermute x1, waiting for transfers between devices, on_device(): from_left = lax.ppermute(own, 'tile', [(i, (i + 1) % 4) for i in range(4)])  11.2 us
    pallas_call x1, Pallas kernels, scores(): pl.pallas_call(score_kernel, in_specs=[pl.BlockSpec(memory_space=pltpu.SM...  7.31 us
    ppermute x3, waiting for transfers between devices, on_device(): moved = lax.ppermute(parts[k], 'tile', [(i, (i + k) % 4) for i in range(4)])  6.81 us
    ppermute x9, starting transfers between devices, plane_permute(): return lax.ppermute(x, PLANE, pairs)  6.73 us
  transfers between devices with their start and end apart: 16, of which 8 were waited for; matrix products, arithmetic and copies ran while one was open for 5% of the time, Pallas kernels for 0%

profile of v1, /device:TPU:0, one launch (start us, length us, event | category | flops | bytes accessed | tf_op | source)
XLA Modules:
  0.0 110.7 jit_solution(1680524493516444571)
XLA Ops:
  0.0 0.6 pad_add_fusion.place
  0.6 4.5 %pack.1 = bf16[18,128,128]{2,1,0:T(8,128)(2,1)} custom-call(s32[2]{0:T(128)} %pad_add_fusion.place, bf16[4608,512]{1,0:T(8,128)(2,1)} %patterns.1), custom_call_target="tpu_custom_call" | custom-call | tf_op jit(solution)/shard_map/pack/pallas_call | solution.py:34
  5.1 5.0 %collective-permute-start = (bf16[18,128,128]{2,1,0:T(8,128)(2,1)}, bf16[18,128,128]{2,1,0:T(8,128)(2,1)S(1)}, u32[]{:S(2)}, u32[]{:S(2)}) collective-permute-start(bf16[18,128,128]{2,1,0:T(8,128)(2,1)} %pack.1), channel_id=1, source_target_pairs={{0,12},{4,0},{8,4},{12,8},{1,13},{5,1},{9,5},{13,9},{2,14},{6,2},{... | collective-permute-start | bytes 1769480 | tf_op jit(solution)/shard_map/ppermute | solution.py:210
  10.1 0.0 collective-permute-start.2
  10.2 14.0 %collective-permute-done = bf16[18,128,128]{2,1,0:T(8,128)(2,1)S(1)} collective-permute-done((bf16[18,128,128]{2,1,0:T(8,128)(2,1)}, bf16[18,128,128]{2,1,0:T(8,128)(2,1)S(1)}, u32[]{:S(2)}, u32[]{:S(2)}) %collective-permute-start) | collective-permute-done | bytes 589856 | tf_op jit(solution)/shard_map/ppermute | solution.py:210
  24.2 1.3 %collective-permute-start.1 = (bf16[18,128,128]{2,1,0:T(8,128)(2,1)S(1)}, bf16[18,128,128]{2,1,0:T(8,128)(2,1)S(1)}, u32[]{:S(2)}, u32[]{:S(2)}) collective-permute-start(bf16[18,128,128]{2,1,0:T(8,128)(2,1)S(1)} %collective-permute-done), channel_id=1, source_target_pairs={{4,0},{8,4},{5,1},{9,5},{6,2},{10,6},{7,3},{11,7},{20,16},{24,20},... | collective-permute-start | bytes 1769480 | tf_op jit(solution)/shard_map/ppermute | solution.py:211
  25.5 11.2 %collective-permute-done.2 = bf16[18,128,128]{2,1,0:T(8,128)(2,1)S(1)} collective-permute-done((bf16[18,128,128]{2,1,0:T(8,128)(2,1)}, bf16[18,128,128]{2,1,0:T(8,128)(2,1)S(1)}, u32[]{:S(2)}, u32[]{:S(2)}) %collective-permute-start.2) | collective-permute-done | bytes 589856 | tf_op jit(solution)/shard_map/ppermute | solution.py:209
  36.7 0.7 collective-permute-start.3
  37.4 0.0 copy-done.7
  37.4 0.6 compare_select_fusion.2.slot
  37.9 11.2 %collective-permute-done.1 = bf16[18,128,128]{2,1,0:T(8,128)(2,1)S(1)} collective-permute-done((bf16[18,128,128]{2,1,0:T(8,128)(2,1)S(1)}, bf16[18,128,128]{2,1,0:T(8,128)(2,1)S(1)}, u32[]{:S(2)}, u32[]{:S(2)}) %collective-permute-start.1) | collective-permute-done | bytes 589856 | tf_op jit(solution)/shard_map/ppermute | solution.py:211
  49.2 0.0 collective-permute-done.3
  49.2 0.0 copy-done.2
  49.2 0.0 copy-done.3
  49.2 0.8 copy-done.4
  50.0 0.2 copy-done.5
  50.2 13.0 %operator.1.rest_0_ = bf16[16,128,128]{2,1,0:T(8,128)(2,1)} custom-call(s32[2]{0:T(128)} %pad_add_fusion.place, s32[128]{0:T(128)} %source.1, s32[128]{0:T(128)} %compare_select_fusion.2.slot, s32[128]{0:T(128)} %block.1, bf16[128,128,128]{2,1,0:T(8,128)(2,1)} %weights.1, bf16[1,18,128,128]{3,2,1,0:T(8,128)(2,1)} %bitcast.9, ...), custom_call_target="tpu_custom_call" | custom-call | tf_op jit(solution)/shard_map/operator/pallas_call | solution.py:97
  63.2 1.6 %collective-permute-start.5 = (bf16[16,128,128]{2,1,0:T(8,128)(2,1)}, bf16[16,128,128]{2,1,0:T(8,128)(2,1)S(1)}, u32[]{:S(2)}, u32[]{:S(2)}) collective-permute-start(bf16[16,128,128]{2,1,0:T(8,128)(2,1)} %operator.1.rest_0_), channel_id=1, source_target_pairs={{0,2},{1,3},{2,0},{3,1},{16,18},{17,19},{18,16},{19,17},{4,6},{5,7... | collective-permute-start | bytes 1572872 | tf_op jit(solution)/shard_map/ppermute | solution.py:182
  64.7 1.5 %collective-permute-start.7 = (bf16[16,128,128]{2,1,0:T(8,128)(2,1)}, bf16[16,128,128]{2,1,0:T(8,128)(2,1)}, u32[]{:S(2)}, u32[]{:S(2)}) collective-permute-start(bf16[16,128,128]{2,1,0:T(8,128)(2,1)} %operator.1.rest_0_), channel_id=1, source_target_pairs={{0,16},{1,17},{2,18},{3,19},{16,0},{17,1},{18,2},{19,3},{4,20},{5,... | collective-permute-start | bytes 1572872 | tf_op jit(solution)/shard_map/ppermute | solution.py:182
  66.2 0.0 collective-permute-start.4
  66.2 11.0 %collective-permute-done.5.rest_2_ = bf16[16,128,128]{2,1,0:T(8,128)(2,1)S(1)} collective-permute-done((bf16[16,128,128]{2,1,0:T(8,128)(2,1)}, bf16[16,128,128]{2,1,0:T(8,128)(2,1)S(1)}, u32[]{:S(2)}, u32[]{:S(2)}) %collective-permute-start.5) | collective-permute-done | bytes 524320 | tf_op jit(solution)/shard_map/ppermute | solution.py:182
  77.3 1.6 %collective-permute-start.9 = (bf16[8,128,128]{2,1,0:T(8,128)(2,1)S(1)}, bf16[8,128,128]{2,1,0:T(8,128)(2,1)S(1)}, u32[]{:S(2)}, u32[]{:S(2)}) collective-permute-start(bf16[8,128,128]{2,1,0:T(8,128)(2,1)S(1)} %slice.8), channel_id=1, source_target_pairs={{0,16},{1,17},{2,18},{3,19},{16,0},{17,1},{18,2},{19,3},{4,20},{5,... | collective-permute-start | bytes 786440 | tf_op jit(solution)/shard_map/ppermute | solution.py:182
  78.9 0.0 collective-permute-done.7.rest_4_
  78.9 1.0 slice.9
  79.8 1.6 %collective-permute-start.11 = (bf16[8,128,128]{2,1,0:T(8,128)(2,1)S(1)}, bf16[8,128,128]{2,1,0:T(8,128)(2,1)}, u32[]{:S(2)}, u32[]{:S(2)}) collective-permute-start(bf16[8,128,128]{2,1,0:T(8,128)(2,1)S(1)} %slice.9), channel_id=1, source_target_pairs={{0,2},{1,3},{2,0},{3,1},{16,18},{17,19},{18,16},{19,17},{4,6},{5,7... | collective-permute-start | bytes 786440 | tf_op jit(solution)/shard_map/ppermute | solution.py:182
  81.4 0.0 collective-permute-start.6
  81.4 0.5 collective-permute-start.8
  81.9 2.9 %collective-permute-done.9.rest_6_ = bf16[8,128,128]{2,1,0:T(8,128)(2,1)S(1)} collective-permute-done((bf16[8,128,128]{2,1,0:T(8,128)(2,1)S(1)}, bf16[8,128,128]{2,1,0:T(8,128)(2,1)S(1)}, u32[]{:S(2)}, u32[]{:S(2)}) %collective-permute-start.9) | collective-permute-done | bytes 262176 | tf_op jit(solution)/shard_map/ppermute | solution.py:182
  84.8 0.0 collective-permute-start.10
  84.8 2.4 %collective-permute-done.11.rest_8_ = bf16[8,128,128]{2,1,0:T(8,128)(2,1)} collective-permute-done((bf16[8,128,128]{2,1,0:T(8,128)(2,1)S(1)}, bf16[8,128,128]{2,1,0:T(8,128)(2,1)}, u32[]{:S(2)}, u32[]{:S(2)}) %collective-permute-start.11) | collective-permute-done | bytes 262176 | tf_op jit(solution)/shard_map/ppermute | solution.py:182
  87.2 0.0 collective-permute-start.12
  87.2 0.0 copy-done
  87.2 1.3 %copy.9 = bf16[8,35,4096]{2,1,0:T(8,128)(2,1)S(1)} copy(bf16[8,35,4096]{2,0,1:T(8,128)(2,1)S(1)} %copy-done) | data formatting | bytes 4587520 | tf_op args[0]
  88.5 2.1 %reshape.8.fields = bf16[280,4096]{1,0:T(8,128)(2,1)} reshape(bf16[8,35,4096]{2,1,0:T(8,128)(2,1)S(1)} %copy.9) | data formatting | bytes 4587520 | tf_op jit(solution)/shard_map/reshape | solution.py:230
  90.6 0.0 collective-permute-done.4.rest_1_
  90.6 0.0 collective-permute-done.10.rest_7_
  90.7 0.0 collective-permute-done.12.rest_9_
  90.7 0.0 collective-permute-done.6.rest_3_
  90.7 0.0 collective-permute-done.8.rest_5_
  90.7 7.3 %scores.1 = (f32[280,128]{1,0:T(8,128)}, bf16[280,128]{1,0:T(8,128)(2,1)}, bf16[280,128]{1,0:T(8,128)(2,1)}, bf16[280,128]{1,0:T(8,128)(2,1)}) custom-call(s32[2]{0:T(128)} %pad_add_fusion.place, bf16[280,4096]{1,0:T(8,128)(2,1)} %reshape.8.fields, bf16[16,128,128]{2,1,0:T(8,128)(2,1)} %operator.1.rest_0_, ...), custom_call_target="tpu_custom_call" | custom-call | tf_op jit(solution)/shard_map/scores/pallas_call | solution.py:165
  98.0 2.8 %collective-permute-start.15 = (bf16[280,128]{1,0:T(8,128)(2,1)}, bf16[280,128]{1,0:T(8,128)(2,1)S(1)}, u32[]{:S(2)}, u32[]{:S(2)}) collective-permute-start(bf16[280,128]{1,0:T(8,128)(2,1)} %get-tuple-element.12), channel_id=1, source_target_pairs={{0,12},{4,0},{8,4},{12,8},{1,13},{5,1},{9,5},{13,9},{2,14},{6,2},{... | collective-permute-start | bytes 215048 | tf_op jit(solution)/shard_map/ppermute | solution.py:235
  100.8 0.0 collective-permute-start.14
  100.8 1.4 %collective-permute-start.13 = (bf16[280,128]{1,0:T(8,128)(2,1)}, bf16[280,128]{1,0:T(8,128)(2,1)S(1)}, u32[]{:S(2)}, u32[]{:S(2)}) collective-permute-start(bf16[280,128]{1,0:T(8,128)(2,1)} %get-tuple-element.10), channel_id=1, source_target_pairs={{0,4},{4,8},{8,12},{12,0},{1,5},{5,9},{9,13},{13,1},{2,6},{6,10},{... | collective-permute-start | bytes 215048 | tf_op jit(solution)/shard_map/ppermute | solution.py:235
  102.2 1.5 %collective-permute-done.15 = bf16[280,128]{1,0:T(8,128)(2,1)S(1)} collective-permute-done((bf16[280,128]{1,0:T(8,128)(2,1)}, bf16[280,128]{1,0:T(8,128)(2,1)S(1)}, u32[]{:S(2)}, u32[]{:S(2)}) %collective-permute-start.15) | collective-permute-done | bytes 71712 | tf_op jit(solution)/shard_map/ppermute | solution.py:235
  103.7 5.3 %collective-permute-done.14 = bf16[280,128]{1,0:T(8,128)(2,1)S(1)} collective-permute-done((bf16[280,128]{1,0:T(8,128)(2,1)}, bf16[280,128]{1,0:T(8,128)(2,1)S(1)}, u32[]{:S(2)}, u32[]{:S(2)}) %collective-permute-start.14) | collective-permute-done | bytes 71712 | tf_op jit(solution)/shard_map/ppermute | solution.py:235
  109.0 0.0 collective-permute-done.13
  109.0 0.9 convert_add_fusion
  110.0 0.7 copy.10
  (12 shorter events, 0.0 us)
Async XLA Ops:
  0.6 36.8 %copy-start.7 = (s32[128,1]{0,1:T(1,128)S(1)}, s32[128,1]{0,1:T(1,128)}, u32[]{:S(2)}) copy-start(s32[128,1]{0,1:T(1,128)} %param.9) | copy-start | bytes 1540
  5.1 19.1 %collective-permute-start = (bf16[18,128,128]{2,1,0:T(8,128)(2,1)}, bf16[18,128,128]{2,1,0:T(8,128)(2,1)S(1)}, u32[]{:S(2)}, u32[]{:S(2)}) collective-permute-start(bf16[18,128,128]{2,1,0:T(8,128)(2,1)} %pack.1), channel_id=1, source_target_pairs={{0,12},{4,0},{8,4},{12,8},{1,13},{5,1},{9,5},{13,9},{2,14},{6,2},{... | collective-permute-start | bytes 1769480 | tf_op jit(solution)/shard_map/ppermute | solution.py:210
  10.1 26.5 %collective-permute-start.2 = (bf16[18,128,128]{2,1,0:T(8,128)(2,1)}, bf16[18,128,128]{2,1,0:T(8,128)(2,1)S(1)}, u32[]{:S(2)}, u32[]{:S(2)}) collective-permute-start(bf16[18,128,128]{2,1,0:T(8,128)(2,1)} %pack.1), channel_id=1, source_target_pairs={{0,4},{4,8},{8,12},{12,0},{1,5},{5,9},{9,13},{13,1},{2,6},{6,10},{... | collective-permute-start | bytes 1769480 | tf_op jit(solution)/shard_map/ppermute | solution.py:209
  24.2 25.0 %copy-start.2 = (bf16[18,128,128]{2,1,0:T(8,128)(2,1)}, bf16[18,128,128]{2,1,0:T(8,128)(2,1)S(1)}, u32[]{:S(2)}) copy-start(bf16[18,128,128]{2,1,0:T(8,128)(2,1)S(1)} %collective-permute-done) | copy-start | bytes 1769476
  24.2 25.0 %collective-permute-start.1 = (bf16[18,128,128]{2,1,0:T(8,128)(2,1)S(1)}, bf16[18,128,128]{2,1,0:T(8,128)(2,1)S(1)}, u32[]{:S(2)}, u32[]{:S(2)}) collective-permute-start(bf16[18,128,128]{2,1,0:T(8,128)(2,1)S(1)} %collective-permute-done), channel_id=1, source_target_pairs={{4,0},{8,4},{5,1},{9,5},{6,2},{10,6},{7,3},{11,7},{20,16},{24,20},... | collective-permute-start | bytes 1769480 | tf_op jit(solution)/shard_map/ppermute | solution.py:211
  36.6 12.5 %copy-start.3 = (bf16[18,128,128]{2,1,0:T(8,128)(2,1)}, bf16[18,128,128]{2,1,0:T(8,128)(2,1)S(1)}, u32[]{:S(2)}) copy-start(bf16[18,128,128]{2,1,0:T(8,128)(2,1)S(1)} %collective-permute-done.2) | copy-start | bytes 1769476
  36.7 12.5 %collective-permute-start.3 = (bf16[18,128,128]{2,1,0:T(8,128)(2,1)S(1)}, bf16[18,128,128]{2,1,0:T(8,128)(2,1)S(1)}, u32[]{:S(2)}, u32[]{:S(2)}) collective-permute-start(bf16[18,128,128]{2,1,0:T(8,128)(2,1)S(1)} %collective-permute-done.2), channel_id=1, source_target_pairs={{4,8},{8,12},{5,9},{9,13},{6,10},{10,14},{7,11},{11,15},{20,24},{2... | collective-permute-start | bytes 1769480 | tf_op jit(solution)/shard_map/ppermute | solution.py:212
  49.2 0.8 copy-start.4
  49.2 1.0 copy-start.5
  50.2 37.0 %copy-start = (bf16[8,35,4096]{2,0,1:T(8,128)(2,1)S(1)}, bf16[8,35,4096]{2,0,1:T(8,128)(2,1)}, u32[]{:S(2)}) copy-start(bf16[8,35,4096]{2,0,1:T(8,128)(2,1)} %param.6) | copy-start | bytes 6881284
  63.2 14.1 %collective-permute-start.5 = (bf16[16,128,128]{2,1,0:T(8,128)(2,1)}, bf16[16,128,128]{2,1,0:T(8,128)(2,1)S(1)}, u32[]{:S(2)}, u32[]{:S(2)}) collective-permute-start(bf16[16,128,128]{2,1,0:T(8,128)(2,1)} %operator.1.rest_0_), channel_id=1, source_target_pairs={{0,2},{1,3},{2,0},{3,1},{16,18},{17,19},{18,16},{19,17},{4,6},{5,7... | collective-permute-start | bytes 1572872 | tf_op jit(solution)/shard_map/ppermute | solution.py:182
  64.7 14.1 %collective-permute-start.7 = (bf16[16,128,128]{2,1,0:T(8,128)(2,1)}, bf16[16,128,128]{2,1,0:T(8,128)(2,1)}, u32[]{:S(2)}, u32[]{:S(2)}) collective-permute-start(bf16[16,128,128]{2,1,0:T(8,128)(2,1)} %operator.1.rest_0_), channel_id=1, source_target_pairs={{0,16},{1,17},{2,18},{3,19},{16,0},{17,1},{18,2},{19,3},{4,20},{5,... | collective-permute-start | bytes 1572872 | tf_op jit(solution)/shard_map/ppermute | solution.py:182
  66.2 24.4 %collective-permute-start.4 = (bf16[16,128,128]{2,1,0:T(8,128)(2,1)}, bf16[16,128,128]{2,1,0:T(8,128)(2,1)}, u32[]{:S(2)}, u32[]{:S(2)}) collective-permute-start(bf16[16,128,128]{2,1,0:T(8,128)(2,1)} %operator.1.rest_0_), channel_id=1, source_target_pairs={{0,1},{1,0},{2,3},{3,2},{16,17},{17,16},{18,19},{19,18},{4,5},{5,4... | collective-permute-start | bytes 1572872 | tf_op jit(solution)/shard_map/ppermute | solution.py:182
  77.3 11.2 %copy-start.1 = (bf16[16,128,128]{2,1,0:T(8,128)(2,1)}, bf16[16,128,128]{2,1,0:T(8,128)(2,1)S(1)}, u32[]{:S(2)}) copy-start(bf16[16,128,128]{2,1,0:T(8,128)(2,1)S(1)} %collective-permute-done.5.rest_2_) | copy-start | bytes 1572868
  77.3 7.5 %collective-permute-start.9 = (bf16[8,128,128]{2,1,0:T(8,128)(2,1)S(1)}, bf16[8,128,128]{2,1,0:T(8,128)(2,1)S(1)}, u32[]{:S(2)}, u32[]{:S(2)}) collective-permute-start(bf16[8,128,128]{2,1,0:T(8,128)(2,1)S(1)} %slice.8), channel_id=1, source_target_pairs={{0,16},{1,17},{2,18},{3,19},{16,0},{17,1},{18,2},{19,3},{4,20},{5,... | collective-permute-start | bytes 786440 | tf_op jit(solution)/shard_map/ppermute | solution.py:182
  79.8 7.3 %collective-permute-start.11 = (bf16[8,128,128]{2,1,0:T(8,128)(2,1)S(1)}, bf16[8,128,128]{2,1,0:T(8,128)(2,1)}, u32[]{:S(2)}, u32[]{:S(2)}) collective-permute-start(bf16[8,128,128]{2,1,0:T(8,128)(2,1)S(1)} %slice.9), channel_id=1, source_target_pairs={{0,2},{1,3},{2,0},{3,1},{16,18},{17,19},{18,16},{19,17},{4,6},{5,7... | collective-permute-start | bytes 786440 | tf_op jit(solution)/shard_map/ppermute | solution.py:182
  81.4 9.3 %collective-permute-start.6 = (bf16[16,128,128]{2,1,0:T(8,128)(2,1)S(1)}, bf16[16,128,128]{2,1,0:T(8,128)(2,1)}, u32[]{:S(2)}, u32[]{:S(2)}) collective-permute-start(bf16[16,128,128]{2,1,0:T(8,128)(2,1)S(1)} %collective-permute-done.5.rest_2_), channel_id=1, source_target_pairs={{0,1},{1,0},{2,3},{3,2},{16,17},{17,16},{18,19},{19,18},{4,5},{5,4... | collective-permute-start | bytes 1572872 | tf_op jit(solution)/shard_map/ppermute | solution.py:182
  81.4 9.3 %collective-permute-start.8 = (bf16[16,128,128]{2,1,0:T(8,128)(2,1)}, bf16[16,128,128]{2,1,0:T(8,128)(2,1)}, u32[]{:S(2)}, u32[]{:S(2)}) collective-permute-start(bf16[16,128,128]{2,1,0:T(8,128)(2,1)} %collective-permute-done.7.rest_4_), channel_id=1, source_target_pairs={{0,1},{1,0},{2,3},{3,2},{16,17},{17,16},{18,19},{19,18},{4,5},{5,4... | collective-permute-start | bytes 1572872 | tf_op jit(solution)/shard_map/ppermute | solution.py:182
  84.8 5.9 %copy-start.6 = (bf16[8,128,128]{2,1,0:T(8,128)(2,1)}, bf16[8,128,128]{2,1,0:T(8,128)(2,1)S(1)}, u32[]{:S(2)}) copy-start(bf16[8,128,128]{2,1,0:T(8,128)(2,1)S(1)} %collective-permute-done.9.rest_6_) | copy-start | bytes 786436
  84.8 5.9 %collective-permute-start.10 = (bf16[8,128,128]{2,1,0:T(8,128)(2,1)S(1)}, bf16[8,128,128]{2,1,0:T(8,128)(2,1)}, u32[]{:S(2)}, u32[]{:S(2)}) collective-permute-start(bf16[8,128,128]{2,1,0:T(8,128)(2,1)S(1)} %collective-permute-done.9.rest_6_), channel_id=1, source_target_pairs={{0,1},{1,0},{2,3},{3,2},{16,17},{17,16},{18,19},{19,18},{4,5},{5,4... | collective-permute-start | bytes 786440 | tf_op jit(solution)/shard_map/ppermute | solution.py:182
  87.2 3.5 %collective-permute-start.12 = (bf16[8,128,128]{2,1,0:T(8,128)(2,1)}, bf16[8,128,128]{2,1,0:T(8,128)(2,1)}, u32[]{:S(2)}, u32[]{:S(2)}) collective-permute-start(bf16[8,128,128]{2,1,0:T(8,128)(2,1)} %collective-permute-done.11.rest_8_), channel_id=1, source_target_pairs={{0,1},{1,0},{2,3},{3,2},{16,17},{17,16},{18,19},{19,18},{4,5},{5,4... | collective-permute-start | bytes 786440 | tf_op jit(solution)/shard_map/ppermute | solution.py:182
  98.0 5.7 %collective-permute-start.15 = (bf16[280,128]{1,0:T(8,128)(2,1)}, bf16[280,128]{1,0:T(8,128)(2,1)S(1)}, u32[]{:S(2)}, u32[]{:S(2)}) collective-permute-start(bf16[280,128]{1,0:T(8,128)(2,1)} %get-tuple-element.12), channel_id=1, source_target_pairs={{0,12},{4,0},{8,4},{12,8},{1,13},{5,1},{9,5},{13,9},{2,14},{6,2},{... | collective-permute-start | bytes 215048 | tf_op jit(solution)/shard_map/ppermute | solution.py:235
  100.8 8.2 %collective-permute-start.14 = (bf16[280,128]{1,0:T(8,128)(2,1)}, bf16[280,128]{1,0:T(8,128)(2,1)S(1)}, u32[]{:S(2)}, u32[]{:S(2)}) collective-permute-start(bf16[280,128]{1,0:T(8,128)(2,1)} %get-tuple-element.11), channel_id=1, source_target_pairs={{0,8},{4,12},{8,0},{12,4},{1,9},{5,13},{9,1},{13,5},{2,10},{6,14},... | collective-permute-start | bytes 215048 | tf_op jit(solution)/shard_map/ppermute | solution.py:235
  100.8 8.2 %collective-permute-start.13 = (bf16[280,128]{1,0:T(8,128)(2,1)}, bf16[280,128]{1,0:T(8,128)(2,1)S(1)}, u32[]{:S(2)}, u32[]{:S(2)}) collective-permute-start(bf16[280,128]{1,0:T(8,128)(2,1)} %get-tuple-element.10), channel_id=1, source_target_pairs={{0,4},{4,8},{8,12},{12,0},{1,5},{5,9},{9,13},{13,1},{2,6},{6,10},{... | collective-permute-start | bytes 215048 | tf_op jit(solution)/shard_map/ppermute | solution.py:235

commit v2 on v0

v2 whole, which is shorter than its diff:
```python
import functools

import jax
import jax.numpy as jnp
from jax import lax
from jax.experimental import pallas as pl
from jax.experimental.pallas import tpu as pltpu
from jax.sharding import PartitionSpec as P

PLANE = ("member", "day")
LANES = 128
CHUNKS = 1
GROUPS = 2 * CHUNKS
WIDTH = LANES // GROUPS
UNROLL = 16
MIB = 2**20

VMEM = pl.BlockSpec(memory_space=pltpu.VMEM)
SMEM = pl.BlockSpec(memory_space=pltpu.SMEM)
ANY = pl.BlockSpec(memory_space=pl.ANY)


def place():
    return lax.axis_index("member") * 4 + lax.axis_index("day")


def params(mib):
    return pltpu.CompilerParams(vmem_limit_bytes=mib * MIB)


def group_of(shape):
    return lax.broadcasted_iota(jnp.int32, shape, 1) // WIDTH


def pick(mask_of, values):
    out = values[-1]
    for k in range(len(values) - 2, -1, -1):
        out = jnp.where(mask_of(k), values[k], out)
    return out


def pack_kernel(parts, patterns, *rest):
    outs, held, sems = rest[:CHUNKS], rest[-2], rest[-1]
    p = place()
    chip, core = p // 2, lax.rem(p, 2)
    count = outs[0].shape[0]
    step = count // parts
    columns = pl.ds(pl.multiple_of(chip * LANES, LANES), LANES)
    copies = []
    for part in range(parts):
        for group in range(GROUPS):
            rows = pl.ds((group * count + part * step) * LANES, step * LANES)
            copies.append(
                pltpu.make_async_copy(
                    patterns.at[rows, columns], held.at[rows, :], sems.at[part, group]
                )
            )
            copies[-1].start()
    shape = (GROUPS * LANES, CHUNKS * LANES)
    k = lax.broadcasted_iota(jnp.int32, shape, 0)
    n = lax.broadcasted_iota(jnp.int32, shape, 1)
    chunk, lane_out = n // LANES, n % LANES
    wanted = chunk * (LANES // CHUNKS) + core * WIDTH + lane_out % WIDTH
    chosen = (k // LANES == lane_out // WIDTH) & (k % LANES == wanted)
    choose = jnp.where(chosen, 1.0, 0.0).astype(held.dtype)
    for part in range(parts):
        for group in range(GROUPS):
            copies[part * GROUPS + group].wait()
        for j in range(part * step, (part + 1) * step):
            blocks = [
                held[(group * count + j) * LANES : (group * count + j + 1) * LANES, :]
                for group in range(GROUPS)
            ]
            both = jnp.dot(
                jnp.concatenate(blocks, 1), choose, preferred_element_type=jnp.float32
            ).astype(held.dtype)
            for chunk in range(CHUNKS):
                outs[chunk][j] = both[:, chunk * LANES : (chunk + 1) * LANES]


def pack(patterns):
    rows = patterns.shape[0]
    count = rows // LANES // GROUPS
    parts = 3
    return pl.pallas_call(
        functools.partial(pack_kernel, parts),
        in_specs=[pl.BlockSpec(memory_space=pltpu.HBM)],
        out_specs=[VMEM] * CHUNKS,
        out_shape=[jax.ShapeDtypeStruct((count, LANES, LANES), patterns.dtype)] * CHUNKS,
        scratch_shapes=[
            pltpu.VMEM((rows, LANES), patterns.dtype),
            pltpu.SemaphoreType.DMA((parts, GROUPS)),
        ],
        compiler_params=params(8),
        name="pack",
    )(patterns)


def add_tiles(table, start, end, weights, held, total):
    group = group_of((LANES, LANES))

    @pl.loop(0, (end - start + UNROLL - 1) // UNROLL)
    def _(step):
        products, targets = [], []
        for u in range(UNROLL):
            i = start + step * UNROLL + u
            code = table[i]
            side = jnp.where(i < end, (code >> 6) & 7, 7)
            targets.append(code & 63)
            rhs = held[(code >> 9) & 1023]
            rhs = jnp.where(group == side, rhs, jnp.zeros_like(rhs))
            products.append(
                jnp.dot(weights[code >> 19], rhs, preferred_element_type=jnp.float32)
            )
        for target, product in zip(targets, products):
            total[target] += product


def early_kernel(table, weights, *rest):
    bands, total, held, sems = rest[:-3], rest[-3], rest[-2], rest[-1]
    count = bands[0].shape[0]
    copies = [
        pltpu.make_async_copy(band, held.at[pl.ds(i * count, count)], sems.at[i])
        for i, band in enumerate(bands)
    ]
    for copy in copies:
        copy.start()
    total[...] = jnp.zeros_like(total)
    for copy in copies:
        copy.wait()
    add_tiles(table, 0, table[table.shape[0] - 1], weights, held, total)


def early(table, weights, bands, source_blocks):
    count = bands[0].shape[0]
    return pl.pallas_call(
        early_kernel,
        in_specs=[SMEM, VMEM] + [ANY] * len(bands),
        out_specs=VMEM,
        out_shape=jax.ShapeDtypeStruct((source_blocks, LANES, LANES), jnp.float32),
        scratch_shapes=[
            pltpu.VMEM((count * len(bands), LANES, LANES), weights.dtype),
            pltpu.SemaphoreType.DMA((len(bands),)),
        ],
        compiler_params=params(10 + count * len(bands) * LANES * LANES * 2 // MIB),
        name="early",
    )(table, weights, *bands)


def late_kernel(table, weights, given, right, left, packed, total, held, sems):
    fetch = pltpu.make_async_copy(given, total, sems.at[0])
    fetch.start()
    first = lax.axis_index("tile") < 2

    @pl.when(first)
    def _():
        pltpu.make_async_copy(right, held, sems.at[1]).start()

    @pl.when(jnp.logical_not(first))
    def _():
        pltpu.make_async_copy(left, held, sems.at[1]).start()

    fetch.wait()
    pltpu.make_async_copy(right, held, sems.at[1]).wait()
    tiles = weights.shape[0]
    add_tiles(table, table[table.shape[0] - 1], tiles, weights, held, total)
    blocks = packed.shape[0]
    me = lax.rem(place(), GROUPS)
    group = group_of((LANES, LANES))
    for j in range(blocks):
        sums = [total[h * blocks + j] for h in range(GROUPS)]
        out = None
        for r in range(GROUPS):
            want = lax.rem(group + (r + GROUPS) - me, GROUPS)
            term = pick(lambda k: want == k, sums)
            if r:
                term = pltpu.roll(term, r * WIDTH, 1)
            out = term if out is None else out + term
        packed[j] = out.astype(packed.dtype)


def late(table, weights, total, right, left):
    source_blocks = total.shape[0]
    return pl.pallas_call(
        late_kernel,
        in_specs=[SMEM, VMEM, ANY, ANY, ANY],
        out_specs=VMEM,
        out_shape=jax.ShapeDtypeStruct((source_blocks // GROUPS, LANES, LANES), weights.dtype),
        scratch_shapes=[
            pltpu.VMEM(total.shape, jnp.float32),
            pltpu.VMEM(right.shape, weights.dtype),
            pltpu.SemaphoreType.DMA((2,)),
        ],
        compiler_params=params(14),
        name="late",
    )(table, weights, total, right, left)


def products_of(fields, pieces, flip):
    depth = fields.shape[1] // GROUPS
    across = lax.rem(place(), 4) // 2
    group = group_of((depth, LANES))
    values = [piece[...].reshape(depth, LANES) for piece in pieces]
    if CHUNKS == 1:
        sets = [[(values[0], 0), (values[1], 1)], [(values[2], 0), (values[3], 1)]]
    else:
        near, away = 2 * across, 2 * (1 - across)
        sets = [
            [(values[0], near), (values[1], near + 1), (values[2], away), (values[3], away + 1)]
        ]
    totals = [None] * len(sets)
    for h in range(GROUPS):
        rhs = []
        for members in sets:
            index = [lax.rem(i + h, GROUPS) for _, i in members]
            rhs.append(pick(lambda k: group == index[k], [value for value, _ in members]))
        rhs = jnp.concatenate(rhs, 1) if len(rhs) > 1 else rhs[0]
        product = jnp.dot(
            fields[:, h * depth : (h + 1) * depth], rhs, preferred_element_type=jnp.float32
        )
        for s in range(len(sets)):
            term = product[:, s * LANES : (s + 1) * LANES]
            if h:
                term = pltpu.roll(term, LANES - h * WIDTH, 1)
            totals[s] = term if totals[s] is None else totals[s] + term
    return totals


def by_core(even, odd, body):
    core = lax.rem(place(), 2)

    @pl.when(core == 0)
    def _():
        body(even)

    @pl.when(core == 1)
    def _():
        body(odd)


def near_kernel(fields, mine, other, r1, r2, s1, s2, out):
    def body(pieces):
        for s, total in enumerate(products_of(fields, pieces, 0)):
            out[s] = total

    by_core([mine, other, r1, r2], [other, mine, s1, s2], body)


def away_kernel(fields, r1, r2, s1, s2, d, s3, out):
    def body(pieces):
        for s, total in enumerate(products_of(fields, pieces, 1)):
            out[s] = total

    by_core([s2, s1, d, s3], [r2, r1, s3, d], body)


def last_kernel(split, fields, r1, r2, s1, s2, d, s3, *rest):
    count = 2 * CHUNKS - 1
    earlier, outs = rest[:count], rest[count:]
    p = place()
    chip = p // 2
    half = LANES // 2

    def emit(to, value):
        if not split:
            outs[0][to] = value.astype(outs[0].dtype)
            return
        hop = lax.rem(to - lax.axis_index("tile") + 4, 4)
        for k, out in enumerate(outs):

            @pl.when(hop == k)
            def _(out=out):
                out[...] = value.astype(out.dtype)

    def body(pieces):
        totals = products_of(fields, pieces, 1)
        if CHUNKS == 1:
            for relative in range(2):
                emit(chip ^ relative, earlier[0][relative])
                emit(chip ^ (2 + relative), totals[relative])
            return
        low = lax.broadcasted_iota(jnp.int32, totals[0].shape, 1) < half
        for e in range(2):
            first = earlier[e][0]
            second = totals[0] if e else earlier[2][0]
            row = 2 * ((p // 4) ^ e)
            emit(row, jnp.where(low, first, pltpu.roll(second, half, 1)))
            emit(row + 1, jnp.where(low, pltpu.roll(first, half, 1), second))

    by_core([s2, s1, d, s3], [r2, r1, s3, d], body)


def half_scores(kernel, fields, pieces, name):
    rows = fields.shape[0]
    return pl.pallas_call(
        kernel,
        in_specs=[VMEM] * (1 + len(pieces)),
        out_specs=VMEM,
        out_shape=jax.ShapeDtypeStruct((2 // CHUNKS, rows, LANES), jnp.float32),
        compiler_params=params(16),
        name=name,
    )(fields, *pieces)


def last_scores(fields, pieces, earlier, split):
    rows = fields.shape[0]
    if split:
        out_shape = [jax.ShapeDtypeStruct((rows, LANES), jnp.float32)] + [
            jax.ShapeDtypeStruct((rows, LANES), jnp.bfloat16)
        ] * 3
    else:
        out_shape = [jax.ShapeDtypeStruct((4, rows, LANES), jnp.float32)]
    return pl.pallas_call(
        functools.partial(last_kernel, split),
        in_specs=[VMEM] * (1 + len(pieces) + len(earlier)),
        out_specs=[VMEM] * len(out_shape),
        out_shape=out_shape,
        compiler_params=params(18),
        name="last",
    )(fields, *pieces, *earlier)


def plane_permute(x, to):
    pairs = []
    for m in range(2):
        for a in range(2):
            for c in range(2):
                tm, ta, tc = to(m, a, c)
                pairs.append((m * 4 + a * 2 + c, tm * 4 + ta * 2 + tc))
    return lax.ppermute(x, PLANE, pairs)


def over_core(x):
    return plane_permute(x, lambda m, a, c: (m, a, 1 - c))


def over_first(x):
    return plane_permute(x, lambda m, a, c: (m, 1 - a, c) if c == 0 else (1 - m, a, c))


def over_second(x):
    return plane_permute(x, lambda m, a, c: (1 - m, a, c) if c == 0 else (m, 1 - a, c))


def gather_plane(piece):
    other = over_core(piece)
    r1 = over_first(piece)
    r2 = over_first(other)
    d = over_second(r1)
    s1, s2, s3 = over_core(r1), over_core(r2), over_core(d)
    return (piece, other, r1, r2, s1, s2), (r1, r2, s1, s2, d, s3)


def tile_table(tile_source, tile_band, tile_block, blocks, bands, z):
    tiles = tile_source.shape[0]
    owner = tile_band[:, 0]
    if bands == 4:
        hop = jnp.remainder(owner - z, 4)
        is_late = hop == 2
        slot = jnp.where(hop == 3, 2, jnp.where(is_late, 0, hop))
    else:
        is_late = jnp.zeros_like(owner, dtype=bool)
        slot = owner
    count = blocks // GROUPS
    side = tile_block // count
    row = slot * count + tile_block - side * count
    order = jnp.arange(tiles, dtype=jnp.int32)
    code = (order << 19) | (row << 9) | (side << 6) | tile_source
    key = order + jnp.where(is_late, tiles, 0)
    rank = jnp.sum((key[None, :] < key[:, None]).astype(jnp.int32), 1)
    size = tiles + 2 * UNROLL
    place_of = jnp.arange(size, dtype=jnp.int32)
    listed = jnp.sum(jnp.where(rank[None, :] == place_of[:, None], code[None, :], 0), 1)
    soon = jnp.sum(jnp.where(is_late, 0, 1))
    return jnp.where(place_of == size - 1, soon, listed).astype(jnp.int32)


def on_device(fields, remap_tiles, tile_source, tile_band, tile_block, patterns):
    bands = lax.axis_size("tile")
    day_count, var_count, source_cells = fields.shape
    row_count = day_count * var_count
    source_blocks = source_cells // LANES
    pattern_count = patterns.shape[1]
    z = lax.axis_index("tile")
    rows = fields.transpose(1, 0, 2).reshape(row_count, source_cells)
    table = tile_table(
        tile_source, tile_band, tile_block, patterns.shape[0] // LANES, bands, z
    )
    owns = pack(patterns)
    totals, rights, lefts = [], [], []
    for own in owns:
        if bands == 4:
            from_left = lax.ppermute(own, "tile", [(i, (i + 1) % 4) for i in range(4)])
            from_right = lax.ppermute(own, "tile", [(i, (i + 3) % 4) for i in range(4)])
            rights.append(lax.ppermute(from_right, "tile", [(1, 0), (2, 1)]))
            lefts.append(lax.ppermute(from_left, "tile", [(1, 2), (2, 3)]))
            near = [own, from_right, from_left]
        else:
            gathered = lax.all_gather(own, "tile", axis=0)
            near = [gathered.reshape((-1,) + gathered.shape[2:])]
            rights.append(own)
            lefts.append(own)
        totals.append(early(table, remap_tiles, near, source_blocks))
    earlier = []
    for chunk in range(CHUNKS):
        piece = late(table, remap_tiles, totals[chunk], rights[chunk], lefts[chunk])
        near, away = gather_plane(piece)
        earlier.append(half_scores(near_kernel, rows, near, "near"))
        if chunk < CHUNKS - 1:
            earlier.append(half_scores(away_kernel, rows, away, "away"))
    parts = last_scores(rows, away, earlier, bands == 4)
    if bands == 4:
        result = parts[0]
        for k in (1, 2, 3):
            moved = lax.ppermute(parts[k], "tile", [(i, (i + k) % 4) for i in range(4)])
            result = result + moved.astype(jnp.float32)
    else:
        partial = parts[0].transpose(1, 0, 2).reshape(row_count, pattern_count)
        result = lax.psum_scatter(partial, "tile", scatter_dimension=1, tiled=True)
    return result.reshape(var_count, day_count, pattern_count // bands).transpose(1, 0, 2)


def solution(mesh):
    return jax.shard_map(
        on_device,
        mesh=mesh,
        in_specs=(
            P(("member", "day"), None, "tile"),
            P("tile", None, None),
            P("tile"),
            P("tile", None),
            P("tile"),
            P("tile", None),
        ),
        out_specs=P(("member", "day"), None, "tile"),
        check_vma=False,
    )
```

time: 543 us -> 84 us (0.15)
  waiting for transfers between devices: 434 us -> 49 us
  local copies, waits for them, and re-layouts: 49.6 us -> 4.54 us
  matrix products: 27.5 us -> 0 us
  between operations: 13.5 us -> 0.12 us
  Pallas kernels: 0 us -> 8.14 us
  starting transfers between devices: 13.8 us -> 20.2 us
    all_to_all x2 -> x0, waiting for transfers between devices: 396 us -> none  [the longest x1 396 us: on_device(): lax.all_to_all(send_values, 'tile', split_axis=0, concat_axis=0, tiled=True)]
    ppermute x0 -> x14, waiting for transfers between devices: none -> 49 us  [the longest x7 16 us: plane_permute(): return lax.ppermute(x, PLANE, pairs)]
    psum x1 -> x0, waiting for transfers between devices: 38.2 us -> none  [on_device(): total_scores = lax.psum(partial_scores, 'tile')]
    dot_general x3 -> x0, matrix products: 27.5 us -> none  [the longest x1 13.4 us: on_device(): jnp.einsum('rtk,tkj->trj', columns, remap_tiles, preferred_element_type=j...]
    scatter x2 -> x0, local copies, waits for them, and re-layouts: 25.6 us -> none  [the longest x1 24.2 us: on_device(): jnp.zeros((slot_count, row_count, block_size), jnp.bfloat16).at[slot_index]]
    ppermute x0 -> x14, starting transfers between devices: none -> 20.2 us  [the longest x3 8.12 us: on_device(): moved = lax.ppermute(parts[k], 'tile', [(i, (i + k) % 4) for i in range(4)])]
    all_to_all x2 -> x0, starting transfers between devices: 13.6 us -> none  [the longest x1 7.3 us: on_device(): lax.all_to_all(send_values, 'tile', split_axis=0, concat_axis=0, tiled=True)]
    pallas_call x0 -> x5, Pallas kernels: none -> 8.14 us  [the longest x1 3.63 us: early(): pl.pallas_call(early_kernel, in_specs=[SMEM, VMEM] + [ANY] * len(bands),...]
  transfers between devices with their start and end apart: 3 -> 14, of which waited for: 2 -> 11; matrix products, arithmetic and copies ran while one was open for 11% -> 2% of each run, Pallas kernels for 0% -> 5%
where the time goes in v2:
time: 84 us; the launch traced here: 84.3 us
  waiting for transfers between devices  49 us (58%)
  starting transfers between devices  20.2 us (24%)
  Pallas kernels  8.14 us (10%)
  local copies, waits for them, and re-layouts  4.54 us (5%)
  other arithmetic  2.32 us (3%)
    ppermute x7, waiting for transfers between devices, plane_permute(): return lax.ppermute(x, PLANE, pairs)  16 us
    ppermute x1, waiting for transfers between devices, on_device(): from_right = lax.ppermute(own, 'tile', [(i, (i + 3) % 4) for i in range(4)])  13.1 us
    ppermute x1, waiting for transfers between devices, on_device(): from_left = lax.ppermute(own, 'tile', [(i, (i + 1) % 4) for i in range(4)])  11.3 us
    ppermute x3, starting transfers between devices, on_device(): moved = lax.ppermute(parts[k], 'tile', [(i, (i + k) % 4) for i in range(4)])  8.12 us
    ppermute x1, starting transfers between devices, on_device(): from_right = lax.ppermute(own, 'tile', [(i, (i + 3) % 4) for i in range(4)])  5.11 us
    ppermute x7, starting transfers between devices, plane_permute(): return lax.ppermute(x, PLANE, pairs)  4.99 us
    ppermute x1, waiting for transfers between devices, on_device(): rights.append(lax.ppermute(from_right, 'tile', [(1, 0), (2, 1)]))  4.98 us
    unnamed x14, local copies, waits for them, and re-layouts  4.54 us
  transfers between devices with their start and end apart: 14, of which 11 were waited for; matrix products, arithmetic and copies ran while one was open for 2% of the time, Pallas kernels for 5%

profile of v2, /device:TPU:0, one launch (start us, length us, event | category | flops | bytes accessed | tf_op | source)
XLA Modules:
  0.0 84.3 jit_solution(13764981511369494309)
XLA Ops:
  0.0 0.0 copy-start.3
  0.0 2.3 %copy-done.3 = bf16[4608,512]{1,0:T(8,128)(2,1)S(1)} copy-done((bf16[4608,512]{1,0:T(8,128)(2,1)S(1)}, bf16[4608,512]{1,0:T(8,128)(2,1)}, u32[]{:S(2)}) %copy-start.3) | copy-done | bytes 4718616
  2.3 1.0 %pack.1.rest_0_ = bf16[18,128,128]{2,1,0:T(8,128)(2,1)S(1)} custom-call(bf16[4608,512]{1,0:T(8,128)(2,1)S(1)} %copy-done.3), custom_call_target="tpu_custom_call" | custom-call | tf_op jit(solution)/shard_map/pack/pallas_call | solution.py:85
  3.4 5.1 %collective-permute-start = (bf16[18,128,128]{2,1,0:T(8,128)(2,1)S(1)}, bf16[18,128,128]{2,1,0:T(8,128)(2,1)S(1)}, u32[]{:S(2)}, u32[]{:S(2)}) collective-permute-start(bf16[18,128,128]{2,1,0:T(8,128)(2,1)S(1)} %pack.1.rest_0_), channel_id=1, source_target_pairs={{0,12},{4,0},{8,4},{12,8},{1,13},{5,1},{9,5},{13,9},{2,14},{6,2},{... | collective-permute-start | bytes 1769480 | tf_op jit(solution)/shard_map/ppermute | solution.py:394
  8.5 0.0 collective-permute-start.1
  8.5 0.0 copy-done.6
  8.5 0.6 fusion
  9.1 0.0 copy-done.4
  9.2 0.0 copy-done.5
  9.2 13.1 %collective-permute-done.rest_1_ = bf16[18,128,128]{2,1,0:T(8,128)(2,1)S(1)} collective-permute-done((bf16[18,128,128]{2,1,0:T(8,128)(2,1)S(1)}, bf16[18,128,128]{2,1,0:T(8,128)(2,1)S(1)}, u32[]{:S(2)}, u32[]{:S(2)}) %collective-permute-start) | collective-permute-done | bytes 589856 | tf_op jit(solution)/shard_map/ppermute | solution.py:394
  22.2 1.3 %collective-permute-start.2 = (bf16[18,128,128]{2,1,0:T(8,128)(2,1)S(1)}, bf16[18,128,128]{2,1,0:T(8,128)(2,1)S(1)}, u32[]{:S(2)}, u32[]{:S(2)}) collective-permute-start(bf16[18,128,128]{2,1,0:T(8,128)(2,1)S(1)} %collective-permute-done.rest_1_), channel_id=1, source_target_pairs={{4,0},{8,4},{5,1},{9,5},{6,2},{10,6},{7,3},{11,7},{20,16},{24,20},... | collective-permute-start | bytes 1769480 | tf_op jit(solution)/shard_map/ppermute | solution.py:395
  23.5 11.3 %collective-permute-done.1.rest_2_ = bf16[18,128,128]{2,1,0:T(8,128)(2,1)S(1)} collective-permute-done((bf16[18,128,128]{2,1,0:T(8,128)(2,1)S(1)}, bf16[18,128,128]{2,1,0:T(8,128)(2,1)S(1)}, u32[]{:S(2)}, u32[]{:S(2)}) %collective-permute-start.1) | collective-permute-done | bytes 589856 | tf_op jit(solution)/shard_map/ppermute | solution.py:393
  34.8 0.7 collective-permute-start.3
  35.5 0.2 convert_reduce_fusion
  35.7 0.1 select_reduce_fusion
  35.8 0.7 compare_select_fusion.6.table
  36.5 0.0 copy-start
  36.5 2.2 %copy-done = bf16[128,128,128]{2,1,0:T(8,128)(2,1)S(1)} copy-done((bf16[128,128,128]{2,1,0:T(8,128)(2,1)S(1)}, bf16[128,128,128]{2,1,0:T(8,128)(2,1)}, u32[]{:S(2)}) %copy-start) | copy-done | bytes 4194328
  38.7 3.6 %early.1.given = f32[32,128,128]{2,1,0:T(8,128)S(1)} custom-call(s32[160]{0:T(256)S(1)} %compare_select_fusion.6.table, bf16[128,128,128]{2,1,0:T(8,128)(2,1)S(1)} %copy-done, bf16[18,128,128]{2,1,0:T(8,128)(2,1)S(1)} %pack.1.rest_0_, bf16[18,128,128]{2,1,0:T(8,128)(2,1)S(1)} %collective-permute-done.rest_1_, ...), custom_call_target="tpu_custom_call" | custom-call | tf_op jit(solution)/shard_map/early/pallas_call | solution.py:136
  42.3 0.0 copy-start.2
  42.3 5.0 %collective-permute-done.2.right = bf16[18,128,128]{2,1,0:T(8,128)(2,1)S(1)} collective-permute-done((bf16[18,128,128]{2,1,0:T(8,128)(2,1)S(1)}, bf16[18,128,128]{2,1,0:T(8,128)(2,1)S(1)}, u32[]{:S(2)}, u32[]{:S(2)}) %collective-permute-start.2) | collective-permute-done | bytes 589856 | tf_op jit(solution)/shard_map/ppermute | solution.py:395
  47.3 0.0 collective-permute-done.3.left
  47.3 0.0 copy-done.1
  47.3 1.5 %late.1.mine = bf16[16,128,128]{2,1,0:T(8,128)(2,1)S(1)} custom-call(s32[160]{0:T(256)S(1)} %compare_select_fusion.6.table, bf16[128,128,128]{2,1,0:T(8,128)(2,1)S(1)} %copy-done.1, f32[32,128,128]{2,1,0:T(8,128)S(1)} %early.1.given, bf16[18,128,128]{2,1,0:T(8,128)(2,1)S(1)} %collective-permute-done.2.right, ...), custom_call_target="tpu_custom_call" | custom-call | tf_op jit(solution)/shard_map/late/pallas_call | solution.py:184
  48.8 0.1 collective-permute-start.5
  48.9 1.6 %collective-permute-start.4 = (bf16[16,128,128]{2,1,0:T(8,128)(2,1)S(1)}, bf16[16,128,128]{2,1,0:T(8,128)(2,1)S(1)}, u32[]{:S(2)}, u32[]{:S(2)}) collective-permute-start(bf16[16,128,128]{2,1,0:T(8,128)(2,1)S(1)} %late.1.mine), channel_id=1, source_target_pairs={{0,2},{1,17},{2,0},{3,19},{16,18},{17,1},{18,16},{19,3},{4,6},{5,2... | collective-permute-start | bytes 1572872 | tf_op jit(solution)/shard_map/ppermute | solution.py:330
  50.5 0.3 collective-permute-done.5.other
  50.8 1.5 %collective-permute-start.6 = (bf16[16,128,128]{2,1,0:T(8,128)(2,1)S(1)}, bf16[16,128,128]{2,1,0:T(8,128)(2,1)S(1)}, u32[]{:S(2)}, u32[]{:S(2)}) collective-permute-start(bf16[16,128,128]{2,1,0:T(8,128)(2,1)S(1)} %collective-permute-done.5.other), channel_id=1, source_target_pairs={{0,2},{1,17},{2,0},{3,19},{16,18},{17,1},{18,16},{19,3},{4,6},{5,2... | collective-permute-start | bytes 1572872 | tf_op jit(solution)/shard_map/ppermute | solution.py:330
  52.3 5.9 %collective-permute-done.4.r1 = bf16[16,128,128]{2,1,0:T(8,128)(2,1)S(1)} collective-permute-done((bf16[16,128,128]{2,1,0:T(8,128)(2,1)S(1)}, bf16[16,128,128]{2,1,0:T(8,128)(2,1)S(1)}, u32[]{:S(2)}, u32[]{:S(2)}) %collective-permute-start.4) | collective-permute-done | bytes 524320 | tf_op jit(solution)/shard_map/ppermute | solution.py:330
  58.2 1.5 %collective-permute-start.9 = (bf16[16,128,128]{2,1,0:T(8,128)(2,1)S(1)}, bf16[16,128,128]{2,1,0:T(8,128)(2,1)S(1)}, u32[]{:S(2)}, u32[]{:S(2)}) collective-permute-start(bf16[16,128,128]{2,1,0:T(8,128)(2,1)S(1)} %collective-permute-done.4.r1), channel_id=1, source_target_pairs={{0,16},{1,3},{2,18},{3,1},{16,0},{17,19},{18,2},{19,17},{4,20},{5,... | collective-permute-start | bytes 1572872 | tf_op jit(solution)/shard_map/ppermute | solution.py:330
  59.7 0.0 collective-permute-start.7
  59.7 7.5 %collective-permute-done.6.r2 = bf16[16,128,128]{2,1,0:T(8,128)(2,1)S(1)} collective-permute-done((bf16[16,128,128]{2,1,0:T(8,128)(2,1)S(1)}, bf16[16,128,128]{2,1,0:T(8,128)(2,1)S(1)}, u32[]{:S(2)}, u32[]{:S(2)}) %collective-permute-start.6) | collective-permute-done | bytes 524320 | tf_op jit(solution)/shard_map/ppermute | solution.py:330
  67.2 0.0 collective-permute-start.8
  67.2 1.7 %collective-permute-done.9.d = bf16[16,128,128]{2,1,0:T(8,128)(2,1)S(1)} collective-permute-done((bf16[16,128,128]{2,1,0:T(8,128)(2,1)S(1)}, bf16[16,128,128]{2,1,0:T(8,128)(2,1)S(1)}, u32[]{:S(2)}, u32[]{:S(2)}) %collective-permute-start.9) | collective-permute-done | bytes 524320 | tf_op jit(solution)/shard_map/ppermute | solution.py:330
  68.9 0.4 collective-permute-start.10
  69.2 0.0 collective-permute-done.7.s1
  69.2 0.0 collective-permute-done.8.s2
  69.2 0.0 copy-done.2
  69.2 0.9 %near.1.rest_0_ = f32[2,280,128]{2,1,0:T(8,128)S(1)} custom-call(bf16[280,4096]{1,0:T(8,128)(2,1)S(1)} %bitcast.12, bf16[16,128,128]{2,1,0:T(8,128)(2,1)S(1)} %late.1.mine, bf16[16,128,128]{2,1,0:T(8,128)(2,1)S(1)} %collective-permute-done.5.other, bf16[16,128,128]{2,1,0:T(8,128)(2,1)S(1)} %collective-permute-done.4.r1, ...), custom_call_target="tpu_custom_call" | custom-call | tf_op jit(solution)/shard_map/near/pallas_call | solution.py:295
  70.2 0.6 collective-permute-done.10.s3
  70.8 1.0 %last.1 = (f32[280,128]{1,0:T(8,128)S(1)}, bf16[280,128]{1,0:T(8,128)(2,1)S(1)}, bf16[280,128]{1,0:T(8,128)(2,1)S(1)}, bf16[280,128]{1,0:T(8,128)(2,1)S(1)}) custom-call(bf16[280,4096]{1,0:T(8,128)(2,1)S(1)} %bitcast.13, bf16[16,128,128]{2,1,0:T(8,128)(2,1)S(1)} %collective-permute-done.4.r1, bf16[16,128,128]{2,1,0:T(8,128)(2,1)S(1)} %collective-permute-done.6.r2, ...), custom_call_target="tpu_custom_call" | custom-call | tf_op jit(solution)/shard_map/last/pallas_call | solution.py:313
  71.8 2.3 %collective-permute-start.11 = (bf16[280,128]{1,0:T(8,128)(2,1)S(1)}, bf16[280,128]{1,0:T(8,128)(2,1)S(1)}, u32[]{:S(2)}, u32[]{:S(2)}) collective-permute-start(bf16[280,128]{1,0:T(8,128)(2,1)S(1)} %get-tuple-element.10), channel_id=1, source_target_pairs={{0,4},{4,8},{8,12},{12,0},{1,5},{5,9},{9,13},{13,1},{2,6},{6,10},{... | collective-permute-start | bytes 215048 | tf_op jit(solution)/shard_map/ppermute | solution.py:415
  74.1 4.1 %collective-permute-start.12 = (bf16[280,128]{1,0:T(8,128)(2,1)S(1)}, bf16[280,128]{1,0:T(8,128)(2,1)S(1)}, u32[]{:S(2)}, u32[]{:S(2)}) collective-permute-start(bf16[280,128]{1,0:T(8,128)(2,1)S(1)} %get-tuple-element.11), channel_id=1, source_target_pairs={{0,8},{4,12},{8,0},{12,4},{1,9},{5,13},{9,1},{13,5},{2,10},{6,14},... | collective-permute-start | bytes 215048 | tf_op jit(solution)/shard_map/ppermute | solution.py:415
  78.2 1.7 %collective-permute-start.13 = (bf16[280,128]{1,0:T(8,128)(2,1)S(1)}, bf16[280,128]{1,0:T(8,128)(2,1)S(1)}, u32[]{:S(2)}, u32[]{:S(2)}) collective-permute-start(bf16[280,128]{1,0:T(8,128)(2,1)S(1)} %get-tuple-element.12), channel_id=1, source_target_pairs={{0,12},{4,0},{8,4},{12,8},{1,13},{5,1},{9,5},{13,9},{2,14},{6,2},{... | collective-permute-start | bytes 215048 | tf_op jit(solution)/shard_map/ppermute | solution.py:415
  79.9 0.6 collective-permute-done.11
  80.5 3.0 %collective-permute-done.12 = bf16[280,128]{1,0:T(8,128)(2,1)S(1)} collective-permute-done((bf16[280,128]{1,0:T(8,128)(2,1)S(1)}, bf16[280,128]{1,0:T(8,128)(2,1)S(1)}, u32[]{:S(2)}, u32[]{:S(2)}) %collective-permute-start.12) | collective-permute-done | bytes 71712 | tf_op jit(solution)/shard_map/ppermute | solution.py:415
  83.5 0.1 collective-permute-done.13
  83.6 0.7 add_bitcast_fusion
  (6 shorter events, 0.0 us)
Async XLA Ops:
  0.0 2.3 %copy-start.3 = (bf16[4608,512]{1,0:T(8,128)(2,1)S(1)}, bf16[4608,512]{1,0:T(8,128)(2,1)}, u32[]{:S(2)}) copy-start(bf16[4608,512]{1,0:T(8,128)(2,1)} %patterns.1) | copy-start | bytes 14155780
  2.3 6.2 %copy-start.6 = (s32[128,1]{0,1:T(1,128)S(1)}, s32[128,1]{0,1:T(1,128)}, u32[]{:S(2)}) copy-start(s32[128,1]{0,1:T(1,128)} %param.9) | copy-start | bytes 1540
  2.3 6.8 %copy-start.4 = (s32[128]{0:T(128)S(1)}, s32[128]{0:T(128)}, u32[]{:S(2)}) copy-start(s32[128]{0:T(128)} %param.8) | copy-start | bytes 1540
  2.3 6.8 %copy-start.5 = (s32[128]{0:T(128)S(1)}, s32[128]{0:T(128)}, u32[]{:S(2)}) copy-start(s32[128]{0:T(128)} %param.10) | copy-start | bytes 1540
  3.4 18.8 %collective-permute-start = (bf16[18,128,128]{2,1,0:T(8,128)(2,1)S(1)}, bf16[18,128,128]{2,1,0:T(8,128)(2,1)S(1)}, u32[]{:S(2)}, u32[]{:S(2)}) collective-permute-start(bf16[18,128,128]{2,1,0:T(8,128)(2,1)S(1)} %pack.1.rest_0_), channel_id=1, source_target_pairs={{0,12},{4,0},{8,4},{12,8},{1,13},{5,1},{9,5},{13,9},{2,14},{6,2},{... | collective-permute-start | bytes 1769480 | tf_op jit(solution)/shard_map/ppermute | solution.py:394
  8.5 26.3 %collective-permute-start.1 = (bf16[18,128,128]{2,1,0:T(8,128)(2,1)S(1)}, bf16[18,128,128]{2,1,0:T(8,128)(2,1)S(1)}, u32[]{:S(2)}, u32[]{:S(2)}) collective-permute-start(bf16[18,128,128]{2,1,0:T(8,128)(2,1)S(1)} %pack.1.rest_0_), channel_id=1, source_target_pairs={{0,4},{4,8},{8,12},{12,0},{1,5},{5,9},{9,13},{13,1},{2,6},{6,10},{... | collective-permute-start | bytes 1769480 | tf_op jit(solution)/shard_map/ppermute | solution.py:393
  22.2 25.1 %collective-permute-start.2 = (bf16[18,128,128]{2,1,0:T(8,128)(2,1)S(1)}, bf16[18,128,128]{2,1,0:T(8,128)(2,1)S(1)}, u32[]{:S(2)}, u32[]{:S(2)}) collective-permute-start(bf16[18,128,128]{2,1,0:T(8,128)(2,1)S(1)} %collective-permute-done.rest_1_), channel_id=1, source_target_pairs={{4,0},{8,4},{5,1},{9,5},{6,2},{10,6},{7,3},{11,7},{20,16},{24,20},... | collective-permute-start | bytes 1769480 | tf_op jit(solution)/shard_map/ppermute | solution.py:395
  34.8 12.5 %collective-permute-start.3 = (bf16[18,128,128]{2,1,0:T(8,128)(2,1)S(1)}, bf16[18,128,128]{2,1,0:T(8,128)(2,1)S(1)}, u32[]{:S(2)}, u32[]{:S(2)}) collective-permute-start(bf16[18,128,128]{2,1,0:T(8,128)(2,1)S(1)} %collective-permute-done.1.rest_2_), channel_id=1, source_target_pairs={{4,8},{8,12},{5,9},{9,13},{6,10},{10,14},{7,11},{11,15},{20,24},{2... | collective-permute-start | bytes 1769480 | tf_op jit(solution)/shard_map/ppermute | solution.py:396
  36.5 2.2 %copy-start = (bf16[128,128,128]{2,1,0:T(8,128)(2,1)S(1)}, bf16[128,128,128]{2,1,0:T(8,128)(2,1)}, u32[]{:S(2)}) copy-start(bf16[128,128,128]{2,1,0:T(8,128)(2,1)} %weights.3) | copy-start | bytes 12582916
  38.7 8.6 %copy-start.1 = (bf16[128,128,128]{2,1,0:T(8,128)(2,1)S(1)}, bf16[128,128,128]{2,1,0:T(8,128)(2,1)}, u32[]{:S(2)}) copy-start(bf16[128,128,128]{2,1,0:T(8,128)(2,1)} %weights.3) | copy-start | bytes 12582916
  42.3 26.9 %copy-start.2 = (bf16[8,35,4096]{2,0,1:T(8,128)(2,1)S(1)}, bf16[8,35,4096]{2,0,1:T(8,128)(2,1)}, u32[]{:S(2)}) copy-start(bf16[8,35,4096]{2,0,1:T(8,128)(2,1)} %param.6) | copy-start | bytes 6881284
  48.8 2.0 %collective-permute-start.5 = (bf16[16,128,128]{2,1,0:T(8,128)(2,1)S(1)}, bf16[16,128,128]{2,1,0:T(8,128)(2,1)S(1)}, u32[]{:S(2)}, u32[]{:S(2)}) collective-permute-start(bf16[16,128,128]{2,1,0:T(8,128)(2,1)S(1)} %late.1.mine), channel_id=1, source_target_pairs={{0,1},{1,0},{2,3},{3,2},{16,17},{17,16},{18,19},{19,18},{4,5},{5,4... | collective-permute-start | bytes 1572872 | tf_op jit(solution)/shard_map/ppermute | solution.py:330
  48.9 9.2 %collective-permute-start.4 = (bf16[16,128,128]{2,1,0:T(8,128)(2,1)S(1)}, bf16[16,128,128]{2,1,0:T(8,128)(2,1)S(1)}, u32[]{:S(2)}, u32[]{:S(2)}) collective-permute-start(bf16[16,128,128]{2,1,0:T(8,128)(2,1)S(1)} %late.1.mine), channel_id=1, source_target_pairs={{0,2},{1,17},{2,0},{3,19},{16,18},{17,1},{18,16},{19,3},{4,6},{5,2... | collective-permute-start | bytes 1572872 | tf_op jit(solution)/shard_map/ppermute | solution.py:330
  50.8 16.3 %collective-permute-start.6 = (bf16[16,128,128]{2,1,0:T(8,128)(2,1)S(1)}, bf16[16,128,128]{2,1,0:T(8,128)(2,1)S(1)}, u32[]{:S(2)}, u32[]{:S(2)}) collective-permute-start(bf16[16,128,128]{2,1,0:T(8,128)(2,1)S(1)} %collective-permute-done.5.other), channel_id=1, source_target_pairs={{0,2},{1,17},{2,0},{3,19},{16,18},{17,1},{18,16},{19,3},{4,6},{5,2... | collective-permute-start | bytes 1572872 | tf_op jit(solution)/shard_map/ppermute | solution.py:330
  58.2 10.7 %collective-permute-start.9 = (bf16[16,128,128]{2,1,0:T(8,128)(2,1)S(1)}, bf16[16,128,128]{2,1,0:T(8,128)(2,1)S(1)}, u32[]{:S(2)}, u32[]{:S(2)}) collective-permute-start(bf16[16,128,128]{2,1,0:T(8,128)(2,1)S(1)} %collective-permute-done.4.r1), channel_id=1, source_target_pairs={{0,16},{1,3},{2,18},{3,1},{16,0},{17,19},{18,2},{19,17},{4,20},{5,... | collective-permute-start | bytes 1572872 | tf_op jit(solution)/shard_map/ppermute | solution.py:330
  59.7 9.5 %collective-permute-start.7 = (bf16[16,128,128]{2,1,0:T(8,128)(2,1)S(1)}, bf16[16,128,128]{2,1,0:T(8,128)(2,1)S(1)}, u32[]{:S(2)}, u32[]{:S(2)}) collective-permute-start(bf16[16,128,128]{2,1,0:T(8,128)(2,1)S(1)} %collective-permute-done.4.r1), channel_id=1, source_target_pairs={{0,1},{1,0},{2,3},{3,2},{16,17},{17,16},{18,19},{19,18},{4,5},{5,4... | collective-permute-start | bytes 1572872 | tf_op jit(solution)/shard_map/ppermute | solution.py:330
  67.2 2.1 %collective-permute-start.8 = (bf16[16,128,128]{2,1,0:T(8,128)(2,1)S(1)}, bf16[16,128,128]{2,1,0:T(8,128)(2,1)S(1)}, u32[]{:S(2)}, u32[]{:S(2)}) collective-permute-start(bf16[16,128,128]{2,1,0:T(8,128)(2,1)S(1)} %collective-permute-done.6.r2), channel_id=1, source_target_pairs={{0,1},{1,0},{2,3},{3,2},{16,17},{17,16},{18,19},{19,18},{4,5},{5,4... | collective-permute-start | bytes 1572872 | tf_op jit(solution)/shard_map/ppermute | solution.py:330
  68.9 1.9 %collective-permute-start.10 = (bf16[16,128,128]{2,1,0:T(8,128)(2,1)S(1)}, bf16[16,128,128]{2,1,0:T(8,128)(2,1)S(1)}, u32[]{:S(2)}, u32[]{:S(2)}) collective-permute-start(bf16[16,128,128]{2,1,0:T(8,128)(2,1)S(1)} %collective-permute-done.9.d), channel_id=1, source_target_pairs={{0,1},{1,0},{2,3},{3,2},{16,17},{17,16},{18,19},{19,18},{4,5},{5,4... | collective-permute-start | bytes 1572872 | tf_op jit(solution)/shard_map/ppermute | solution.py:330
  71.8 8.7 %collective-permute-start.11 = (bf16[280,128]{1,0:T(8,128)(2,1)S(1)}, bf16[280,128]{1,0:T(8,128)(2,1)S(1)}, u32[]{:S(2)}, u32[]{:S(2)}) collective-permute-start(bf16[280,128]{1,0:T(8,128)(2,1)S(1)} %get-tuple-element.10), channel_id=1, source_target_pairs={{0,4},{4,8},{8,12},{12,0},{1,5},{5,9},{9,13},{13,1},{2,6},{6,10},{... | collective-permute-start | bytes 215048 | tf_op jit(solution)/shard_map/ppermute | solution.py:415
  74.1 9.4 %collective-permute-start.12 = (bf16[280,128]{1,0:T(8,128)(2,1)S(1)}, bf16[280,128]{1,0:T(8,128)(2,1)S(1)}, u32[]{:S(2)}, u32[]{:S(2)}) collective-permute-start(bf16[280,128]{1,0:T(8,128)(2,1)S(1)} %get-tuple-element.11), channel_id=1, source_target_pairs={{0,8},{4,12},{8,0},{12,4},{1,9},{5,13},{9,1},{13,5},{2,10},{6,14},... | collective-permute-start | bytes 215048 | tf_op jit(solution)/shard_map/ppermute | solution.py:415
  78.2 5.4 %collective-permute-start.13 = (bf16[280,128]{1,0:T(8,128)(2,1)S(1)}, bf16[280,128]{1,0:T(8,128)(2,1)S(1)}, u32[]{:S(2)}, u32[]{:S(2)}) collective-permute-start(bf16[280,128]{1,0:T(8,128)(2,1)S(1)} %get-tuple-element.12), channel_id=1, source_target_pairs={{0,12},{4,0},{8,4},{12,8},{1,13},{5,1},{9,5},{13,9},{2,14},{6,2},{... | collective-permute-start | bytes 215048 | tf_op jit(solution)/shard_map/ppermute | solution.py:415

commit v3 on v2

--- a/solution.py
+++ b/solution.py
@@ -9,10 +9,23 @@
 
 PLANE = ("member", "day")
 LANES = 128
-CHUNKS = 1
+CHUNKS = 2
 GROUPS = 2 * CHUNKS
 WIDTH = LANES // GROUPS
 UNROLL = 16
+COST_EARLY = (11, 0.4)
+COST_LATE = (8, 0.2)
+COST_NEAR = (5, 0.6)
+COST_AWAY = (5, 0.6)
+DIRECT = True
+TIE_EARLY = True
+TIE_LATE = 0
+TIE_HOP = True
+TIE_SWAP = ["s1"]
+TIE_RS = []
+TIE_B = False
+PARTS = 3
+TIE_WHAT = 2
 MIB = 2**20
 
 VMEM = pl.BlockSpec(memory_space=pltpu.VMEM)
@@ -26,6 +39,12 @@
 
 def params(mib):
     return pltpu.CompilerParams(vmem_limit_bytes=mib * MIB)
+
+
+def cost(mib, gflop):
+    return pl.CostEstimate(
+        flops=int(gflop * 1e9), bytes_accessed=int(mib * MIB), transcendentals=0
+    )
 
 
 def group_of(shape):
@@ -39,11 +58,11 @@
     return out
 
 
-def pack_kernel(parts, patterns, *rest):
-    outs, held, sems = rest[:CHUNKS], rest[-2], rest[-1]
+def pack_kernel(parts, chunk, patterns, *rest):
+    out, held, sems = rest[-3:]
     p = place()
     chip, core = p // 2, lax.rem(p, 2)
-    count = outs[0].shape[0]
+    count = out.shape[0]
     step = count // parts
     columns = pl.ds(pl.multiple_of(chip * LANES, LANES), LANES)
     copies = []
@@ -56,12 +75,11 @@
                 )
             )
             copies[-1].start()
-    shape = (GROUPS * LANES, CHUNKS * LANES)
+    shape = (GROUPS * LANES, LANES)
     k = lax.broadcasted_iota(jnp.int32, shape, 0)
     n = lax.broadcasted_iota(jnp.int32, shape, 1)
-    chunk, lane_out = n // LANES, n % LANES
-    wanted = chunk * (LANES // CHUNKS) + core * WIDTH + lane_out % WIDTH
-    chosen = (k // LANES == lane_out // WIDTH) & (k % LANES == wanted)
+    wanted = chunk * (LANES // CHUNKS) + core * WIDTH + n % WIDTH
+    chosen = (k // LANES == n // WIDTH) & (k % LANES == wanted)
     choose = jnp.where(chosen, 1.0, 0.0).astype(held.dtype)
     for part in range(parts):
         for group in range(GROUPS):
@@ -71,29 +89,28 @@
                 held[(group * count + j) * LANES : (group * count + j + 1) * LANES, :]
                 for group in range(GROUPS)
             ]
-            both = jnp.dot(
+            out[j] = jnp.dot(
                 jnp.concatenate(blocks, 1), choose, preferred_element_type=jnp.float32
-            ).astype(held.dtype)
-            for chunk in range(CHUNKS):
-                outs[chunk][j] = both[:, chunk * LANES : (chunk + 1) * LANES]
-
-
-def pack(patterns):
+            ).astype(out.dtype)
+
+
+def pack(patterns, chunk, after):
     rows = patterns.shape[0]
     count = rows // LANES // GROUPS
-    parts = 3
+    parts = PARTS
     return pl.pallas_call(
-        functools.partial(pack_kernel, parts),
-        in_specs=[pl.BlockSpec(memory_space=pltpu.HBM)],
-        out_specs=[VMEM] * CHUNKS,
-        out_shape=[jax.ShapeDtypeStruct((count, LANES, LANES), patterns.dtype)] * CHUNKS,
+        functools.partial(pack_kernel, parts, chunk),
+        in_specs=[ANY] * (1 + len(after)),
+        out_specs=VMEM,
+        out_shape=jax.ShapeDtypeStruct((count, LANES, LANES), patterns.dtype),
         scratch_shapes=[
             pltpu.VMEM((rows, LANES), patterns.dtype),
             pltpu.SemaphoreType.DMA((parts, GROUPS)),
         ],
-        compiler_params=params(8),
+        compiler_params=params(58),
+        cost_estimate=cost(2.3, 0.15),
         name="pack",
-    )(patterns)
+    )(patterns, *after)
 
 
 def add_tiles(table, start, end, weights, held, total):
@@ -143,6 +160,7 @@
             pltpu.SemaphoreType.DMA((len(bands),)),
         ],
         compiler_params=params(10 + count * len(bands) * LANES * LANES * 2 // MIB),
+        cost_estimate=cost(*COST_EARLY),
         name="early",
     )(table, weights, *bands)
 
@@ -192,38 +210,30 @@
             pltpu.SemaphoreType.DMA((2,)),
         ],
         compiler_params=params(14),
+        cost_estimate=cost(*COST_LATE),
         name="late",
     )(table, weights, total, right, left)
 
 
-def products_of(fields, pieces, flip):
+def products_of(fields, pieces):
     depth = fields.shape[1] // GROUPS
     across = lax.rem(place(), 4) // 2
     group = group_of((depth, LANES))
     values = [piece[...].reshape(depth, LANES) for piece in pieces]
-    if CHUNKS == 1:
-        sets = [[(values[0], 0), (values[1], 1)], [(values[2], 0), (values[3], 1)]]
-    else:
-        near, away = 2 * across, 2 * (1 - across)
-        sets = [
-            [(values[0], near), (values[1], near + 1), (values[2], away), (values[3], away + 1)]
-        ]
-    totals = [None] * len(sets)
+    near, away = 2 * across, 2 * (1 - across)
+    members = [near, near + 1, away, away + 1]
+    total = None
     for h in range(GROUPS):
-        rhs = []
-        for members in sets:
-            index = [lax.rem(i + h, GROUPS) for _, i in members]
-            rhs.append(pick(lambda k: group == index[k], [value for value, _ in members]))
-        rhs = jnp.concatenate(rhs, 1) if len(rhs) > 1 else rhs[0]
-        product = jnp.dot(
-            fields[:, h * depth : (h + 1) * depth], rhs, preferred_element_type=jnp.float32
+        index = [lax.rem(i + h, GROUPS) for i in members]
+        term = jnp.dot(
+            fields[:, h * depth : (h + 1) * depth],
+            pick(lambda k: group == index[k], values),
+            preferred_element_type=jnp.float32,
         )
-        for s in range(len(sets)):
-            term = product[:, s * LANES : (s + 1) * LANES]
-            if h:
-                term = pltpu.roll(term, LANES - h * WIDTH, 1)
-            totals[s] = term if totals[s] is None else totals[s] + term
-    return totals
+        if h:
+            term = pltpu.roll(term, LANES - h * WIDTH, 1)
+        total = term if total is None else total + term
+    return total
 
 
 def by_core(even, odd, body):
@@ -238,28 +248,34 @@
         body(odd)
 
 
-def near_kernel(fields, mine, other, r1, r2, s1, s2, out):
+def near_kernel(fields, mine, other, *rest):
+    x_even, x_odd, out = rest[:2], rest[2:4], rest[4]
+
     def body(pieces):
-        for s, total in enumerate(products_of(fields, pieces, 0)):
-            out[s] = total
-
-    by_core([mine, other, r1, r2], [other, mine, s1, s2], body)
-
-
-def away_kernel(fields, r1, r2, s1, s2, d, s3, out):
-    def body(pieces):
-        for s, total in enumerate(products_of(fields, pieces, 1)):
-            out[s] = total
-
-    by_core([s2, s1, d, s3], [r2, r1, s3, d], body)
-
-
-def last_kernel(split, fields, r1, r2, s1, s2, d, s3, *rest):
-    count = 2 * CHUNKS - 1
-    earlier, outs = rest[:count], rest[count:]
-    p = place()
-    chip = p // 2
+        out[...] = products_of(fields, pieces)
+
+    by_core([mine, other, *x_even], [other, mine, *x_odd], body)
+
+
+def near_scores(fields, pieces):
+    rows = fields.shape[0]
+    return pl.pallas_call(
+        near_kernel,
+        in_specs=[VMEM] * (1 + len(pieces)),
+        out_specs=VMEM,
+        out_shape=jax.ShapeDtypeStruct((rows, LANES), jnp.float32),
+        compiler_params=params(16),
+        cost_estimate=cost(*COST_NEAR),
+        name="near",
+    )(fields, *pieces)
+
+
+def away_kernel(split, fields, *rest):
+    even, odd, first, outs = rest[:4], rest[4:8], rest[8], rest[9:]
+    m = place() // 4
     half = LANES // 2
+    rows = fields.shape[0]
+    folded = outs[0].shape[-2]
 
     def emit(to, value):
         if not split:
@@ -273,51 +289,63 @@
                 out[...] = value.astype(out.dtype)
 
     def body(pieces):
-        totals = products_of(fields, pieces, 1)
-        if CHUNKS == 1:
-            for relative in range(2):
-                emit(chip ^ relative, earlier[0][relative])
-                emit(chip ^ (2 + relative), totals[relative])
-            return
-        low = lax.broadcasted_iota(jnp.int32, totals[0].shape, 1) < half
-        for e in range(2):
-            first = earlier[e][0]
-            second = totals[0] if e else earlier[2][0]
-            row = 2 * ((p // 4) ^ e)
-            emit(row, jnp.where(low, first, pltpu.roll(second, half, 1)))
-            emit(row + 1, jnp.where(low, pltpu.roll(first, half, 1), second))
-
-    by_core([s2, s1, d, s3], [r2, r1, s3, d], body)
-
-
-def half_scores(kernel, fields, pieces, name):
-    rows = fields.shape[0]
-    return pl.pallas_call(
-        kernel,
-        in_specs=[VMEM] * (1 + len(pieces)),
-        out_specs=VMEM,
-        out_shape=jax.ShapeDtypeStruct((2 // CHUNKS, rows, LANES), jnp.float32),
-        compiler_params=params(16),
-        name=name,
-    )(fields, *pieces)
-
-
-def last_scores(fields, pieces, earlier, split):
-    rows = fields.shape[0]
+        low = lax.broadcasted_iota(jnp.int32, (folded, LANES), 1) < half
+        for e, total in enumerate([first[...], products_of(fields, pieces)]):
+            turned = pltpu.roll(total, half, 1)
+            top, bottom = slice(0, folded), slice(rows - folded, rows)
+            emit(2 * (m ^ e), jnp.where(low, total[top], turned[bottom]))
+            emit(2 * (m ^ e) + 1, jnp.where(low, turned[top], total[bottom]))
+
+    by_core(even, odd, body)
+
+
+def away_scores(fields, pieces, near, split):
+    folded = fold_rows(fields.shape[0])
     if split:
-        out_shape = [jax.ShapeDtypeStruct((rows, LANES), jnp.float32)] + [
-            jax.ShapeDtypeStruct((rows, LANES), jnp.bfloat16)
+        out_shape = [jax.ShapeDtypeStruct((folded, LANES), jnp.float32)] + [
+            jax.ShapeDtypeStruct((folded, LANES), jnp.bfloat16)
         ] * 3
     else:
-        out_shape = [jax.ShapeDtypeStruct((4, rows, LANES), jnp.float32)]
+        out_shape = [jax.ShapeDtypeStruct((4, folded, LANES), jnp.float32)]
     return pl.pallas_call(
-        functools.partial(last_kernel, split),
-        in_specs=[VMEM] * (1 + len(pieces) + len(earlier)),
+        functools.partial(away_kernel, split),
+        in_specs=[VMEM] * (2 + len(pieces)),
         out_specs=[VMEM] * len(out_shape),
         out_shape=out_shape,
         compiler_params=params(18),
-        name="last",
-    )(fields, *pieces, *earlier)
+        cost_estimate=cost(*COST_AWAY),
+        name="away",
+    )(fields, *pieces, near)
+
+
+def fold_rows(rows):
+    return -(-rows // 32) * 16
+
+
+def final_kernel(*refs):
+    parts, out = refs[:-1], refs[-1]
+    rows, half = out.shape[0], LANES // 2
+    folded = parts[0].shape[0]
+    low = lax.broadcasted_iota(jnp.int32, (folded, LANES), 1) < half
+    a, b = [
+        parts[c][...] + sum(part[...].astype(jnp.float32) for part in parts[c + 1 : c + 4])
+        for c in (0, 4)
+    ]
+    skip = 2 * folded - rows
+    out[:folded, :] = jnp.where(low, a, pltpu.roll(b, half, 1))
+    below = jnp.where(low, pltpu.roll(a, half, 1), b)
+    out[folded:, :] = below[skip:]
+
+
+def final(parts, rows):
+    return pl.pallas_call(
+        final_kernel,
+        in_specs=[VMEM] * len(parts),
+        out_specs=VMEM,
+        out_shape=jax.ShapeDtypeStruct((rows, LANES), jnp.float32),
+        compiler_params=params(8),
+        name="final",
+    )(*parts)
 
 
 def plane_permute(x, to):
@@ -342,13 +370,21 @@
     return plane_permute(x, lambda m, a, c: (1 - m, a, c) if c == 0 else (m, 1 - a, c))
 
 
-def gather_plane(piece):
-    other = over_core(piece)
+def gather_plane(piece, after):
+    def tie(x, name):
+        return lax.optimization_barrier((x, *after[name]))[0] if after.get(name) else x
+
     r1 = over_first(piece)
-    r2 = over_first(other)
-    d = over_second(r1)
-    s1, s2, s3 = over_core(r1), over_core(r2), over_core(d)
-    return (piece, other, r1, r2, s1, s2), (r1, r2, s1, s2, d, s3)
+    other = over_core(tie(piece, "other") if DIRECT else piece)
+    if DIRECT:
+        r2 = over_second(piece)
+    else:
+        r2 = over_first(other)
+    d = over_second(tie(r1, "d"))
+    s1, s2, s3 = over_core(tie(r1, "s1")), over_core(tie(r2, "s2")), over_core(tie(d, "s3"))
+    if DIRECT:
+        return (piece, other, r1, s2, s1, r2), (r2, s1, d, s3, s2, r1, s3, d), r1, r2, d
+    return (piece, other, r1, r2, s1, s2), (s2, s1, d, s3, r2, r1, s3, d), r1, r2, d
 
 
 def tile_table(tile_source, tile_band, tile_block, blocks, bands, z):
@@ -386,36 +422,66 @@
     table = tile_table(
         tile_source, tile_band, tile_block, patterns.shape[0] // LANES, bands, z
     )
-    owns = pack(patterns)
-    totals, rights, lefts = [], [], []
+    owns = []
+    for chunk in range(CHUNKS):
+        owns.append(pack(patterns, chunk, owns[-1:]))
+    totals, rights, lefts, nears = [], [], [], []
     for own in owns:
         if bands == 4:
             from_left = lax.ppermute(own, "tile", [(i, (i + 1) % 4) for i in range(4)])
             from_right = lax.ppermute(own, "tile", [(i, (i + 3) % 4) for i in range(4)])
+            near = [own, from_right, from_left]
+            if totals and TIE_HOP:
+                totals[-1], from_right, from_left = lax.optimization_barrier(
+                    (totals[-1], from_right, from_left)
+                )
             rights.append(lax.ppermute(from_right, "tile", [(1, 0), (2, 1)]))
             lefts.append(lax.ppermute(from_left, "tile", [(1, 2), (2, 3)]))
-            near = [own, from_right, from_left]
         else:
             gathered = lax.all_gather(own, "tile", axis=0)
             near = [gathered.reshape((-1,) + gathered.shape[2:])]
             rights.append(own)
             lefts.append(own)
+        nears.append(near)
+        if TIE_B and len(nears) == 2:
+            continue
         totals.append(early(table, remap_tiles, near, source_blocks))
-    earlier = []
+    if TIE_EARLY and not TIE_B:
+        totals = list(lax.optimization_barrier(totals))
+    sums, done = [], {}
     for chunk in range(CHUNKS):
         piece = late(table, remap_tiles, totals[chunk], rights[chunk], lefts[chunk])
-        near, away = gather_plane(piece)
-        earlier.append(half_scores(near_kernel, rows, near, "near"))
-        if chunk < CHUNKS - 1:
-            earlier.append(half_scores(away_kernel, rows, away, "away"))
-    parts = last_scores(rows, away, earlier, bands == 4)
+        if TIE_B and chunk == 0:
+            own, *_ = lax.optimization_barrier((nears[1][0], piece))
+            totals.append(early(table, remap_tiles, [own, *nears[1][1:]], source_blocks))
+        near, away, r1, r2, d = gather_plane(piece, done)
+        if chunk == 0 and TIE_LATE:
+            tied = {1: near[1:2], 2: (r1,), 3: (r2,), 4: (d,), 5: (r1, near[1])}[TIE_LATE]
+            totals[1], *_ = lax.optimization_barrier((totals[1], *tied))
+        if done_near := done.get("near"):
+            near = lax.optimization_barrier((*near, *done_near))[: len(near)]
+        part = near_scores(rows, near)
+        parts = list(away_scores(rows, away, part, bands == 4))
+        done = {}
+        for name in TIE_SWAP:
+            done.setdefault(name, []).append(part if TIE_WHAT == 1 else parts[0])
+        if bands == 4:
+            for k in (1, 2, 3):
+                pairs = [(i, (i + k) % 4) for i in range(4)]
+                parts[k] = lax.ppermute(parts[k], "tile", pairs)
+            sums += parts
+            for name in TIE_RS:
+                done.setdefault(name, []).extend(parts[1:4])
+        else:
+            folded = parts[0]
+            half, skip = LANES // 2, 2 * folded.shape[1] - row_count
+            sums.append(
+                jnp.concatenate([folded[:, :, :half], folded[:, skip:, half:]], 1)
+            )
     if bands == 4:
-        result = parts[0]
-        for k in (1, 2, 3):
-            moved = lax.ppermute(parts[k], "tile", [(i, (i + k) % 4) for i in range(4)])
-            result = result + moved.astype(jnp.float32)
+        result = final(sums, row_count)
     else:
-        partial = parts[0].transpose(1, 0, 2).reshape(row_count, pattern_count)
+        partial = jnp.concatenate(sums, 2).transpose(1, 0, 2).reshape(row_count, pattern_count)
         result = lax.psum_scatter(partial, "tile", scatter_dimension=1, tiled=True)
     return result.reshape(var_count, day_count, pattern_count // bands).transpose(1, 0, 2)
 

time: 84 us -> 80.5 us (0.958); the launches traced: 84.3 us -> 80 us
  waiting for transfers between devices: 49 us -> 23 us
  starting transfers between devices: 20.2 us -> 32.8 us
  Pallas kernels: 8.14 us -> 20.1 us
  local copies, waits for them, and re-layouts: 4.54 us -> 2.22 us
    ppermute x1 -> x2, waiting for transfers between devices: 13.1 us -> 0.22 us  [on_device(): from_right = lax.ppermute(own, 'tile', [(i, (i + 3) % 4) for i in range(4)])]
    ppermute x7 -> x14, waiting for transfers between devices: 16 us -> 7.62 us  [plane_permute(): return lax.ppermute(x, PLANE, pairs)]
    pallas_call x3 -> x7, Pallas kernels: 2.97 us -> 10.1 us  [the longest x2 5.27 us: pack(): pl.pallas_call(functools.partial(pack_kernel, parts, chunk), in_specs=[AN...]
    ppermute x7 -> x14, starting transfers between devices: 4.99 us -> 9.58 us  [plane_permute(): return lax.ppermute(x, PLANE, pairs)]
    ppermute x1 -> x2, starting transfers between devices: 5.11 us -> 8.98 us  [on_device(): from_right = lax.ppermute(own, 'tile', [(i, (i + 3) % 4) for i in range(4)])]
    ppermute x1 -> x2, waiting for transfers between devices: 4.98 us -> 1.63 us  [on_device(): rights.append(lax.ppermute(from_right, 'tile', [(1, 0), (2, 1)]))]
    pallas_call x1 -> x2, Pallas kernels: 3.63 us -> 6.18 us  [early(): pl.pallas_call(early_kernel, in_specs=[SMEM, VMEM] + [ANY] * len(bands),...]
    pallas_call x1 -> x2, Pallas kernels: 1.54 us -> 3.86 us  [late(): pl.pallas_call(late_kernel, in_specs=[SMEM, VMEM, ANY, ANY, ANY], out_spe...]
  transfers between devices with their start and end apart: 14 -> 28, of which waited for: 11 -> 10; matrix products, arithmetic and copies ran while one was open for 2% -> 2% of each run, Pallas kernels for 5% -> 21%
where the time goes in v3:
time: 80.5 us; the launch traced here: 80 us
  starting transfers between devices  32.8 us (41%)
  waiting for transfers between devices  23 us (29%)
  Pallas kernels  20.1 us (25%)
  local copies, waits for them, and re-layouts  2.22 us (3%)
  other arithmetic  1.62 us (2%)
    ppermute x2, waiting for transfers between devices, on_device(): from_left = lax.ppermute(own, 'tile', [(i, (i + 1) % 4) for i in range(4)])  10.9 us
    ppermute x6, starting transfers between devices, on_device(): parts[k] = lax.ppermute(parts[k], 'tile', pairs)  10.3 us
    ppermute x14, starting transfers between devices, plane_permute(): return lax.ppermute(x, PLANE, pairs)  9.58 us
    ppermute x2, starting transfers between devices, on_device(): from_right = lax.ppermute(own, 'tile', [(i, (i + 3) % 4) for i in range(4)])  8.98 us
    ppermute x14, waiting for transfers between devices, plane_permute(): return lax.ppermute(x, PLANE, pairs)  7.62 us
    pallas_call x2, Pallas kernels, early(): pl.pallas_call(early_kernel, in_specs=[SMEM, VMEM] + [ANY] * len(bands),...  6.18 us
    pallas_call x2, Pallas kernels, pack(): pl.pallas_call(functools.partial(pack_kernel, parts, chunk), in_specs=[AN...  5.27 us
    pallas_call x2, Pallas kernels, late(): pl.pallas_call(late_kernel, in_specs=[SMEM, VMEM, ANY, ANY, ANY], out_spe...  3.86 us
  transfers between devices with their start and end apart: 28, of which 10 were waited for; matrix products, arithmetic and copies ran while one was open for 2% of the time, Pallas kernels for 21%

profile of v3, /device:TPU:0, one launch (start us, length us, event | category | flops | bytes accessed | tf_op | source)
XLA Modules:
  0.0 80.0 jit_solution(7257224627709247918)
XLA Ops:
  0.0 2.6 %pack.2.rest_0_ = bf16[9,128,128]{2,1,0:T(8,128)(2,1)} custom-call(bf16[4608,512]{1,0:T(8,128)(2,1)} %patterns.3), custom_call_target="tpu_custom_call" | custom-call | flops 150000000 | bytes 2411724 | tf_op jit(solution)/shard_map/pack/pallas_call | solution.py:101
  2.7 5.1 %collective-permute-start = (bf16[9,128,128]{2,1,0:T(8,128)(2,1)}, bf16[9,128,128]{2,1,0:T(8,128)(2,1)S(1)}, u32[]{:S(2)}, u32[]{:S(2)}) collective-permute-start(bf16[9,128,128]{2,1,0:T(8,128)(2,1)} %pack.2.rest_0_), channel_id=1, source_target_pairs={{0,12},{4,0},{8,4},{12,8},{1,13},{5,1},{9,5},{13,9},{2,14},{6,2},{... | collective-permute-start | bytes 884744 | tf_op jit(solution)/shard_map/ppermute | solution.py:432
  7.8 2.6 %pack.3.rest_0_ = bf16[9,128,128]{2,1,0:T(8,128)(2,1)} custom-call(bf16[4608,512]{1,0:T(8,128)(2,1)} %patterns.3, bf16[9,128,128]{2,1,0:T(8,128)(2,1)} %pack.2.rest_0_), custom_call_target="tpu_custom_call" | custom-call | flops 150000000 | bytes 2411724 | tf_op jit(solution)/shard_map/pack/pallas_call | solution.py:101
  10.4 3.9 %collective-permute-start.2 = (bf16[9,128,128]{2,1,0:T(8,128)(2,1)}, bf16[9,128,128]{2,1,0:T(8,128)(2,1)S(1)}, u32[]{:S(2)}, u32[]{:S(2)}) collective-permute-start(bf16[9,128,128]{2,1,0:T(8,128)(2,1)} %pack.3.rest_0_), channel_id=1, source_target_pairs={{0,12},{4,0},{8,4},{12,8},{1,13},{5,1},{9,5},{13,9},{2,14},{6,2},{... | collective-permute-start | bytes 884744 | tf_op jit(solution)/shard_map/ppermute | solution.py:432
  14.3 0.6 fusion
  15.0 0.2 convert_reduce_fusion
  15.2 0.1 select_reduce_fusion
  15.3 0.2 collective-permute-done.rest_1_
  15.5 1.3 %collective-permute-start.4 = (bf16[9,128,128]{2,1,0:T(8,128)(2,1)S(1)}, bf16[9,128,128]{2,1,0:T(8,128)(2,1)S(1)}, u32[]{:S(2)}, u32[]{:S(2)}) collective-permute-start(bf16[9,128,128]{2,1,0:T(8,128)(2,1)S(1)} %collective-permute-done.rest_1_), channel_id=1, source_target_pairs={{4,0},{8,4},{5,1},{9,5},{6,2},{10,6},{7,3},{11,7},{20,16},{24,20},... | collective-permute-start | bytes 884744 | tf_op jit(solution)/shard_map/ppermute | solution.py:438
  16.8 5.9 %collective-permute-done.1.rest_2_ = bf16[9,128,128]{2,1,0:T(8,128)(2,1)S(1)} collective-permute-done((bf16[9,128,128]{2,1,0:T(8,128)(2,1)}, bf16[9,128,128]{2,1,0:T(8,128)(2,1)S(1)}, u32[]{:S(2)}, u32[]{:S(2)}) %collective-permute-start.1) | collective-permute-done | bytes 294944 | tf_op jit(solution)/shard_map/ppermute | solution.py:431
  22.7 0.7 collective-permute-start.5
  23.4 0.7 compare_select_fusion.6.table
  24.0 2.2 %copy-done = bf16[128,128,128]{2,1,0:T(8,128)(2,1)S(1)} copy-done((bf16[128,128,128]{2,1,0:T(8,128)(2,1)S(1)}, bf16[128,128,128]{2,1,0:T(8,128)(2,1)}, u32[]{:S(2)}) %copy-start) | copy-done | bytes 4194328
  26.2 3.1 %early.2.given = f32[32,128,128]{2,1,0:T(8,128)S(1)} custom-call(s32[160]{0:T(256)S(1)} %compare_select_fusion.6.table, bf16[128,128,128]{2,1,0:T(8,128)(2,1)S(1)} %copy-done, bf16[9,128,128]{2,1,0:T(8,128)(2,1)S(1)} %copy-done.3, bf16[9,128,128]{2,1,0:T(8,128)(2,1)S(1)} %collective-permute-done.rest_1_, bf16[9,128,128]{2,1,0:T(8,128)(2,1)S(1)} %collective-permute-done.1.rest_2_), custom_call_target="tpu_custom_call" | custom-call | flops 400000000 | bytes 11534336 | tf_op jit(solution)/shard_map/early/pallas_call | solution.py:153
  29.3 5.0 %collective-permute-done.3.rest_2_ = bf16[9,128,128]{2,1,0:T(8,128)(2,1)S(1)} collective-permute-done((bf16[9,128,128]{2,1,0:T(8,128)(2,1)}, bf16[9,128,128]{2,1,0:T(8,128)(2,1)S(1)}, u32[]{:S(2)}, u32[]{:S(2)}) %collective-permute-start.3) | collective-permute-done | bytes 294944 | tf_op jit(solution)/shard_map/ppermute | solution.py:431
  34.3 1.3 %collective-permute-start.16 = (bf16[9,128,128]{2,1,0:T(8,128)(2,1)S(1)}, bf16[9,128,128]{2,1,0:T(8,128)(2,1)S(1)}, u32[]{:S(2)}, u32[]{:S(2)}) collective-permute-start(bf16[9,128,128]{2,1,0:T(8,128)(2,1)S(1)} %collective-permute-done.2.rest_1_), channel_id=1, source_target_pairs={{4,0},{8,4},{5,1},{9,5},{6,2},{10,6},{7,3},{11,7},{20,16},{24,20},... | collective-permute-start | bytes 884744 | tf_op jit(solution)/shard_map/ppermute | solution.py:438
  35.6 0.7 collective-permute-start.17
  36.3 3.1 %early.3.given = f32[32,128,128]{2,1,0:T(8,128)S(1)} custom-call(s32[160]{0:T(256)S(1)} %compare_select_fusion.6.table, bf16[128,128,128]{2,1,0:T(8,128)(2,1)S(1)} %copy-done.1, bf16[9,128,128]{2,1,0:T(8,128)(2,1)S(1)} %copy-done.4, bf16[9,128,128]{2,1,0:T(8,128)(2,1)S(1)} %collective-permute-done.2.rest_1_, ...), custom_call_target="tpu_custom_call" | custom-call | flops 400000000 | bytes 11534336 | tf_op jit(solution)/shard_map/early/pallas_call | solution.py:153
  39.5 1.9 %late.2.mine = bf16[8,128,128]{2,1,0:T(8,128)(2,1)S(1)} custom-call(s32[160]{0:T(256)S(1)} %compare_select_fusion.6.table, bf16[128,128,128]{2,1,0:T(8,128)(2,1)S(1)} %copy-done.1, f32[32,128,128]{2,1,0:T(8,128)S(1)} %early.2.given, bf16[9,128,128]{2,1,0:T(8,128)(2,1)S(1)} %collective-permute-done.4.right, bf16[9,128,128]{2,1,0:T(8,128)(2,1)S(1)} %collective-permute-done.5.left), custom_call_target="tpu_custom_call" | custom-call | flops 200000000 | bytes 8388608 | tf_op jit(solution)/shard_map/late/pallas_call | solution.py:202
  41.4 1.6 %collective-permute-start.7 = (bf16[8,128,128]{2,1,0:T(8,128)(2,1)S(1)}, bf16[8,128,128]{2,1,0:T(8,128)(2,1)S(1)}, u32[]{:S(2)}, u32[]{:S(2)}) collective-permute-start(bf16[8,128,128]{2,1,0:T(8,128)(2,1)S(1)} %late.2.mine), channel_id=1, source_target_pairs={{0,2},{1,17},{2,0},{3,19},{16,18},{17,1},{18,16},{19,3},{4,6},{5,2... | collective-permute-start | bytes 786440 | tf_op jit(solution)/shard_map/ppermute | solution.py:358
  43.0 1.6 %collective-permute-done.16.right = bf16[9,128,128]{2,1,0:T(8,128)(2,1)S(1)} collective-permute-done((bf16[9,128,128]{2,1,0:T(8,128)(2,1)S(1)}, bf16[9,128,128]{2,1,0:T(8,128)(2,1)S(1)}, u32[]{:S(2)}, u32[]{:S(2)}) %collective-permute-start.16) | collective-permute-done | bytes 294944 | tf_op jit(solution)/shard_map/ppermute | solution.py:438
  44.6 1.9 %late.3.mine = bf16[8,128,128]{2,1,0:T(8,128)(2,1)S(1)} custom-call(s32[160]{0:T(256)S(1)} %compare_select_fusion.6.table, bf16[128,128,128]{2,1,0:T(8,128)(2,1)S(1)} %copy-done.1, f32[32,128,128]{2,1,0:T(8,128)S(1)} %early.3.given, bf16[9,128,128]{2,1,0:T(8,128)(2,1)S(1)} %collective-permute-done.16.right, bf16[9,128,128]{2,1,0:T(8,128)(2,1)S(1)} %collective-permute-done.17.left), custom_call_target="tpu_custom_call" | custom-call | flops 200000000 | bytes 8388608 | tf_op jit(solution)/shard_map/late/pallas_call | solution.py:202
  46.5 1.7 %collective-permute-start.19 = (bf16[8,128,128]{2,1,0:T(8,128)(2,1)S(1)}, bf16[8,128,128]{2,1,0:T(8,128)(2,1)S(1)}, u32[]{:S(2)}, u32[]{:S(2)}) collective-permute-start(bf16[8,128,128]{2,1,0:T(8,128)(2,1)S(1)} %late.3.mine), channel_id=1, source_target_pairs={{0,2},{1,17},{2,0},{3,19},{16,18},{17,1},{18,16},{19,3},{4,6},{5,2... | collective-permute-start | bytes 786440 | tf_op jit(solution)/shard_map/ppermute | solution.py:358
  48.3 1.5 %collective-permute-start.6 = (bf16[8,128,128]{2,1,0:T(8,128)(2,1)S(1)}, bf16[8,128,128]{2,1,0:T(8,128)(2,1)S(1)}, u32[]{:S(2)}, u32[]{:S(2)}) collective-permute-start(bf16[8,128,128]{2,1,0:T(8,128)(2,1)S(1)} %late.2.mine), channel_id=1, source_target_pairs={{0,16},{1,3},{2,18},{3,1},{16,0},{17,19},{18,2},{19,17},{4,20},{5,... | collective-permute-start | bytes 786440 | tf_op jit(solution)/shard_map/ppermute | solution.py:358
  49.8 0.5 collective-permute-start.9
  50.3 1.5 %collective-permute-start.18 = (bf16[8,128,128]{2,1,0:T(8,128)(2,1)S(1)}, bf16[8,128,128]{2,1,0:T(8,128)(2,1)S(1)}, u32[]{:S(2)}, u32[]{:S(2)}) collective-permute-start(bf16[8,128,128]{2,1,0:T(8,128)(2,1)S(1)} %late.3.mine), channel_id=1, source_target_pairs={{0,16},{1,3},{2,18},{3,1},{16,0},{17,19},{18,2},{19,17},{4,20},{5,... | collective-permute-start | bytes 786440 | tf_op jit(solution)/shard_map/ppermute | solution.py:358
  51.8 4.0 %collective-permute-done.19.rest_0_.rest_5_ = bf16[8,128,128]{2,1,0:T(8,128)(2,1)S(1)} collective-permute-done((bf16[8,128,128]{2,1,0:T(8,128)(2,1)S(1)}, bf16[8,128,128]{2,1,0:T(8,128)(2,1)S(1)}, u32[]{:S(2)}, u32[]{:S(2)}) %collective-permute-start.19) | collective-permute-done | bytes 262176 | tf_op jit(solution)/shard_map/ppermute | solution.py:358
  55.8 0.5 collective-permute-start.11
  56.3 1.2 %collective-permute-done.9.rest_2_.rest_7_ = bf16[8,128,128]{2,1,0:T(8,128)(2,1)S(1)} collective-permute-done((bf16[8,128,128]{2,1,0:T(8,128)(2,1)S(1)}, bf16[8,128,128]{2,1,0:T(8,128)(2,1)S(1)}, u32[]{:S(2)}, u32[]{:S(2)}) %collective-permute-start.9) | collective-permute-done | bytes 262176 | tf_op jit(solution)/shard_map/ppermute | solution.py:358
  57.4 0.4 collective-permute-start.10
  57.8 1.1 %collective-permute-start.21 = (bf16[8,128,128]{2,1,0:T(8,128)(2,1)S(1)}, bf16[8,128,128]{2,1,0:T(8,128)(2,1)S(1)}, u32[]{:S(2)}, u32[]{:S(2)}) collective-permute-start(bf16[8,128,128]{2,1,0:T(8,128)(2,1)S(1)} %collective-permute-done.19.rest_0_.rest_5_), channel_id=1, source_target_pairs={{0,16},{1,3},{2,18},{3,1},{16,0},{17,19},{18,2},{19,17},{4,20},{5,... | collective-permute-start | bytes 786440 | tf_op jit(solution)/shard_map/ppermute | solution.py:358
  59.0 1.3 %collective-permute-done.18.rest_3_.rest_0_ = bf16[8,128,128]{2,1,0:T(8,128)(2,1)S(1)} collective-permute-done((bf16[8,128,128]{2,1,0:T(8,128)(2,1)S(1)}, bf16[8,128,128]{2,1,0:T(8,128)(2,1)S(1)}, u32[]{:S(2)}, u32[]{:S(2)}) %collective-permute-start.18) | collective-permute-done | bytes 262176 | tf_op jit(solution)/shard_map/ppermute | solution.py:358
  60.4 0.4 collective-permute-start.23
  60.8 0.9 %near.2.rest_8_ = f32[280,128]{1,0:T(8,128)S(1)} custom-call(bf16[280,4096]{1,0:T(8,128)(2,1)S(1)} %bitcast.11, bf16[8,128,128]{2,1,0:T(8,128)(2,1)S(1)} %late.2.mine, bf16[8,128,128]{2,1,0:T(8,128)(2,1)S(1)} %collective-permute-done.12.other, bf16[8,128,128]{2,1,0:T(8,128)(2,1)S(1)} %collective-permute-done.7.rest_0_.rest_5_, ...), custom_call_target="tpu_custom_call" | custom-call | flops 600000000 | bytes 5242880 | tf_op jit(solution)/shard_map/near/pallas_call | solution.py:262
  61.7 1.1 %away.2 = (f32[144,128]{1,0:T(8,128)S(1)}, bf16[144,128]{1,0:T(8,128)(2,1)S(1)}, bf16[144,128]{1,0:T(8,128)(2,1)S(1)}, bf16[144,128]{1,0:T(8,128)(2,1)S(1)}) custom-call(bf16[280,4096]{1,0:T(8,128)(2,1)S(1)} %bitcast.12, bf16[8,128,128]{2,1,0:T(8,128)(2,1)S(1)} %collective-permute-done.6.rest_3_.rest_0_, ...), custom_call_target="tpu_custom_call" | custom-call | flops 600000000 | bytes 5242880 | tf_op jit(solution)/shard_map/away/pallas_call | solution.py:310
  62.8 0.2 collective-permute-start.20
  63.0 1.2 %collective-permute-done.21.rest_2_.rest_7_ = bf16[8,128,128]{2,1,0:T(8,128)(2,1)S(1)} collective-permute-done((bf16[8,128,128]{2,1,0:T(8,128)(2,1)S(1)}, bf16[8,128,128]{2,1,0:T(8,128)(2,1)S(1)}, u32[]{:S(2)}, u32[]{:S(2)}) %collective-permute-start.21) | collective-permute-done | bytes 262176 | tf_op jit(solution)/shard_map/ppermute | solution.py:358
  64.2 4.0 %collective-permute-start.13 = (bf16[144,128]{1,0:T(8,128)(2,1)S(1)}, bf16[144,128]{1,0:T(8,128)(2,1)S(1)}, u32[]{:S(2)}, u32[]{:S(2)}) collective-permute-start(bf16[144,128]{1,0:T(8,128)(2,1)S(1)} %get-tuple-element.22), channel_id=1, source_target_pairs={{0,4},{4,8},{8,12},{12,0},{1,5},{5,9},{9,13},{13,1},{2,6},{6,10},{... | collective-permute-start | bytes 110600 | tf_op jit(solution)/shard_map/ppermute | solution.py:471
  68.2 0.6 collective-permute-start.14
  68.8 1.8 %collective-permute-start.15 = (bf16[144,128]{1,0:T(8,128)(2,1)S(1)}, bf16[144,128]{1,0:T(8,128)(2,1)S(1)}, u32[]{:S(2)}, u32[]{:S(2)}) collective-permute-start(bf16[144,128]{1,0:T(8,128)(2,1)S(1)} %get-tuple-element.24), channel_id=1, source_target_pairs={{0,12},{4,0},{8,4},{12,8},{1,13},{5,1},{9,5},{13,9},{2,14},{6,2},{... | collective-permute-start | bytes 110600 | tf_op jit(solution)/shard_map/ppermute | solution.py:471
  70.6 0.9 %near.3.rest_8_ = f32[280,128]{1,0:T(8,128)S(1)} custom-call(bf16[280,4096]{1,0:T(8,128)(2,1)S(1)} %bitcast.13, bf16[8,128,128]{2,1,0:T(8,128)(2,1)S(1)} %late.3.mine, bf16[8,128,128]{2,1,0:T(8,128)(2,1)S(1)} %collective-permute-done.24.other, bf16[8,128,128]{2,1,0:T(8,128)(2,1)S(1)} %collective-permute-done.19.rest_0_.rest_5_, ...), custom_call_target="tpu_custom_call" | custom-call | flops 600000000 | bytes 5242880 | tf_op jit(solution)/shard_map/near/pallas_call | solution.py:262
  71.6 1.1 %away.3 = (f32[144,128]{1,0:T(8,128)S(1)}, bf16[144,128]{1,0:T(8,128)(2,1)S(1)}, bf16[144,128]{1,0:T(8,128)(2,1)S(1)}, bf16[144,128]{1,0:T(8,128)(2,1)S(1)}) custom-call(bf16[280,4096]{1,0:T(8,128)(2,1)S(1)} %bitcast.14, bf16[8,128,128]{2,1,0:T(8,128)(2,1)S(1)} %collective-permute-done.18.rest_3_.rest_0_, ...), custom_call_target="tpu_custom_call" | custom-call | flops 600000000 | bytes 5242880 | tf_op jit(solution)/shard_map/away/pallas_call | solution.py:310
  72.7 0.2 collective-permute-start.25
  72.9 2.3 %collective-permute-start.26 = (bf16[144,128]{1,0:T(8,128)(2,1)S(1)}, bf16[144,128]{1,0:T(8,128)(2,1)S(1)}, u32[]{:S(2)}, u32[]{:S(2)}) collective-permute-start(bf16[144,128]{1,0:T(8,128)(2,1)S(1)} %get-tuple-element.31), channel_id=1, source_target_pairs={{0,8},{4,12},{8,0},{12,4},{1,9},{5,13},{9,1},{13,5},{2,10},{6,14},... | collective-permute-start | bytes 110600 | tf_op jit(solution)/shard_map/ppermute | solution.py:471
  75.2 1.3 %collective-permute-start.27 = (bf16[144,128]{1,0:T(8,128)(2,1)S(1)}, bf16[144,128]{1,0:T(8,128)(2,1)S(1)}, u32[]{:S(2)}, u32[]{:S(2)}) collective-permute-start(bf16[144,128]{1,0:T(8,128)(2,1)S(1)} %get-tuple-element.32), channel_id=1, source_target_pairs={{0,12},{4,0},{8,4},{12,8},{1,13},{5,1},{9,5},{13,9},{2,14},{6,2},{... | collective-permute-start | bytes 110600 | tf_op jit(solution)/shard_map/ppermute | solution.py:471
  76.6 2.0 %collective-permute-done.25.refs_5_ = bf16[144,128]{1,0:T(8,128)(2,1)S(1)} collective-permute-done((bf16[144,128]{1,0:T(8,128)(2,1)S(1)}, bf16[144,128]{1,0:T(8,128)(2,1)S(1)}, u32[]{:S(2)}, u32[]{:S(2)}) %collective-permute-start.25) | collective-permute-done | bytes 36896 | tf_op jit(solution)/shard_map/ppermute | solution.py:471
  78.6 0.6 collective-permute-done.27.refs_7_
  79.2 0.8 final.1
  (41 shorter events, 0.2 us)
Async XLA Ops:
  2.6 11.7 %copy-start.7 = (s32[128,1]{0,1:T(1,128)S(1)}, s32[128,1]{0,1:T(1,128)}, u32[]{:S(2)}) copy-start(s32[128,1]{0,1:T(1,128)} %param.9) | copy-start | bytes 1540
  2.7 12.3 %copy-start.5 = (s32[128]{0:T(128)S(1)}, s32[128]{0:T(128)}, u32[]{:S(2)}) copy-start(s32[128]{0:T(128)} %param.8) | copy-start | bytes 1540
  2.7 12.3 %copy-start.6 = (s32[128]{0:T(128)S(1)}, s32[128]{0:T(128)}, u32[]{:S(2)}) copy-start(s32[128]{0:T(128)} %param.10) | copy-start | bytes 1540
  2.7 21.3 %copy-start.3 = (bf16[9,128,128]{2,1,0:T(8,128)(2,1)S(1)}, bf16[9,128,128]{2,1,0:T(8,128)(2,1)}, u32[]{:S(2)}) copy-start(bf16[9,128,128]{2,1,0:T(8,128)(2,1)} %pack.2.rest_0_) | copy-start | bytes 884740
  2.7 12.8 %collective-permute-start = (bf16[9,128,128]{2,1,0:T(8,128)(2,1)}, bf16[9,128,128]{2,1,0:T(8,128)(2,1)S(1)}, u32[]{:S(2)}, u32[]{:S(2)}) collective-permute-start(bf16[9,128,128]{2,1,0:T(8,128)(2,1)} %pack.2.rest_0_), channel_id=1, source_target_pairs={{0,12},{4,0},{8,4},{12,8},{1,13},{5,1},{9,5},{13,9},{2,14},{6,2},{... | collective-permute-start | bytes 884744 | tf_op jit(solution)/shard_map/ppermute | solution.py:432
  7.8 14.9 %collective-permute-start.1 = (bf16[9,128,128]{2,1,0:T(8,128)(2,1)}, bf16[9,128,128]{2,1,0:T(8,128)(2,1)S(1)}, u32[]{:S(2)}, u32[]{:S(2)}) collective-permute-start(bf16[9,128,128]{2,1,0:T(8,128)(2,1)} %pack.2.rest_0_), channel_id=1, source_target_pairs={{0,4},{4,8},{8,12},{12,0},{1,5},{5,9},{9,13},{13,1},{2,6},{6,10},{... | collective-permute-start | bytes 884744 | tf_op jit(solution)/shard_map/ppermute | solution.py:431
  10.4 18.9 %collective-permute-start.2 = (bf16[9,128,128]{2,1,0:T(8,128)(2,1)}, bf16[9,128,128]{2,1,0:T(8,128)(2,1)S(1)}, u32[]{:S(2)}, u32[]{:S(2)}) collective-permute-start(bf16[9,128,128]{2,1,0:T(8,128)(2,1)} %pack.3.rest_0_), channel_id=1, source_target_pairs={{0,12},{4,0},{8,4},{12,8},{1,13},{5,1},{9,5},{13,9},{2,14},{6,2},{... | collective-permute-start | bytes 884744 | tf_op jit(solution)/shard_map/ppermute | solution.py:432
  14.3 20.0 %collective-permute-start.3 = (bf16[9,128,128]{2,1,0:T(8,128)(2,1)}, bf16[9,128,128]{2,1,0:T(8,128)(2,1)S(1)}, u32[]{:S(2)}, u32[]{:S(2)}) collective-permute-start(bf16[9,128,128]{2,1,0:T(8,128)(2,1)} %pack.3.rest_0_), channel_id=1, source_target_pairs={{0,4},{4,8},{8,12},{12,0},{1,5},{5,9},{9,13},{13,1},{2,6},{6,10},{... | collective-permute-start | bytes 884744 | tf_op jit(solution)/shard_map/ppermute | solution.py:431
  15.5 23.9 %collective-permute-start.4 = (bf16[9,128,128]{2,1,0:T(8,128)(2,1)S(1)}, bf16[9,128,128]{2,1,0:T(8,128)(2,1)S(1)}, u32[]{:S(2)}, u32[]{:S(2)}) collective-permute-start(bf16[9,128,128]{2,1,0:T(8,128)(2,1)S(1)} %collective-permute-done.rest_1_), channel_id=1, source_target_pairs={{4,0},{8,4},{5,1},{9,5},{6,2},{10,6},{7,3},{11,7},{20,16},{24,20},... | collective-permute-start | bytes 884744 | tf_op jit(solution)/shard_map/ppermute | solution.py:438
  22.7 16.7 %collective-permute-start.5 = (bf16[9,128,128]{2,1,0:T(8,128)(2,1)S(1)}, bf16[9,128,128]{2,1,0:T(8,128)(2,1)S(1)}, u32[]{:S(2)}, u32[]{:S(2)}) collective-permute-start(bf16[9,128,128]{2,1,0:T(8,128)(2,1)S(1)} %collective-permute-done.1.rest_2_), channel_id=1, source_target_pairs={{4,8},{8,12},{5,9},{9,13},{6,10},{10,14},{7,11},{11,15},{20,24},{2... | collective-permute-start | bytes 884744 | tf_op jit(solution)/shard_map/ppermute | solution.py:439
  24.0 2.2 %copy-start = (bf16[128,128,128]{2,1,0:T(8,128)(2,1)S(1)}, bf16[128,128,128]{2,1,0:T(8,128)(2,1)}, u32[]{:S(2)}) copy-start(bf16[128,128,128]{2,1,0:T(8,128)(2,1)} %weights.7) | copy-start | bytes 12582916
  26.2 10.1 %copy-start.1 = (bf16[128,128,128]{2,1,0:T(8,128)(2,1)S(1)}, bf16[128,128,128]{2,1,0:T(8,128)(2,1)}, u32[]{:S(2)}) copy-start(bf16[128,128,128]{2,1,0:T(8,128)(2,1)} %weights.7) | copy-start | bytes 12582916
  26.2 10.1 %copy-start.4 = (bf16[9,128,128]{2,1,0:T(8,128)(2,1)S(1)}, bf16[9,128,128]{2,1,0:T(8,128)(2,1)}, u32[]{:S(2)}) copy-start(bf16[9,128,128]{2,1,0:T(8,128)(2,1)} %pack.3.rest_0_) | copy-start | bytes 884740
  34.3 10.3 %collective-permute-start.16 = (bf16[9,128,128]{2,1,0:T(8,128)(2,1)S(1)}, bf16[9,128,128]{2,1,0:T(8,128)(2,1)S(1)}, u32[]{:S(2)}, u32[]{:S(2)}) collective-permute-start(bf16[9,128,128]{2,1,0:T(8,128)(2,1)S(1)} %collective-permute-done.2.rest_1_), channel_id=1, source_target_pairs={{4,0},{8,4},{5,1},{9,5},{6,2},{10,6},{7,3},{11,7},{20,16},{24,20},... | collective-permute-start | bytes 884744 | tf_op jit(solution)/shard_map/ppermute | solution.py:438
  35.6 9.0 %collective-permute-start.17 = (bf16[9,128,128]{2,1,0:T(8,128)(2,1)S(1)}, bf16[9,128,128]{2,1,0:T(8,128)(2,1)S(1)}, u32[]{:S(2)}, u32[]{:S(2)}) collective-permute-start(bf16[9,128,128]{2,1,0:T(8,128)(2,1)S(1)} %collective-permute-done.3.rest_2_), channel_id=1, source_target_pairs={{4,8},{8,12},{5,9},{9,13},{6,10},{10,14},{7,11},{11,15},{20,24},{2... | collective-permute-start | bytes 884744 | tf_op jit(solution)/shard_map/ppermute | solution.py:439
  41.4 19.4 %copy-start.2 = (bf16[8,35,4096]{2,0,1:T(8,128)(2,1)S(1)}, bf16[8,35,4096]{2,0,1:T(8,128)(2,1)}, u32[]{:S(2)}) copy-start(bf16[8,35,4096]{2,0,1:T(8,128)(2,1)} %param.6) | copy-start | bytes 6881284
  41.4 8.4 %collective-permute-start.7 = (bf16[8,128,128]{2,1,0:T(8,128)(2,1)S(1)}, bf16[8,128,128]{2,1,0:T(8,128)(2,1)S(1)}, u32[]{:S(2)}, u32[]{:S(2)}) collective-permute-start(bf16[8,128,128]{2,1,0:T(8,128)(2,1)S(1)} %late.2.mine), channel_id=1, source_target_pairs={{0,2},{1,17},{2,0},{3,19},{16,18},{17,1},{18,16},{19,3},{4,6},{5,2... | collective-permute-start | bytes 786440 | tf_op jit(solution)/shard_map/ppermute | solution.py:358
  46.5 9.2 %collective-permute-start.19 = (bf16[8,128,128]{2,1,0:T(8,128)(2,1)S(1)}, bf16[8,128,128]{2,1,0:T(8,128)(2,1)S(1)}, u32[]{:S(2)}, u32[]{:S(2)}) collective-permute-start(bf16[8,128,128]{2,1,0:T(8,128)(2,1)S(1)} %late.3.mine), channel_id=1, source_target_pairs={{0,2},{1,17},{2,0},{3,19},{16,18},{17,1},{18,16},{19,3},{4,6},{5,2... | collective-permute-start | bytes 786440 | tf_op jit(solution)/shard_map/ppermute | solution.py:358
  48.3 7.5 %collective-permute-start.6 = (bf16[8,128,128]{2,1,0:T(8,128)(2,1)S(1)}, bf16[8,128,128]{2,1,0:T(8,128)(2,1)S(1)}, u32[]{:S(2)}, u32[]{:S(2)}) collective-permute-start(bf16[8,128,128]{2,1,0:T(8,128)(2,1)S(1)} %late.2.mine), channel_id=1, source_target_pairs={{0,16},{1,3},{2,18},{3,1},{16,0},{17,19},{18,2},{19,17},{4,20},{5,... | collective-permute-start | bytes 786440 | tf_op jit(solution)/shard_map/ppermute | solution.py:358
  49.8 7.7 %collective-permute-start.9 = (bf16[8,128,128]{2,1,0:T(8,128)(2,1)S(1)}, bf16[8,128,128]{2,1,0:T(8,128)(2,1)S(1)}, u32[]{:S(2)}, u32[]{:S(2)}) collective-permute-start(bf16[8,128,128]{2,1,0:T(8,128)(2,1)S(1)} %collective-permute-done.7.rest_0_.rest_5_), channel_id=1, source_target_pairs={{0,16},{1,3},{2,18},{3,1},{16,0},{17,19},{18,2},{19,17},{4,20},{5,... | collective-permute-start | bytes 786440 | tf_op jit(solution)/shard_map/ppermute | solution.py:358
  50.3 7.5 %collective-permute-start.12 = (bf16[8,128,128]{2,1,0:T(8,128)(2,1)S(1)}, bf16[8,128,128]{2,1,0:T(8,128)(2,1)S(1)}, u32[]{:S(2)}, u32[]{:S(2)}) collective-permute-start(bf16[8,128,128]{2,1,0:T(8,128)(2,1)S(1)} %late.2.mine), channel_id=1, source_target_pairs={{0,1},{1,0},{2,3},{3,2},{16,17},{17,16},{18,19},{19,18},{4,5},{5,4... | collective-permute-start | bytes 786440 | tf_op jit(solution)/shard_map/ppermute | solution.py:358
  50.3 10.0 %collective-permute-start.18 = (bf16[8,128,128]{2,1,0:T(8,128)(2,1)S(1)}, bf16[8,128,128]{2,1,0:T(8,128)(2,1)S(1)}, u32[]{:S(2)}, u32[]{:S(2)}) collective-permute-start(bf16[8,128,128]{2,1,0:T(8,128)(2,1)S(1)} %late.3.mine), channel_id=1, source_target_pairs={{0,16},{1,3},{2,18},{3,1},{16,0},{17,19},{18,2},{19,17},{4,20},{5,... | collective-permute-start | bytes 786440 | tf_op jit(solution)/shard_map/ppermute | solution.py:358
  55.8 4.6 %collective-permute-start.8 = (bf16[8,128,128]{2,1,0:T(8,128)(2,1)S(1)}, bf16[8,128,128]{2,1,0:T(8,128)(2,1)S(1)}, u32[]{:S(2)}, u32[]{:S(2)}) collective-permute-start(bf16[8,128,128]{2,1,0:T(8,128)(2,1)S(1)} %collective-permute-done.7.rest_0_.rest_5_), channel_id=1, source_target_pairs={{0,1},{1,0},{2,3},{3,2},{16,17},{17,16},{18,19},{19,18},{4,5},{5,4... | collective-permute-start | bytes 786440 | tf_op jit(solution)/shard_map/ppermute | solution.py:358
  55.8 5.0 %collective-permute-start.11 = (bf16[8,128,128]{2,1,0:T(8,128)(2,1)S(1)}, bf16[8,128,128]{2,1,0:T(8,128)(2,1)S(1)}, u32[]{:S(2)}, u32[]{:S(2)}) collective-permute-start(bf16[8,128,128]{2,1,0:T(8,128)(2,1)S(1)} %collective-permute-done.6.rest_3_.rest_0_), channel_id=1, source_target_pairs={{0,1},{1,0},{2,3},{3,2},{16,17},{17,16},{18,19},{19,18},{4,5},{5,4... | collective-permute-start | bytes 786440 | tf_op jit(solution)/shard_map/ppermute | solution.py:358
  57.4 4.3 %collective-permute-start.10 = (bf16[8,128,128]{2,1,0:T(8,128)(2,1)S(1)}, bf16[8,128,128]{2,1,0:T(8,128)(2,1)S(1)}, u32[]{:S(2)}, u32[]{:S(2)}) collective-permute-start(bf16[8,128,128]{2,1,0:T(8,128)(2,1)S(1)} %collective-permute-done.9.rest_2_.rest_7_), channel_id=1, source_target_pairs={{0,1},{1,0},{2,3},{3,2},{16,17},{17,16},{18,19},{19,18},{4,5},{5,4... | collective-permute-start | bytes 786440 | tf_op jit(solution)/shard_map/ppermute | solution.py:358
  57.8 6.4 %collective-permute-start.21 = (bf16[8,128,128]{2,1,0:T(8,128)(2,1)S(1)}, bf16[8,128,128]{2,1,0:T(8,128)(2,1)S(1)}, u32[]{:S(2)}, u32[]{:S(2)}) collective-permute-start(bf16[8,128,128]{2,1,0:T(8,128)(2,1)S(1)} %collective-permute-done.19.rest_0_.rest_5_), channel_id=1, source_target_pairs={{0,16},{1,3},{2,18},{3,1},{16,0},{17,19},{18,2},{19,17},{4,20},{5,... | collective-permute-start | bytes 786440 | tf_op jit(solution)/shard_map/ppermute | solution.py:358
  60.2 7.9 %collective-permute-start.24 = (bf16[8,128,128]{2,1,0:T(8,128)(2,1)S(1)}, bf16[8,128,128]{2,1,0:T(8,128)(2,1)S(1)}, u32[]{:S(2)}, u32[]{:S(2)}) collective-permute-start(bf16[8,128,128]{2,1,0:T(8,128)(2,1)S(1)} %late.3.mine), channel_id=1, source_target_pairs={{0,1},{1,0},{2,3},{3,2},{16,17},{17,16},{18,19},{19,18},{4,5},{5,4... | collective-permute-start | bytes 786440 | tf_op jit(solution)/shard_map/ppermute | solution.py:358
  60.4 8.4 %collective-permute-start.23 = (bf16[8,128,128]{2,1,0:T(8,128)(2,1)S(1)}, bf16[8,128,128]{2,1,0:T(8,128)(2,1)S(1)}, u32[]{:S(2)}, u32[]{:S(2)}) collective-permute-start(bf16[8,128,128]{2,1,0:T(8,128)(2,1)S(1)} %collective-permute-done.18.rest_3_.rest_0_), channel_id=1, source_target_pairs={{0,1},{1,0},{2,3},{3,2},{16,17},{17,16},{18,19},{19,18},{4,5},{5,4... | collective-permute-start | bytes 786440 | tf_op jit(solution)/shard_map/ppermute | solution.py:358
  62.8 7.8 %collective-permute-start.20 = (bf16[8,128,128]{2,1,0:T(8,128)(2,1)S(1)}, bf16[8,128,128]{2,1,0:T(8,128)(2,1)S(1)}, u32[]{:S(2)}, u32[]{:S(2)}) collective-permute-start(bf16[8,128,128]{2,1,0:T(8,128)(2,1)S(1)} %collective-permute-done.19.rest_0_.rest_5_), channel_id=1, source_target_pairs={{0,1},{1,0},{2,3},{3,2},{16,17},{17,16},{18,19},{19,18},{4,5},{5,4... | collective-permute-start | bytes 786440 | tf_op jit(solution)/shard_map/ppermute | solution.py:358
  64.2 7.4 %collective-permute-start.22 = (bf16[8,128,128]{2,1,0:T(8,128)(2,1)S(1)}, bf16[8,128,128]{2,1,0:T(8,128)(2,1)S(1)}, u32[]{:S(2)}, u32[]{:S(2)}) collective-permute-start(bf16[8,128,128]{2,1,0:T(8,128)(2,1)S(1)} %collective-permute-done.21.rest_2_.rest_7_), channel_id=1, source_target_pairs={{0,1},{1,0},{2,3},{3,2},{16,17},{17,16},{18,19},{19,18},{4,5},{5,4... | collective-permute-start | bytes 786440 | tf_op jit(solution)/shard_map/ppermute | solution.py:358
  64.2 11.0 %collective-permute-start.13 = (bf16[144,128]{1,0:T(8,128)(2,1)S(1)}, bf16[144,128]{1,0:T(8,128)(2,1)S(1)}, u32[]{:S(2)}, u32[]{:S(2)}) collective-permute-start(bf16[144,128]{1,0:T(8,128)(2,1)S(1)} %get-tuple-element.22), channel_id=1, source_target_pairs={{0,4},{4,8},{8,12},{12,0},{1,5},{5,9},{9,13},{13,1},{2,6},{6,10},{... | collective-permute-start | bytes 110600 | tf_op jit(solution)/shard_map/ppermute | solution.py:471
  68.2 8.4 %collective-permute-start.14 = (bf16[144,128]{1,0:T(8,128)(2,1)S(1)}, bf16[144,128]{1,0:T(8,128)(2,1)S(1)}, u32[]{:S(2)}, u32[]{:S(2)}) collective-permute-start(bf16[144,128]{1,0:T(8,128)(2,1)S(1)} %get-tuple-element.23), channel_id=1, source_target_pairs={{0,8},{4,12},{8,0},{12,4},{1,9},{5,13},{9,1},{13,5},{2,10},{6,14},... | collective-permute-start | bytes 110600 | tf_op jit(solution)/shard_map/ppermute | solution.py:471
  68.8 7.8 %collective-permute-start.15 = (bf16[144,128]{1,0:T(8,128)(2,1)S(1)}, bf16[144,128]{1,0:T(8,128)(2,1)S(1)}, u32[]{:S(2)}, u32[]{:S(2)}) collective-permute-start(bf16[144,128]{1,0:T(8,128)(2,1)S(1)} %get-tuple-element.24), channel_id=1, source_target_pairs={{0,12},{4,0},{8,4},{12,8},{1,13},{5,1},{9,5},{13,9},{2,14},{6,2},{... | collective-permute-start | bytes 110600 | tf_op jit(solution)/shard_map/ppermute | solution.py:471
  72.7 5.9 %collective-permute-start.25 = (bf16[144,128]{1,0:T(8,128)(2,1)S(1)}, bf16[144,128]{1,0:T(8,128)(2,1)S(1)}, u32[]{:S(2)}, u32[]{:S(2)}) collective-permute-start(bf16[144,128]{1,0:T(8,128)(2,1)S(1)} %get-tuple-element.30), channel_id=1, source_target_pairs={{0,4},{4,8},{8,12},{12,0},{1,5},{5,9},{9,13},{13,1},{2,6},{6,10},{... | collective-permute-start | bytes 110600 | tf_op jit(solution)/shard_map/ppermute | solution.py:471
  72.9 5.7 %collective-permute-start.26 = (bf16[144,128]{1,0:T(8,128)(2,1)S(1)}, bf16[144,128]{1,0:T(8,128)(2,1)S(1)}, u32[]{:S(2)}, u32[]{:S(2)}) collective-permute-start(bf16[144,128]{1,0:T(8,128)(2,1)S(1)} %get-tuple-element.31), channel_id=1, source_target_pairs={{0,8},{4,12},{8,0},{12,4},{1,9},{5,13},{9,1},{13,5},{2,10},{6,14},... | collective-permute-start | bytes 110600 | tf_op jit(solution)/shard_map/ppermute | solution.py:471
  75.2 4.0 %collective-permute-start.27 = (bf16[144,128]{1,0:T(8,128)(2,1)S(1)}, bf16[144,128]{1,0:T(8,128)(2,1)S(1)}, u32[]{:S(2)}, u32[]{:S(2)}) collective-permute-start(bf16[144,128]{1,0:T(8,128)(2,1)S(1)} %get-tuple-element.32), channel_id=1, source_target_pairs={{0,12},{4,0},{8,4},{12,8},{1,13},{5,1},{9,5},{13,9},{2,14},{6,2},{... | collective-permute-start | bytes 110600 | tf_op jit(solution)/shard_map/ppermute | solution.py:471

commit v4 on v3

--- a/solution.py
+++ b/solution.py
@@ -15,17 +15,14 @@
 UNROLL = 16
 COST_EARLY = (11, 0.4)
 COST_LATE = (8, 0.2)
-COST_NEAR = (5, 0.6)
-COST_AWAY = (5, 0.6)
+COST_NEAR = [(5, 0.6), (5, 0.6)]
+COST_AWAY = [(5, 0.6), (5, 0.6)]
 DIRECT = True
-TIE_EARLY = True
-TIE_LATE = 0
-TIE_HOP = True
-TIE_SWAP = ["s1"]
-TIE_RS = []
-TIE_B = False
+MERGED = True
+TIE_LATE = []
+TIE_SWAP = {'s1': ['near'], 's2': ['near']}
+TIE_NEAR = []
 PARTS = 3
-TIE_WHAT = 2
 MIB = 2**20
 
 VMEM = pl.BlockSpec(memory_space=pltpu.VMEM)
@@ -257,7 +254,7 @@
     by_core([mine, other, *x_even], [other, mine, *x_odd], body)
 
 
-def near_scores(fields, pieces):
+def near_scores(fields, pieces, chunk):
     rows = fields.shape[0]
     return pl.pallas_call(
         near_kernel,
@@ -265,7 +262,7 @@
         out_specs=VMEM,
         out_shape=jax.ShapeDtypeStruct((rows, LANES), jnp.float32),
         compiler_params=params(16),
-        cost_estimate=cost(*COST_NEAR),
+        cost_estimate=cost(*COST_NEAR[chunk]),
         name="near",
     )(fields, *pieces)
 
@@ -299,7 +296,7 @@
     by_core(even, odd, body)
 
 
-def away_scores(fields, pieces, near, split):
+def away_scores(fields, pieces, near, split, chunk):
     folded = fold_rows(fields.shape[0])
     if split:
         out_shape = [jax.ShapeDtypeStruct((folded, LANES), jnp.float32)] + [
@@ -313,9 +310,77 @@
         out_specs=[VMEM] * len(out_shape),
         out_shape=out_shape,
         compiler_params=params(18),
-        cost_estimate=cost(*COST_AWAY),
+        cost_estimate=cost(*COST_AWAY[chunk]),
         name="away",
     )(fields, *pieces, near)
+
+
+def raw_kernel(fields, *rest):
+    even, odd, out = rest[:4], rest[4:8], rest[8]
+
+    def body(pieces):
+        out[...] = products_of(fields, pieces)
+
+    by_core(even, odd, body)
+
+
+def raw_scores(fields, pieces, chunk):
+    rows = fields.shape[0]
+    return pl.pallas_call(
+        raw_kernel,
+        in_specs=[VMEM] * (1 + len(pieces)),
+        out_specs=VMEM,
+        out_shape=jax.ShapeDtypeStruct((rows, LANES), jnp.float32),
+        compiler_params=params(16),
+        cost_estimate=cost(*COST_AWAY[chunk]),
+        name="raw",
+    )(fields, *pieces)
+
+
+def last_kernel(split, fields, *rest):
+    even, odd, earlier, outs = rest[:4], rest[4:8], rest[8:11], rest[11:]
+    m = place() // 4
+    half = LANES // 2
+    low = lax.broadcasted_iota(jnp.int32, earlier[0].shape, 1) < half
+
+    def emit(to, value):
+        if not split:
+            outs[0][to] = value.astype(outs[0].dtype)
+            return
+        hop = lax.rem(to - lax.axis_index("tile") + 4, 4)
+        for k, out in enumerate(outs):
+
+            @pl.when(hop == k)
+            def _(out=out):
+                out[...] = value.astype(out.dtype)
+
+    def body(pieces):
+        second = products_of(fields, pieces)
+        pairs = [(earlier[0][...], earlier[2][...]), (earlier[1][...], second)]
+        for e, (a, b) in enumerate(pairs):
+            emit(2 * (m ^ e), jnp.where(low, a, pltpu.roll(b, half, 1)))
+            emit(2 * (m ^ e) + 1, jnp.where(low, pltpu.roll(a, half, 1), b))
+
+    by_core(even, odd, body)
+
+
+def last_scores(fields, pieces, earlier, split):
+    rows = fields.shape[0]
+    if split:
+        out_shape = [jax.ShapeDtypeStruct((rows, LANES), jnp.float32)] + [
+            jax.ShapeDtypeStruct((rows, LANES), jnp.bfloat16)
+        ] * 3
+    else:
+        out_shape = [jax.ShapeDtypeStruct((4, rows, LANES), jnp.float32)]
+    return pl.pallas_call(
+        functools.partial(last_kernel, split),
+        in_specs=[VMEM] * (1 + len(pieces) + len(earlier)),
+        out_specs=[VMEM] * len(out_shape),
+        out_shape=out_shape,
+        compiler_params=params(18),
+        cost_estimate=cost(*COST_AWAY[1]),
+        name="last",
+    )(fields, *pieces, *earlier)
 
 
 def fold_rows(rows):
@@ -377,9 +442,9 @@
     r1 = over_first(piece)
     other = over_core(tie(piece, "other") if DIRECT else piece)
     if DIRECT:
-        r2 = over_second(piece)
+        r2 = over_second(tie(piece, "r2"))
     else:
-        r2 = over_first(other)
+        r2 = over_first(tie(other, "r2"))
     d = over_second(tie(r1, "d"))
     s1, s2, s3 = over_core(tie(r1, "s1")), over_core(tie(r2, "s2")), over_core(tie(d, "s3"))
     if DIRECT:
@@ -422,16 +487,15 @@
     table = tile_table(
         tile_source, tile_band, tile_block, patterns.shape[0] // LANES, bands, z
     )
-    owns = []
+    owns, totals, rights, lefts = [], [], [], []
     for chunk in range(CHUNKS):
-        owns.append(pack(patterns, chunk, owns[-1:]))
-    totals, rights, lefts, nears = [], [], [], []
-    for own in owns:
+        own = pack(patterns, chunk, owns[-1:])
+        owns.append(own)
         if bands == 4:
             from_left = lax.ppermute(own, "tile", [(i, (i + 1) % 4) for i in range(4)])
             from_right = lax.ppermute(own, "tile", [(i, (i + 3) % 4) for i in range(4)])
             near = [own, from_right, from_left]
-            if totals and TIE_HOP:
+            if chunk:
                 totals[-1], from_right, from_left = lax.optimization_barrier(
                     (totals[-1], from_right, from_left)
                 )
@@ -442,36 +506,38 @@
             near = [gathered.reshape((-1,) + gathered.shape[2:])]
             rights.append(own)
             lefts.append(own)
-        nears.append(near)
-        if TIE_B and len(nears) == 2:
+        totals.append(early(table, remap_tiles, near, source_blocks))
+    totals = list(lax.optimization_barrier(totals))
+    sums, past, raw = [], {}, []
+    for chunk in range(CHUNKS):
+
+        def after(x, names):
+            held = [past[name] for name in names if name in past]
+            return lax.optimization_barrier((x, *held))[0] if held else x
+
+        total = after(totals[chunk], TIE_LATE)
+        piece = late(table, remap_tiles, total, rights[chunk], lefts[chunk])
+        near, away, r1, r2, d = gather_plane(piece, {k: [past[n] for n in v if n in past] for k, v in TIE_SWAP.items()})
+        part = near_scores(rows, [after(near[0], TIE_NEAR), *near[1:]], chunk)
+        raw.append(part)
+        if MERGED and chunk == 0:
+            far_part = raw_scores(rows, away, chunk)
+            raw.append(far_part)
+            past = dict(piece=piece, other=near[1], r1=r1, r2=r2, d=d, near=part, away=far_part)
             continue
-        totals.append(early(table, remap_tiles, near, source_blocks))
-    if TIE_EARLY and not TIE_B:
-        totals = list(lax.optimization_barrier(totals))
-    sums, done = [], {}
-    for chunk in range(CHUNKS):
-        piece = late(table, remap_tiles, totals[chunk], rights[chunk], lefts[chunk])
-        if TIE_B and chunk == 0:
-            own, *_ = lax.optimization_barrier((nears[1][0], piece))
-            totals.append(early(table, remap_tiles, [own, *nears[1][1:]], source_blocks))
-        near, away, r1, r2, d = gather_plane(piece, done)
-        if chunk == 0 and TIE_LATE:
-            tied = {1: near[1:2], 2: (r1,), 3: (r2,), 4: (d,), 5: (r1, near[1])}[TIE_LATE]
-            totals[1], *_ = lax.optimization_barrier((totals[1], *tied))
-        if done_near := done.get("near"):
-            near = lax.optimization_barrier((*near, *done_near))[: len(near)]
-        part = near_scores(rows, near)
-        parts = list(away_scores(rows, away, part, bands == 4))
-        done = {}
-        for name in TIE_SWAP:
-            done.setdefault(name, []).append(part if TIE_WHAT == 1 else parts[0])
+        if MERGED:
+            parts = list(last_scores(rows, away, raw, bands == 4))
+        else:
+            parts = list(away_scores(rows, away, part, bands == 4, chunk))
+        past = dict(piece=piece, other=near[1], r1=r1, r2=r2, d=d, near=part, away=parts[0])
         if bands == 4:
             for k in (1, 2, 3):
                 pairs = [(i, (i + k) % 4) for i in range(4)]
                 parts[k] = lax.ppermute(parts[k], "tile", pairs)
             sums += parts
-            for name in TIE_RS:
-                done.setdefault(name, []).extend(parts[1:4])
+            past["sum1"], past["sum2"], past["sum3"] = parts[1:]
+        elif MERGED:
+            sums.append(parts[0])
         else:
             folded = parts[0]
             half, skip = LANES // 2, 2 * folded.shape[1] - row_count
@@ -479,7 +545,12 @@
                 jnp.concatenate([folded[:, :, :half], folded[:, skip:, half:]], 1)
             )
     if bands == 4:
-        result = final(sums, row_count)
+        if MERGED:
+            result = sums[0]
+            for moved in sums[1:]:
+                result = result + moved.astype(jnp.float32)
+        else:
+            result = final(sums, row_count)
     else:
         partial = jnp.concatenate(sums, 2).transpose(1, 0, 2).reshape(row_count, pattern_count)
         result = lax.psum_scatter(partial, "tile", scatter_dimension=1, tiled=True)

time: 80.5 us -> 77.6 us (0.964)
  starting transfers between devices: 32.8 us -> 30.8 us
    ppermute x6 -> x3, starting transfers between devices: 10.3 us -> 7.77 us  [on_device(): parts[k] = lax.ppermute(parts[k], 'tile', pairs)]
    ppermute x2, waiting for transfers between devices: 1.63 us -> 0.11 us  [on_device(): rights.append(lax.ppermute(from_right, 'tile', [(1, 0), (2, 1)]))]
    ppermute x6 -> x3, waiting for transfers between devices: 2.65 us -> 3.88 us  [on_device(): parts[k] = lax.ppermute(parts[k], 'tile', pairs)]
    pallas_call x3 -> x2, Pallas kernels: 2.94 us -> 2.2 us  [the longest x1 1.28 us: last_scores(): pl.pallas_call(functools.partial(last_kernel, split), in_specs=[VMEM] * (...]
  transfers between devices with their start and end apart: 28 -> 25, of which waited for: 10 -> 10; matrix products, arithmetic and copies ran while one was open for 2% -> 2% of each run, Pallas kernels for 21% -> 20%
where the time goes in v4:
time: 77.6 us; the launch traced here: 77.4 us
  starting transfers between devices  30.8 us (40%)
  waiting for transfers between devices  22.3 us (29%)
  Pallas kernels  19.5 us (25%)
  other arithmetic  2.32 us (3%)
  local copies, waits for them, and re-layouts  2.22 us (3%)
    ppermute x2, waiting for transfers between devices, on_device(): from_left = lax.ppermute(own, 'tile', [(i, (i + 1) % 4) for i in range(4)])  10.5 us
    ppermute x14, starting transfers between devices, plane_permute(): return lax.ppermute(x, PLANE, pairs)  10.1 us
    ppermute x2, starting transfers between devices, on_device(): from_right = lax.ppermute(own, 'tile', [(i, (i + 3) % 4) for i in range(4)])  8.97 us
    ppermute x3, starting transfers between devices, on_device(): parts[k] = lax.ppermute(parts[k], 'tile', pairs)  7.77 us
    ppermute x14, waiting for transfers between devices, plane_permute(): return lax.ppermute(x, PLANE, pairs)  7.56 us
    pallas_call x2, Pallas kernels, early(): pl.pallas_call(early_kernel, in_specs=[SMEM, VMEM] + [ANY] * len(bands),...  6.81 us
    pallas_call x2, Pallas kernels, pack(): pl.pallas_call(functools.partial(pack_kernel, parts, chunk), in_specs=[AN...  5.3 us
    ppermute x3, waiting for transfers between devices, on_device(): parts[k] = lax.ppermute(parts[k], 'tile', pairs)  3.88 us
  transfers between devices with their start and end apart: 25, of which 10 were waited for; matrix products, arithmetic and copies ran while one was open for 2% of the time, Pallas kernels for 20%

profile of v4, /device:TPU:0, one launch (start us, length us, event | category | flops | bytes accessed | tf_op | source)
XLA Modules:
  0.0 77.4 jit_solution(26473215907632739)
XLA Ops:
  0.0 2.6 %pack.2.rest_0_ = bf16[9,128,128]{2,1,0:T(8,128)(2,1)} custom-call(bf16[4608,512]{1,0:T(8,128)(2,1)} %patterns.3), custom_call_target="tpu_custom_call" | custom-call | flops 150000000 | bytes 2411724 | tf_op jit(solution)/shard_map/pack/pallas_call | solution.py:98
  2.7 0.0 copy-start.7
  2.7 0.0 copy-start.5
  2.7 0.0 copy-start.6
  2.7 5.1 %collective-permute-start = (bf16[9,128,128]{2,1,0:T(8,128)(2,1)}, bf16[9,128,128]{2,1,0:T(8,128)(2,1)S(1)}, u32[]{:S(2)}, u32[]{:S(2)}) collective-permute-start(bf16[9,128,128]{2,1,0:T(8,128)(2,1)} %pack.2.rest_0_), channel_id=1, source_target_pairs={{0,12},{4,0},{8,4},{12,8},{1,13},{5,1},{9,5},{13,9},{2,14},{6,2},{... | collective-permute-start | bytes 884744 | tf_op jit(solution)/shard_map/ppermute | solution.py:496
  7.8 2.7 %pack.3.rest_0_ = bf16[9,128,128]{2,1,0:T(8,128)(2,1)} custom-call(bf16[4608,512]{1,0:T(8,128)(2,1)} %patterns.3, bf16[9,128,128]{2,1,0:T(8,128)(2,1)} %pack.2.rest_0_), custom_call_target="tpu_custom_call" | custom-call | flops 150000000 | bytes 2411724 | tf_op jit(solution)/shard_map/pack/pallas_call | solution.py:98
  10.5 3.9 %collective-permute-start.2 = (bf16[9,128,128]{2,1,0:T(8,128)(2,1)}, bf16[9,128,128]{2,1,0:T(8,128)(2,1)S(1)}, u32[]{:S(2)}, u32[]{:S(2)}) collective-permute-start(bf16[9,128,128]{2,1,0:T(8,128)(2,1)} %pack.3.rest_0_), channel_id=1, source_target_pairs={{0,12},{4,0},{8,4},{12,8},{1,13},{5,1},{9,5},{13,9},{2,14},{6,2},{... | collective-permute-start | bytes 884744 | tf_op jit(solution)/shard_map/ppermute | solution.py:496
  14.3 0.6 fusion
  15.0 0.2 convert_reduce_fusion
  15.2 0.1 select_reduce_fusion
  15.3 0.2 collective-permute-done.rest_1_
  15.5 1.3 %collective-permute-start.8 = (bf16[9,128,128]{2,1,0:T(8,128)(2,1)S(1)}, bf16[9,128,128]{2,1,0:T(8,128)(2,1)S(1)}, u32[]{:S(2)}, u32[]{:S(2)}) collective-permute-start(bf16[9,128,128]{2,1,0:T(8,128)(2,1)S(1)} %collective-permute-done.rest_1_), channel_id=1, source_target_pairs={{4,0},{8,4},{5,1},{9,5},{6,2},{10,6},{7,3},{11,7},{20,16},{24,20},... | collective-permute-start | bytes 884744 | tf_op jit(solution)/shard_map/ppermute | solution.py:502
  16.8 5.9 %collective-permute-done.1.rest_2_ = bf16[9,128,128]{2,1,0:T(8,128)(2,1)S(1)} collective-permute-done((bf16[9,128,128]{2,1,0:T(8,128)(2,1)}, bf16[9,128,128]{2,1,0:T(8,128)(2,1)S(1)}, u32[]{:S(2)}, u32[]{:S(2)}) %collective-permute-start.1) | collective-permute-done | bytes 294944 | tf_op jit(solution)/shard_map/ppermute | solution.py:495
  22.7 0.7 collective-permute-start.9
  23.4 0.7 compare_select_fusion.6.table
  24.0 0.0 copy-start
  24.1 2.2 %copy-done = bf16[128,128,128]{2,1,0:T(8,128)(2,1)S(1)} copy-done((bf16[128,128,128]{2,1,0:T(8,128)(2,1)S(1)}, bf16[128,128,128]{2,1,0:T(8,128)(2,1)}, u32[]{:S(2)}) %copy-start) | copy-done | bytes 4194328
  26.2 3.4 %early.2.given = f32[32,128,128]{2,1,0:T(8,128)S(1)} custom-call(s32[160]{0:T(256)S(1)} %compare_select_fusion.6.table, bf16[128,128,128]{2,1,0:T(8,128)(2,1)S(1)} %copy-done, bf16[9,128,128]{2,1,0:T(8,128)(2,1)S(1)} %copy-done.3, bf16[9,128,128]{2,1,0:T(8,128)(2,1)S(1)} %collective-permute-done.rest_1_, bf16[9,128,128]{2,1,0:T(8,128)(2,1)S(1)} %collective-permute-done.1.rest_2_), custom_call_target="tpu_custom_call" | custom-call | flops 400000000 | bytes 11534336 | tf_op jit(solution)/shard_map/early/pallas_call | solution.py:150
  29.6 0.0 copy-start.1
  29.7 4.7 %collective-permute-done.3.rest_2_ = bf16[9,128,128]{2,1,0:T(8,128)(2,1)S(1)} collective-permute-done((bf16[9,128,128]{2,1,0:T(8,128)(2,1)}, bf16[9,128,128]{2,1,0:T(8,128)(2,1)S(1)}, u32[]{:S(2)}, u32[]{:S(2)}) %collective-permute-start.3) | collective-permute-done | bytes 294944 | tf_op jit(solution)/shard_map/ppermute | solution.py:495
  34.3 1.3 %collective-permute-start.4 = (bf16[9,128,128]{2,1,0:T(8,128)(2,1)S(1)}, bf16[9,128,128]{2,1,0:T(8,128)(2,1)S(1)}, u32[]{:S(2)}, u32[]{:S(2)}) collective-permute-start(bf16[9,128,128]{2,1,0:T(8,128)(2,1)S(1)} %collective-permute-done.2.rest_1_), channel_id=1, source_target_pairs={{4,0},{8,4},{5,1},{9,5},{6,2},{10,6},{7,3},{11,7},{20,16},{24,20},... | collective-permute-start | bytes 884744 | tf_op jit(solution)/shard_map/ppermute | solution.py:502
  35.6 0.7 collective-permute-start.5
  36.3 3.4 %early.3.given = f32[32,128,128]{2,1,0:T(8,128)S(1)} custom-call(s32[160]{0:T(256)S(1)} %compare_select_fusion.6.table, bf16[128,128,128]{2,1,0:T(8,128)(2,1)S(1)} %copy-done, bf16[9,128,128]{2,1,0:T(8,128)(2,1)S(1)} %copy-done.4, bf16[9,128,128]{2,1,0:T(8,128)(2,1)S(1)} %collective-permute-done.2.rest_1_, ...), custom_call_target="tpu_custom_call" | custom-call | flops 400000000 | bytes 11534336 | tf_op jit(solution)/shard_map/early/pallas_call | solution.py:150
  39.8 1.6 %late.3.mine = bf16[8,128,128]{2,1,0:T(8,128)(2,1)S(1)} custom-call(s32[160]{0:T(256)S(1)} %compare_select_fusion.6.table, bf16[128,128,128]{2,1,0:T(8,128)(2,1)S(1)} %copy-done.1, f32[32,128,128]{2,1,0:T(8,128)S(1)} %early.2.given, bf16[9,128,128]{2,1,0:T(8,128)(2,1)S(1)} %collective-permute-done.8.right, bf16[9,128,128]{2,1,0:T(8,128)(2,1)S(1)} %collective-permute-done.9.left), custom_call_target="tpu_custom_call" | custom-call | flops 200000000 | bytes 8388608 | tf_op jit(solution)/shard_map/late/pallas_call | solution.py:199
  41.4 0.0 copy-start.2
  41.4 1.6 %collective-permute-start.11 = (bf16[8,128,128]{2,1,0:T(8,128)(2,1)S(1)}, bf16[8,128,128]{2,1,0:T(8,128)(2,1)S(1)}, u32[]{:S(2)}, u32[]{:S(2)}) collective-permute-start(bf16[8,128,128]{2,1,0:T(8,128)(2,1)S(1)} %late.3.mine), channel_id=1, source_target_pairs={{0,2},{1,17},{2,0},{3,19},{16,18},{17,1},{18,16},{19,3},{4,6},{5,2... | collective-permute-start | bytes 786440 | tf_op jit(solution)/shard_map/ppermute | solution.py:423
  43.0 1.5 %collective-permute-start.12 = (bf16[8,128,128]{2,1,0:T(8,128)(2,1)S(1)}, bf16[8,128,128]{2,1,0:T(8,128)(2,1)S(1)}, u32[]{:S(2)}, u32[]{:S(2)}) collective-permute-start(bf16[8,128,128]{2,1,0:T(8,128)(2,1)S(1)} %late.3.mine), channel_id=1, source_target_pairs={{0,16},{1,3},{2,18},{3,1},{16,0},{17,19},{18,2},{19,17},{4,20},{5,... | collective-permute-start | bytes 786440 | tf_op jit(solution)/shard_map/ppermute | solution.py:423
  44.5 0.1 collective-permute-done.4.right
  44.6 1.6 %late.2.mine = bf16[8,128,128]{2,1,0:T(8,128)(2,1)S(1)} custom-call(s32[160]{0:T(256)S(1)} %compare_select_fusion.6.table, bf16[128,128,128]{2,1,0:T(8,128)(2,1)S(1)} %copy-done.1, f32[32,128,128]{2,1,0:T(8,128)S(1)} %early.3.given, bf16[9,128,128]{2,1,0:T(8,128)(2,1)S(1)} %collective-permute-done.4.right, bf16[9,128,128]{2,1,0:T(8,128)(2,1)S(1)} %collective-permute-done.5.left), custom_call_target="tpu_custom_call" | custom-call | flops 200000000 | bytes 8388608 | tf_op jit(solution)/shard_map/late/pallas_call | solution.py:199
  46.2 1.7 %collective-permute-start.7 = (bf16[8,128,128]{2,1,0:T(8,128)(2,1)S(1)}, bf16[8,128,128]{2,1,0:T(8,128)(2,1)S(1)}, u32[]{:S(2)}, u32[]{:S(2)}) collective-permute-start(bf16[8,128,128]{2,1,0:T(8,128)(2,1)S(1)} %late.2.mine), channel_id=1, source_target_pairs={{0,2},{1,17},{2,0},{3,19},{16,18},{17,1},{18,16},{19,3},{4,6},{5,2... | collective-permute-start | bytes 786440 | tf_op jit(solution)/shard_map/ppermute | solution.py:423
  47.9 1.8 %collective-permute-done.11.rest_0_.rest_5_ = bf16[8,128,128]{2,1,0:T(8,128)(2,1)S(1)} collective-permute-done((bf16[8,128,128]{2,1,0:T(8,128)(2,1)S(1)}, bf16[8,128,128]{2,1,0:T(8,128)(2,1)S(1)}, u32[]{:S(2)}, u32[]{:S(2)}) %collective-permute-start.11) | collective-permute-done | bytes 262176 | tf_op jit(solution)/shard_map/ppermute | solution.py:423
  49.8 0.5 collective-permute-start.19
  50.3 1.2 %collective-permute-start.13 = (bf16[8,128,128]{2,1,0:T(8,128)(2,1)S(1)}, bf16[8,128,128]{2,1,0:T(8,128)(2,1)S(1)}, u32[]{:S(2)}, u32[]{:S(2)}) collective-permute-start(bf16[8,128,128]{2,1,0:T(8,128)(2,1)S(1)} %collective-permute-done.12.rest_3_.rest_0_), channel_id=1, source_target_pairs={{0,1},{1,0},{2,3},{3,2},{16,17},{17,16},{18,19},{19,18},{4,5},{5,4... | collective-permute-start | bytes 786440 | tf_op jit(solution)/shard_map/ppermute | solution.py:423
  51.5 0.5 collective-permute-start.6
  52.0 0.7 collective-permute-done.7.rest_0_.rest_5_
  52.7 2.6 %collective-permute-start.16 = (bf16[8,128,128]{2,1,0:T(8,128)(2,1)S(1)}, bf16[8,128,128]{2,1,0:T(8,128)(2,1)S(1)}, u32[]{:S(2)}, u32[]{:S(2)}) collective-permute-start(bf16[8,128,128]{2,1,0:T(8,128)(2,1)S(1)} %collective-permute-done.7.rest_0_.rest_5_), channel_id=1, source_target_pairs={{0,16},{1,3},{2,18},{3,1},{16,0},{17,19},{18,2},{19,17},{4,20},{5,... | collective-permute-start | bytes 786440 | tf_op jit(solution)/shard_map/ppermute | solution.py:423
  55.2 0.9 %collective-permute-done.19.rest_2_.rest_7_ = bf16[8,128,128]{2,1,0:T(8,128)(2,1)S(1)} collective-permute-done((bf16[8,128,128]{2,1,0:T(8,128)(2,1)S(1)}, bf16[8,128,128]{2,1,0:T(8,128)(2,1)S(1)}, u32[]{:S(2)}, u32[]{:S(2)}) %collective-permute-start.19) | collective-permute-done | bytes 262176 | tf_op jit(solution)/shard_map/ppermute | solution.py:423
  56.2 1.0 %near.2.rest_8_ = f32[280,128]{1,0:T(8,128)S(1)} custom-call(bf16[280,4096]{1,0:T(8,128)(2,1)S(1)} %bitcast.12, bf16[8,128,128]{2,1,0:T(8,128)(2,1)S(1)} %late.3.mine, bf16[8,128,128]{2,1,0:T(8,128)(2,1)S(1)} %collective-permute-done.10.other, bf16[8,128,128]{2,1,0:T(8,128)(2,1)S(1)} %collective-permute-done.11.rest_0_.rest_5_, ...), custom_call_target="tpu_custom_call" | custom-call | flops 600000000 | bytes 5242880 | tf_op jit(solution)/shard_map/near/pallas_call | solution.py:259
  57.1 1.8 %collective-permute-done.6.rest_3_.rest_0_ = bf16[8,128,128]{2,1,0:T(8,128)(2,1)S(1)} collective-permute-done((bf16[8,128,128]{2,1,0:T(8,128)(2,1)S(1)}, bf16[8,128,128]{2,1,0:T(8,128)(2,1)S(1)}, u32[]{:S(2)}, u32[]{:S(2)}) %collective-permute-start.6) | collective-permute-done | bytes 262176 | tf_op jit(solution)/shard_map/ppermute | solution.py:423
  59.0 0.5 collective-permute-start.15
  59.5 2.3 %collective-permute-done.16.rest_2_.rest_7_ = bf16[8,128,128]{2,1,0:T(8,128)(2,1)S(1)} collective-permute-done((bf16[8,128,128]{2,1,0:T(8,128)(2,1)S(1)}, bf16[8,128,128]{2,1,0:T(8,128)(2,1)S(1)}, u32[]{:S(2)}, u32[]{:S(2)}) %collective-permute-start.16) | collective-permute-done | bytes 262176 | tf_op jit(solution)/shard_map/ppermute | solution.py:423
  61.8 0.9 %raw.1.rest_9_ = f32[280,128]{1,0:T(8,128)S(1)} custom-call(bf16[280,4096]{1,0:T(8,128)(2,1)S(1)} %bitcast.13, bf16[8,128,128]{2,1,0:T(8,128)(2,1)S(1)} %collective-permute-done.12.rest_3_.rest_0_, bf16[8,128,128]{2,1,0:T(8,128)(2,1)S(1)} %collective-permute-done.14.rest_2_.rest_1_, bf16[8,128,128]{2,1,0:T(8,128)(2,1)S(1)} %collective-permute-done.19.rest_2_.rest_7_, ...), custom_call_target="tpu_custom_call" | custom-call | flops 600000000 | bytes 5242880 | tf_op jit(solution)/shard_map/raw/pallas_call | solution.py:329
  62.7 0.9 %near.3.rest_10_ = f32[280,128]{1,0:T(8,128)S(1)} custom-call(bf16[280,4096]{1,0:T(8,128)(2,1)S(1)} %bitcast.14, bf16[8,128,128]{2,1,0:T(8,128)(2,1)S(1)} %late.2.mine, bf16[8,128,128]{2,1,0:T(8,128)(2,1)S(1)} %collective-permute-done.21.other, bf16[8,128,128]{2,1,0:T(8,128)(2,1)S(1)} %collective-permute-done.7.rest_0_.rest_5_, ...), custom_call_target="tpu_custom_call" | custom-call | flops 600000000 | bytes 5242880 | tf_op jit(solution)/shard_map/near/pallas_call | solution.py:259
  63.7 1.3 %last.1 = (f32[280,128]{1,0:T(8,128)S(1)}, bf16[280,128]{1,0:T(8,128)(2,1)S(1)}, bf16[280,128]{1,0:T(8,128)(2,1)S(1)}, bf16[280,128]{1,0:T(8,128)(2,1)S(1)}) custom-call(bf16[280,4096]{1,0:T(8,128)(2,1)S(1)} %bitcast.15, bf16[8,128,128]{2,1,0:T(8,128)(2,1)S(1)} %collective-permute-done.6.rest_3_.rest_0_, ...), custom_call_target="tpu_custom_call" | custom-call | flops 600000000 | bytes 5242880 | tf_op jit(solution)/shard_map/last/pallas_call | solution.py:375
  65.0 5.0 %collective-permute-start.22 = (bf16[280,128]{1,0:T(8,128)(2,1)S(1)}, bf16[280,128]{1,0:T(8,128)(2,1)S(1)}, u32[]{:S(2)}, u32[]{:S(2)}) collective-permute-start(bf16[280,128]{1,0:T(8,128)(2,1)S(1)} %get-tuple-element.24), channel_id=1, source_target_pairs={{0,4},{4,8},{8,12},{12,0},{1,5},{5,9},{9,13},{13,1},{2,6},{6,10},{... | collective-permute-start | bytes 215048 | tf_op jit(solution)/shard_map/ppermute | solution.py:536
  70.0 2.8 %collective-permute-start.24 = (bf16[280,128]{1,0:T(8,128)(2,1)S(1)}, bf16[280,128]{1,0:T(8,128)(2,1)S(1)}, u32[]{:S(2)}, u32[]{:S(2)}) collective-permute-start(bf16[280,128]{1,0:T(8,128)(2,1)S(1)} %get-tuple-element.26), channel_id=1, source_target_pairs={{0,12},{4,0},{8,4},{12,8},{1,13},{5,1},{9,5},{13,9},{2,14},{6,2},{... | collective-permute-start | bytes 215048 | tf_op jit(solution)/shard_map/ppermute | solution.py:536
  72.8 3.9 %collective-permute-done.23 = bf16[280,128]{1,0:T(8,128)(2,1)S(1)} collective-permute-done((bf16[280,128]{1,0:T(8,128)(2,1)S(1)}, bf16[280,128]{1,0:T(8,128)(2,1)S(1)}, u32[]{:S(2)}, u32[]{:S(2)}) %collective-permute-start.23) | collective-permute-done | bytes 71712 | tf_op jit(solution)/shard_map/ppermute | solution.py:536
  76.7 0.7 add_bitcast_fusion
  (35 shorter events, 0.1 us)
Async XLA Ops:
  2.7 11.7 %copy-start.7 = (s32[128,1]{0,1:T(1,128)S(1)}, s32[128,1]{0,1:T(1,128)}, u32[]{:S(2)}) copy-start(s32[128,1]{0,1:T(1,128)} %param.9) | copy-start | bytes 1540
  2.7 12.3 %copy-start.5 = (s32[128]{0:T(128)S(1)}, s32[128]{0:T(128)}, u32[]{:S(2)}) copy-start(s32[128]{0:T(128)} %param.8) | copy-start | bytes 1540
  2.7 12.3 %copy-start.6 = (s32[128]{0:T(128)S(1)}, s32[128]{0:T(128)}, u32[]{:S(2)}) copy-start(s32[128]{0:T(128)} %param.10) | copy-start | bytes 1540
  2.7 21.3 %copy-start.3 = (bf16[9,128,128]{2,1,0:T(8,128)(2,1)S(1)}, bf16[9,128,128]{2,1,0:T(8,128)(2,1)}, u32[]{:S(2)}) copy-start(bf16[9,128,128]{2,1,0:T(8,128)(2,1)} %pack.2.rest_0_) | copy-start | bytes 884740
  2.7 12.8 %collective-permute-start = (bf16[9,128,128]{2,1,0:T(8,128)(2,1)}, bf16[9,128,128]{2,1,0:T(8,128)(2,1)S(1)}, u32[]{:S(2)}, u32[]{:S(2)}) collective-permute-start(bf16[9,128,128]{2,1,0:T(8,128)(2,1)} %pack.2.rest_0_), channel_id=1, source_target_pairs={{0,12},{4,0},{8,4},{12,8},{1,13},{5,1},{9,5},{13,9},{2,14},{6,2},{... | collective-permute-start | bytes 884744 | tf_op jit(solution)/shard_map/ppermute | solution.py:496
  7.8 14.9 %collective-permute-start.1 = (bf16[9,128,128]{2,1,0:T(8,128)(2,1)}, bf16[9,128,128]{2,1,0:T(8,128)(2,1)S(1)}, u32[]{:S(2)}, u32[]{:S(2)}) collective-permute-start(bf16[9,128,128]{2,1,0:T(8,128)(2,1)} %pack.2.rest_0_), channel_id=1, source_target_pairs={{0,4},{4,8},{8,12},{12,0},{1,5},{5,9},{9,13},{13,1},{2,6},{6,10},{... | collective-permute-start | bytes 884744 | tf_op jit(solution)/shard_map/ppermute | solution.py:495
  10.5 19.2 %collective-permute-start.2 = (bf16[9,128,128]{2,1,0:T(8,128)(2,1)}, bf16[9,128,128]{2,1,0:T(8,128)(2,1)S(1)}, u32[]{:S(2)}, u32[]{:S(2)}) collective-permute-start(bf16[9,128,128]{2,1,0:T(8,128)(2,1)} %pack.3.rest_0_), channel_id=1, source_target_pairs={{0,12},{4,0},{8,4},{12,8},{1,13},{5,1},{9,5},{13,9},{2,14},{6,2},{... | collective-permute-start | bytes 884744 | tf_op jit(solution)/shard_map/ppermute | solution.py:496
  14.3 20.0 %collective-permute-start.3 = (bf16[9,128,128]{2,1,0:T(8,128)(2,1)}, bf16[9,128,128]{2,1,0:T(8,128)(2,1)S(1)}, u32[]{:S(2)}, u32[]{:S(2)}) collective-permute-start(bf16[9,128,128]{2,1,0:T(8,128)(2,1)} %pack.3.rest_0_), channel_id=1, source_target_pairs={{0,4},{4,8},{8,12},{12,0},{1,5},{5,9},{9,13},{13,1},{2,6},{6,10},{... | collective-permute-start | bytes 884744 | tf_op jit(solution)/shard_map/ppermute | solution.py:495
  15.5 24.2 %collective-permute-start.8 = (bf16[9,128,128]{2,1,0:T(8,128)(2,1)S(1)}, bf16[9,128,128]{2,1,0:T(8,128)(2,1)S(1)}, u32[]{:S(2)}, u32[]{:S(2)}) collective-permute-start(bf16[9,128,128]{2,1,0:T(8,128)(2,1)S(1)} %collective-permute-done.rest_1_), channel_id=1, source_target_pairs={{4,0},{8,4},{5,1},{9,5},{6,2},{10,6},{7,3},{11,7},{20,16},{24,20},... | collective-permute-start | bytes 884744 | tf_op jit(solution)/shard_map/ppermute | solution.py:502
  22.7 17.1 %collective-permute-start.9 = (bf16[9,128,128]{2,1,0:T(8,128)(2,1)S(1)}, bf16[9,128,128]{2,1,0:T(8,128)(2,1)S(1)}, u32[]{:S(2)}, u32[]{:S(2)}) collective-permute-start(bf16[9,128,128]{2,1,0:T(8,128)(2,1)S(1)} %collective-permute-done.1.rest_2_), channel_id=1, source_target_pairs={{4,8},{8,12},{5,9},{9,13},{6,10},{10,14},{7,11},{11,15},{20,24},{2... | collective-permute-start | bytes 884744 | tf_op jit(solution)/shard_map/ppermute | solution.py:503
  24.0 2.2 %copy-start = (bf16[128,128,128]{2,1,0:T(8,128)(2,1)S(1)}, bf16[128,128,128]{2,1,0:T(8,128)(2,1)}, u32[]{:S(2)}) copy-start(bf16[128,128,128]{2,1,0:T(8,128)(2,1)} %weights.7) | copy-start | bytes 12582916
  26.2 10.1 %copy-start.4 = (bf16[9,128,128]{2,1,0:T(8,128)(2,1)S(1)}, bf16[9,128,128]{2,1,0:T(8,128)(2,1)}, u32[]{:S(2)}) copy-start(bf16[9,128,128]{2,1,0:T(8,128)(2,1)} %pack.3.rest_0_) | copy-start | bytes 884740
  29.6 10.1 %copy-start.1 = (bf16[128,128,128]{2,1,0:T(8,128)(2,1)S(1)}, bf16[128,128,128]{2,1,0:T(8,128)(2,1)}, u32[]{:S(2)}) copy-start(bf16[128,128,128]{2,1,0:T(8,128)(2,1)} %weights.7) | copy-start | bytes 12582916
  34.3 10.3 %collective-permute-start.4 = (bf16[9,128,128]{2,1,0:T(8,128)(2,1)S(1)}, bf16[9,128,128]{2,1,0:T(8,128)(2,1)S(1)}, u32[]{:S(2)}, u32[]{:S(2)}) collective-permute-start(bf16[9,128,128]{2,1,0:T(8,128)(2,1)S(1)} %collective-permute-done.2.rest_1_), channel_id=1, source_target_pairs={{4,0},{8,4},{5,1},{9,5},{6,2},{10,6},{7,3},{11,7},{20,16},{24,20},... | collective-permute-start | bytes 884744 | tf_op jit(solution)/shard_map/ppermute | solution.py:502
  35.6 9.0 %collective-permute-start.5 = (bf16[9,128,128]{2,1,0:T(8,128)(2,1)S(1)}, bf16[9,128,128]{2,1,0:T(8,128)(2,1)S(1)}, u32[]{:S(2)}, u32[]{:S(2)}) collective-permute-start(bf16[9,128,128]{2,1,0:T(8,128)(2,1)S(1)} %collective-permute-done.3.rest_2_), channel_id=1, source_target_pairs={{4,8},{8,12},{5,9},{9,13},{6,10},{10,14},{7,11},{11,15},{20,24},{2... | collective-permute-start | bytes 884744 | tf_op jit(solution)/shard_map/ppermute | solution.py:503
  41.4 14.8 %copy-start.2 = (bf16[8,35,4096]{2,0,1:T(8,128)(2,1)S(1)}, bf16[8,35,4096]{2,0,1:T(8,128)(2,1)}, u32[]{:S(2)}) copy-start(bf16[8,35,4096]{2,0,1:T(8,128)(2,1)} %param.6) | copy-start | bytes 6881284
  41.4 8.4 %collective-permute-start.11 = (bf16[8,128,128]{2,1,0:T(8,128)(2,1)S(1)}, bf16[8,128,128]{2,1,0:T(8,128)(2,1)S(1)}, u32[]{:S(2)}, u32[]{:S(2)}) collective-permute-start(bf16[8,128,128]{2,1,0:T(8,128)(2,1)S(1)} %late.3.mine), channel_id=1, source_target_pairs={{0,2},{1,17},{2,0},{3,19},{16,18},{17,1},{18,16},{19,3},{4,6},{5,2... | collective-permute-start | bytes 786440 | tf_op jit(solution)/shard_map/ppermute | solution.py:423
  43.0 7.3 %collective-permute-start.12 = (bf16[8,128,128]{2,1,0:T(8,128)(2,1)S(1)}, bf16[8,128,128]{2,1,0:T(8,128)(2,1)S(1)}, u32[]{:S(2)}, u32[]{:S(2)}) collective-permute-start(bf16[8,128,128]{2,1,0:T(8,128)(2,1)S(1)} %late.3.mine), channel_id=1, source_target_pairs={{0,16},{1,3},{2,18},{3,1},{16,0},{17,19},{18,2},{19,17},{4,20},{5,... | collective-permute-start | bytes 786440 | tf_op jit(solution)/shard_map/ppermute | solution.py:423
  44.5 7.0 %collective-permute-start.10 = (bf16[8,128,128]{2,1,0:T(8,128)(2,1)S(1)}, bf16[8,128,128]{2,1,0:T(8,128)(2,1)S(1)}, u32[]{:S(2)}, u32[]{:S(2)}) collective-permute-start(bf16[8,128,128]{2,1,0:T(8,128)(2,1)S(1)} %late.3.mine), channel_id=1, source_target_pairs={{0,1},{1,0},{2,3},{3,2},{16,17},{17,16},{18,19},{19,18},{4,5},{5,4... | collective-permute-start | bytes 786440 | tf_op jit(solution)/shard_map/ppermute | solution.py:423
  46.2 6.4 %collective-permute-start.7 = (bf16[8,128,128]{2,1,0:T(8,128)(2,1)S(1)}, bf16[8,128,128]{2,1,0:T(8,128)(2,1)S(1)}, u32[]{:S(2)}, u32[]{:S(2)}) collective-permute-start(bf16[8,128,128]{2,1,0:T(8,128)(2,1)S(1)} %late.2.mine), channel_id=1, source_target_pairs={{0,2},{1,17},{2,0},{3,19},{16,18},{17,1},{18,16},{19,3},{4,6},{5,2... | collective-permute-start | bytes 786440 | tf_op jit(solution)/shard_map/ppermute | solution.py:423
  49.8 5.5 %collective-permute-start.14 = (bf16[8,128,128]{2,1,0:T(8,128)(2,1)S(1)}, bf16[8,128,128]{2,1,0:T(8,128)(2,1)S(1)}, u32[]{:S(2)}, u32[]{:S(2)}) collective-permute-start(bf16[8,128,128]{2,1,0:T(8,128)(2,1)S(1)} %collective-permute-done.11.rest_0_.rest_5_), channel_id=1, source_target_pairs={{0,1},{1,0},{2,3},{3,2},{16,17},{17,16},{18,19},{19,18},{4,5},{5,4... | collective-permute-start | bytes 786440 | tf_op jit(solution)/shard_map/ppermute | solution.py:423
  49.8 6.4 %collective-permute-start.19 = (bf16[8,128,128]{2,1,0:T(8,128)(2,1)S(1)}, bf16[8,128,128]{2,1,0:T(8,128)(2,1)S(1)}, u32[]{:S(2)}, u32[]{:S(2)}) collective-permute-start(bf16[8,128,128]{2,1,0:T(8,128)(2,1)S(1)} %collective-permute-done.11.rest_0_.rest_5_), channel_id=1, source_target_pairs={{0,16},{1,3},{2,18},{3,1},{16,0},{17,19},{18,2},{19,17},{4,20},{5,... | collective-permute-start | bytes 786440 | tf_op jit(solution)/shard_map/ppermute | solution.py:423
  50.3 5.9 %collective-permute-start.13 = (bf16[8,128,128]{2,1,0:T(8,128)(2,1)S(1)}, bf16[8,128,128]{2,1,0:T(8,128)(2,1)S(1)}, u32[]{:S(2)}, u32[]{:S(2)}) collective-permute-start(bf16[8,128,128]{2,1,0:T(8,128)(2,1)S(1)} %collective-permute-done.12.rest_3_.rest_0_), channel_id=1, source_target_pairs={{0,1},{1,0},{2,3},{3,2},{16,17},{17,16},{18,19},{19,18},{4,5},{5,4... | collective-permute-start | bytes 786440 | tf_op jit(solution)/shard_map/ppermute | solution.py:423
  51.5 7.5 %collective-permute-start.6 = (bf16[8,128,128]{2,1,0:T(8,128)(2,1)S(1)}, bf16[8,128,128]{2,1,0:T(8,128)(2,1)S(1)}, u32[]{:S(2)}, u32[]{:S(2)}) collective-permute-start(bf16[8,128,128]{2,1,0:T(8,128)(2,1)S(1)} %late.2.mine), channel_id=1, source_target_pairs={{0,16},{1,3},{2,18},{3,1},{16,0},{17,19},{18,2},{19,17},{4,20},{5,... | collective-permute-start | bytes 786440 | tf_op jit(solution)/shard_map/ppermute | solution.py:423
  52.7 9.1 %collective-permute-start.16 = (bf16[8,128,128]{2,1,0:T(8,128)(2,1)S(1)}, bf16[8,128,128]{2,1,0:T(8,128)(2,1)S(1)}, u32[]{:S(2)}, u32[]{:S(2)}) collective-permute-start(bf16[8,128,128]{2,1,0:T(8,128)(2,1)S(1)} %collective-permute-done.7.rest_0_.rest_5_), channel_id=1, source_target_pairs={{0,16},{1,3},{2,18},{3,1},{16,0},{17,19},{18,2},{19,17},{4,20},{5,... | collective-permute-start | bytes 786440 | tf_op jit(solution)/shard_map/ppermute | solution.py:423
  55.2 7.5 %collective-permute-start.21 = (bf16[8,128,128]{2,1,0:T(8,128)(2,1)S(1)}, bf16[8,128,128]{2,1,0:T(8,128)(2,1)S(1)}, u32[]{:S(2)}, u32[]{:S(2)}) collective-permute-start(bf16[8,128,128]{2,1,0:T(8,128)(2,1)S(1)} %late.2.mine), channel_id=1, source_target_pairs={{0,1},{1,0},{2,3},{3,2},{16,17},{17,16},{18,19},{19,18},{4,5},{5,4... | collective-permute-start | bytes 786440 | tf_op jit(solution)/shard_map/ppermute | solution.py:423
  56.2 5.6 %collective-permute-start.20 = (bf16[8,128,128]{2,1,0:T(8,128)(2,1)S(1)}, bf16[8,128,128]{2,1,0:T(8,128)(2,1)S(1)}, u32[]{:S(2)}, u32[]{:S(2)}) collective-permute-start(bf16[8,128,128]{2,1,0:T(8,128)(2,1)S(1)} %collective-permute-done.19.rest_2_.rest_7_), channel_id=1, source_target_pairs={{0,1},{1,0},{2,3},{3,2},{16,17},{17,16},{18,19},{19,18},{4,5},{5,4... | collective-permute-start | bytes 786440 | tf_op jit(solution)/shard_map/ppermute | solution.py:423
  59.0 3.8 %collective-permute-start.18 = (bf16[8,128,128]{2,1,0:T(8,128)(2,1)S(1)}, bf16[8,128,128]{2,1,0:T(8,128)(2,1)S(1)}, u32[]{:S(2)}, u32[]{:S(2)}) collective-permute-start(bf16[8,128,128]{2,1,0:T(8,128)(2,1)S(1)} %collective-permute-done.6.rest_3_.rest_0_), channel_id=1, source_target_pairs={{0,1},{1,0},{2,3},{3,2},{16,17},{17,16},{18,19},{19,18},{4,5},{5,4... | collective-permute-start | bytes 786440 | tf_op jit(solution)/shard_map/ppermute | solution.py:423
  59.0 3.8 %collective-permute-start.15 = (bf16[8,128,128]{2,1,0:T(8,128)(2,1)S(1)}, bf16[8,128,128]{2,1,0:T(8,128)(2,1)S(1)}, u32[]{:S(2)}, u32[]{:S(2)}) collective-permute-start(bf16[8,128,128]{2,1,0:T(8,128)(2,1)S(1)} %collective-permute-done.7.rest_0_.rest_5_), channel_id=1, source_target_pairs={{0,1},{1,0},{2,3},{3,2},{16,17},{17,16},{18,19},{19,18},{4,5},{5,4... | collective-permute-start | bytes 786440 | tf_op jit(solution)/shard_map/ppermute | solution.py:423
  61.8 1.9 %collective-permute-start.17 = (bf16[8,128,128]{2,1,0:T(8,128)(2,1)S(1)}, bf16[8,128,128]{2,1,0:T(8,128)(2,1)S(1)}, u32[]{:S(2)}, u32[]{:S(2)}) collective-permute-start(bf16[8,128,128]{2,1,0:T(8,128)(2,1)S(1)} %collective-permute-done.16.rest_2_.rest_7_), channel_id=1, source_target_pairs={{0,1},{1,0},{2,3},{3,2},{16,17},{17,16},{18,19},{19,18},{4,5},{5,4... | collective-permute-start | bytes 786440 | tf_op jit(solution)/shard_map/ppermute | solution.py:423
  65.0 7.8 %collective-permute-start.22 = (bf16[280,128]{1,0:T(8,128)(2,1)S(1)}, bf16[280,128]{1,0:T(8,128)(2,1)S(1)}, u32[]{:S(2)}, u32[]{:S(2)}) collective-permute-start(bf16[280,128]{1,0:T(8,128)(2,1)S(1)} %get-tuple-element.24), channel_id=1, source_target_pairs={{0,4},{4,8},{8,12},{12,0},{1,5},{5,9},{9,13},{13,1},{2,6},{6,10},{... | collective-permute-start | bytes 215048 | tf_op jit(solution)/shard_map/ppermute | solution.py:536
  70.0 6.6 %collective-permute-start.23 = (bf16[280,128]{1,0:T(8,128)(2,1)S(1)}, bf16[280,128]{1,0:T(8,128)(2,1)S(1)}, u32[]{:S(2)}, u32[]{:S(2)}) collective-permute-start(bf16[280,128]{1,0:T(8,128)(2,1)S(1)} %get-tuple-element.25), channel_id=1, source_target_pairs={{0,8},{4,12},{8,0},{12,4},{1,9},{5,13},{9,1},{13,5},{2,10},{6,14},... | collective-permute-start | bytes 215048 | tf_op jit(solution)/shard_map/ppermute | solution.py:536
  70.0 6.6 %collective-permute-start.24 = (bf16[280,128]{1,0:T(8,128)(2,1)S(1)}, bf16[280,128]{1,0:T(8,128)(2,1)S(1)}, u32[]{:S(2)}, u32[]{:S(2)}) collective-permute-start(bf16[280,128]{1,0:T(8,128)(2,1)S(1)} %get-tuple-element.26), channel_id=1, source_target_pairs={{0,12},{4,0},{8,4},{12,8},{1,13},{5,1},{9,5},{13,9},{2,14},{6,2},{... | collective-permute-start | bytes 215048 | tf_op jit(solution)/shard_map/ppermute | solution.py:536

commit v5 on v4

--- a/solution.py
+++ b/solution.py
@@ -12,7 +12,9 @@
 CHUNKS = 2
 GROUPS = 2 * CHUNKS
 WIDTH = LANES // GROUPS
-UNROLL = 16
+UNROLL = 32
+EARLY = 32
+LATE = 16
 COST_EARLY = (11, 0.4)
 COST_LATE = (8, 0.2)
 COST_NEAR = [(5, 0.6), (5, 0.6)]
@@ -20,9 +22,12 @@
 DIRECT = True
 MERGED = True
 TIE_LATE = []
+TIE_OWN = True
+TIE_HOP = True
+TIE_EARLY = False
 TIE_SWAP = {'s1': ['near'], 's2': ['near']}
 TIE_NEAR = []
-PARTS = 3
+PARTS = 1
 MIB = 2**20
 
 VMEM = pl.BlockSpec(memory_space=pltpu.VMEM)
@@ -81,14 +86,12 @@
     for part in range(parts):
         for group in range(GROUPS):
             copies[part * GROUPS + group].wait()
-        for j in range(part * step, (part + 1) * step):
-            blocks = [
-                held[(group * count + j) * LANES : (group * count + j + 1) * LANES, :]
-                for group in range(GROUPS)
-            ]
-            out[j] = jnp.dot(
-                jnp.concatenate(blocks, 1), choose, preferred_element_type=jnp.float32
-            ).astype(out.dtype)
+        blocks = [
+            held[pl.ds((group * count + part * step) * LANES, step * LANES), :]
+            for group in range(GROUPS)
+        ]
+        both = jnp.dot(jnp.concatenate(blocks, 1), choose, preferred_element_type=jnp.float32)
+        out[part * step : (part + 1) * step] = both.astype(out.dtype).reshape(step, LANES, LANES)
 
 
 def pack(patterns, chunk, after):
@@ -110,14 +113,14 @@
     )(patterns, *after)
 
 
-def add_tiles(table, start, end, weights, held, total):
+def add_tiles(unroll, table, start, end, weights, held, total):
     group = group_of((LANES, LANES))
 
-    @pl.loop(0, (end - start + UNROLL - 1) // UNROLL)
+    @pl.loop(0, (end - start + unroll - 1) // unroll)
     def _(step):
         products, targets = [], []
-        for u in range(UNROLL):
-            i = start + step * UNROLL + u
+        for u in range(unroll):
+            i = start + step * unroll + u
             code = table[i]
             side = jnp.where(i < end, (code >> 6) & 7, 7)
             targets.append(code & 63)
@@ -142,7 +145,7 @@
     total[...] = jnp.zeros_like(total)
     for copy in copies:
         copy.wait()
-    add_tiles(table, 0, table[table.shape[0] - 1], weights, held, total)
+    add_tiles(EARLY, table, 0, table[table.shape[0] - 1], weights, held, total)
 
 
 def early(table, weights, bands, source_blocks):
@@ -162,28 +165,16 @@
     )(table, weights, *bands)
 
 
-def late_kernel(table, weights, given, right, left, packed, total, held, sems):
-    fetch = pltpu.make_async_copy(given, total, sems.at[0])
-    fetch.start()
-    first = lax.axis_index("tile") < 2
-
-    @pl.when(first)
-    def _():
-        pltpu.make_async_copy(right, held, sems.at[1]).start()
-
-    @pl.when(jnp.logical_not(first))
-    def _():
-        pltpu.make_async_copy(left, held, sems.at[1]).start()
-
-    fetch.wait()
-    pltpu.make_async_copy(right, held, sems.at[1]).wait()
-    tiles = weights.shape[0]
-    add_tiles(table, table[table.shape[0] - 1], tiles, weights, held, total)
+def late_kernel(table, weights, given, band, packed, total):
+    total[...] = jnp.zeros_like(total)
+    start = table[table.shape[0] - 1]
+    add_tiles(LATE, table, start, weights.shape[0], weights, band, total)
     blocks = packed.shape[0]
     me = lax.rem(place(), GROUPS)
     group = group_of((LANES, LANES))
     for j in range(blocks):
-        sums = [total[h * blocks + j] for h in range(GROUPS)]
+        places = [h * blocks + j for h in range(GROUPS)]
+        sums = [given[i] + total[i] for i in places]
         out = None
         for r in range(GROUPS):
             want = lax.rem(group + (r + GROUPS) - me, GROUPS)
@@ -194,22 +185,20 @@
         packed[j] = out.astype(packed.dtype)
 
 
-def late(table, weights, total, right, left):
+def late(table, weights, total, band):
     source_blocks = total.shape[0]
     return pl.pallas_call(
         late_kernel,
-        in_specs=[SMEM, VMEM, ANY, ANY, ANY],
+        in_specs=[SMEM, VMEM, VMEM, VMEM],
         out_specs=VMEM,
         out_shape=jax.ShapeDtypeStruct((source_blocks // GROUPS, LANES, LANES), weights.dtype),
         scratch_shapes=[
             pltpu.VMEM(total.shape, jnp.float32),
-            pltpu.VMEM(right.shape, weights.dtype),
-            pltpu.SemaphoreType.DMA((2,)),
         ],
         compiler_params=params(14),
         cost_estimate=cost(*COST_LATE),
         name="late",
-    )(table, weights, total, right, left)
+    )(table, weights, total, band)
 
 
 def products_of(fields, pieces):
@@ -278,7 +267,7 @@
         if not split:
             outs[0][to] = value.astype(outs[0].dtype)
             return
-        hop = lax.rem(to - lax.axis_index("tile") + 4, 4)
+        hop = to ^ lax.axis_index("tile")
         for k, out in enumerate(outs):
 
             @pl.when(hop == k)
@@ -347,7 +336,7 @@
         if not split:
             outs[0][to] = value.astype(outs[0].dtype)
             return
-        hop = lax.rem(to - lax.axis_index("tile") + 4, 4)
+        hop = to ^ lax.axis_index("tile")
         for k, out in enumerate(outs):
 
             @pl.when(hop == k)
@@ -413,6 +402,10 @@
     )(*parts)
 
 
+def over_tile(x, flip):
+    return lax.ppermute(x, "tile", [(i, i ^ flip) for i in range(4)])
+
+
 def plane_permute(x, to):
     pairs = []
     for m in range(2):
@@ -456,7 +449,7 @@
     tiles = tile_source.shape[0]
     owner = tile_band[:, 0]
     if bands == 4:
-        hop = jnp.remainder(owner - z, 4)
+        hop = owner ^ z
         is_late = hop == 2
         slot = jnp.where(hop == 3, 2, jnp.where(is_late, 0, hop))
     else:
@@ -487,27 +480,29 @@
     table = tile_table(
         tile_source, tile_band, tile_block, patterns.shape[0] // LANES, bands, z
     )
-    owns, totals, rights, lefts = [], [], [], []
+    owns, totals, lasts, pieces = [], [], [], []
     for chunk in range(CHUNKS):
         own = pack(patterns, chunk, owns[-1:])
         owns.append(own)
         if bands == 4:
-            from_left = lax.ppermute(own, "tile", [(i, (i + 1) % 4) for i in range(4)])
-            from_right = lax.ppermute(own, "tile", [(i, (i + 3) % 4) for i in range(4)])
-            near = [own, from_right, from_left]
-            if chunk:
-                totals[-1], from_right, from_left = lax.optimization_barrier(
-                    (totals[-1], from_right, from_left)
-                )
-            rights.append(lax.ppermute(from_right, "tile", [(1, 0), (2, 1)]))
-            lefts.append(lax.ppermute(from_left, "tile", [(1, 2), (2, 3)]))
+            if chunk and TIE_OWN:
+                own = lax.optimization_barrier((own, far))[0]
+            far = over_tile(own, 3)
+            near = over_tile(own, 1)
+            known = [own, near, far]
+            if chunk and TIE_HOP:
+                pieces.append(late(table, remap_tiles, totals[0], lasts[0]))
+                passed = lax.optimization_barrier((far, pieces[0]))[0]
+            else:
+                passed = far
+            lasts.append(over_tile(passed, 1))
         else:
             gathered = lax.all_gather(own, "tile", axis=0)
-            near = [gathered.reshape((-1,) + gathered.shape[2:])]
-            rights.append(own)
-            lefts.append(own)
-        totals.append(early(table, remap_tiles, near, source_blocks))
-    totals = list(lax.optimization_barrier(totals))
+            known = [gathered.reshape((-1,) + gathered.shape[2:])]
+            lasts.append(own)
+        totals.append(early(table, remap_tiles, known, source_blocks))
+    if TIE_EARLY:
+        totals = list(lax.optimization_barrier(totals))
     sums, past, raw = [], {}, []
     for chunk in range(CHUNKS):
 
@@ -515,8 +510,11 @@
             held = [past[name] for name in names if name in past]
             return lax.optimization_barrier((x, *held))[0] if held else x
 
-        total = after(totals[chunk], TIE_LATE)
-        piece = late(table, remap_tiles, total, rights[chunk], lefts[chunk])
+        if chunk < len(pieces):
+            piece = pieces[chunk]
+        else:
+            total = after(totals[chunk], TIE_LATE)
+            piece = late(table, remap_tiles, total, lasts[chunk])
         near, away, r1, r2, d = gather_plane(piece, {k: [past[n] for n in v if n in past] for k, v in TIE_SWAP.items()})
         part = near_scores(rows, [after(near[0], TIE_NEAR), *near[1:]], chunk)
         raw.append(part)
@@ -532,8 +530,7 @@
         past = dict(piece=piece, other=near[1], r1=r1, r2=r2, d=d, near=part, away=parts[0])
         if bands == 4:
             for k in (1, 2, 3):
-                pairs = [(i, (i + k) % 4) for i in range(4)]
-                parts[k] = lax.ppermute(parts[k], "tile", pairs)
+                parts[k] = over_tile(parts[k], k)
             sums += parts
             past["sum1"], past["sum2"], past["sum3"] = parts[1:]
         elif MERGED:

time: 77.6 us -> 77.7 us (level)
  waiting for transfers between devices: 22.3 us -> 24.4 us
  Pallas kernels: 19.5 us -> 17.9 us
    ppermute x11 -> x9, waiting for transfers between devices: 14.8 us -> 17.7 us  [over_tile(): return lax.ppermute(x, 'tile', [(i, i ^ flip) for i in range(4)])]
    pallas_call x2, Pallas kernels: 6.81 us -> 5.66 us  [early(): pl.pallas_call(early_kernel, in_specs=[SMEM, VMEM] + [ANY] * len(bands),...]
    ppermute x14, waiting for transfers between devices: 7.56 us -> 6.77 us  [plane_permute(): return lax.ppermute(x, PLANE, pairs)]
    ppermute x11 -> x9, starting transfers between devices: 20.6 us -> 20.5 us  [over_tile(): return lax.ppermute(x, 'tile', [(i, i ^ flip) for i in range(4)])]
  transfers between devices with their start and end apart: 25 -> 23, of which waited for: 10 -> 7; matrix products, arithmetic and copies ran while one was open for 2% -> 2% of each run, Pallas kernels for 20% -> 18%
where the time goes in v5:
time: 77.7 us; the launch traced here: 77.5 us
  starting transfers between devices  30.5 us (39%)
  waiting for transfers between devices  24.4 us (31%)
  Pallas kernels  17.9 us (23%)
  other arithmetic  2.29 us (3%)
  local copies, waits for them, and re-layouts  2.21 us (3%)
    ppermute x9, starting transfers between devices, over_tile(): return lax.ppermute(x, 'tile', [(i, i ^ flip) for i in range(4)])  20.5 us
    ppermute x9, waiting for transfers between devices, over_tile(): return lax.ppermute(x, 'tile', [(i, i ^ flip) for i in range(4)])  17.7 us
    ppermute x14, starting transfers between devices, plane_permute(): return lax.ppermute(x, PLANE, pairs)  9.97 us
    ppermute x14, waiting for transfers between devices, plane_permute(): return lax.ppermute(x, PLANE, pairs)  6.77 us
    pallas_call x2, Pallas kernels, early(): pl.pallas_call(early_kernel, in_specs=[SMEM, VMEM] + [ANY] * len(bands),...  5.66 us
    pallas_call x2, Pallas kernels, pack(): pl.pallas_call(functools.partial(pack_kernel, parts, chunk), in_specs=[AN...  5 us
    pallas_call x2, Pallas kernels, late(): pl.pallas_call(late_kernel, in_specs=[SMEM, VMEM, VMEM, VMEM], out_specs=...  3.11 us
    unnamed x16, local copies, waits for them, and re-layouts  2.21 us
  transfers between devices with their start and end apart: 23, of which 7 were waited for; matrix products, arithmetic and copies ran while one was open for 2% of the time, Pallas kernels for 18%

profile of v5, /device:TPU:0, one launch (start us, length us, event | category | flops | bytes accessed | tf_op | source)
XLA Modules:
  0.0 77.5 jit_solution(17069891157727731903)
XLA Ops:
  0.0 2.5 %pack.2.rest_0_ = bf16[9,128,128]{2,1,0:T(8,128)(2,1)} custom-call(bf16[4608,512]{1,0:T(8,128)(2,1)} %patterns.3), custom_call_target="tpu_custom_call" | custom-call | flops 150000000 | bytes 2411724 | tf_op jit(solution)/shard_map/pack/pallas_call | solution.py:101
  2.5 5.1 %collective-permute-start = (bf16[9,128,128]{2,1,0:T(8,128)(2,1)}, bf16[9,128,128]{2,1,0:T(8,128)(2,1)S(1)}, u32[]{:S(2)}, u32[]{:S(2)}) collective-permute-start(bf16[9,128,128]{2,1,0:T(8,128)(2,1)} %pack.2.rest_0_), channel_id=1, source_target_pairs={{0,12},{4,8},{8,4},{12,0},{1,13},{5,9},{9,5},{13,1},{2,14},{6,10},... | collective-permute-start | bytes 884744 | tf_op jit(solution)/shard_map/ppermute | solution.py:406
  7.6 2.5 %pack.3.rest_0_ = bf16[9,128,128]{2,1,0:T(8,128)(2,1)} custom-call(bf16[4608,512]{1,0:T(8,128)(2,1)} %patterns.3, bf16[9,128,128]{2,1,0:T(8,128)(2,1)} %pack.2.rest_0_), custom_call_target="tpu_custom_call" | custom-call | flops 150000000 | bytes 2411724 | tf_op jit(solution)/shard_map/pack/pallas_call | solution.py:101
  10.2 0.6 fusion
  10.8 0.2 convert_reduce_fusion
  11.0 4.7 %collective-permute-done.rest_2_ = bf16[9,128,128]{2,1,0:T(8,128)(2,1)S(1)} collective-permute-done((bf16[9,128,128]{2,1,0:T(8,128)(2,1)}, bf16[9,128,128]{2,1,0:T(8,128)(2,1)S(1)}, u32[]{:S(2)}, u32[]{:S(2)}) %collective-permute-start) | collective-permute-done | bytes 294944 | tf_op jit(solution)/shard_map/ppermute | solution.py:406
  15.7 3.8 %collective-permute-start.2 = (bf16[9,128,128]{2,1,0:T(8,128)(2,1)}, bf16[9,128,128]{2,1,0:T(8,128)(2,1)S(1)}, u32[]{:S(2)}, u32[]{:S(2)}) collective-permute-start(bf16[9,128,128]{2,1,0:T(8,128)(2,1)} %pack.3.rest_0_), channel_id=1, source_target_pairs={{0,12},{4,8},{8,4},{12,0},{1,13},{5,9},{9,5},{13,1},{2,14},{6,10},... | collective-permute-start | bytes 884744 | tf_op jit(solution)/shard_map/ppermute | solution.py:406
  19.5 2.9 %collective-permute-start.4 = (bf16[9,128,128]{2,1,0:T(8,128)(2,1)S(1)}, bf16[9,128,128]{2,1,0:T(8,128)(2,1)S(1)}, u32[]{:S(2)}, u32[]{:S(2)}) collective-permute-start(bf16[9,128,128]{2,1,0:T(8,128)(2,1)S(1)} %collective-permute-done.rest_2_), channel_id=1, source_target_pairs={{0,4},{4,0},{8,12},{12,8},{1,5},{5,1},{9,13},{13,9},{2,6},{6,2},{1... | collective-permute-start | bytes 884744 | tf_op jit(solution)/shard_map/ppermute | solution.py:406
  22.4 0.1 select_reduce_fusion
  22.5 0.7 compare_select_fusion.2.table
  23.2 0.1 collective-permute-start.1
  23.3 0.0 copy-start
  23.3 2.2 %copy-done = bf16[128,128,128]{2,1,0:T(8,128)(2,1)S(1)} copy-done((bf16[128,128,128]{2,1,0:T(8,128)(2,1)S(1)}, bf16[128,128,128]{2,1,0:T(8,128)(2,1)}, u32[]{:S(2)}) %copy-start) | copy-done | bytes 4194328
  25.5 2.8 %early.3.given = f32[32,128,128]{2,1,0:T(8,128)S(1)} custom-call(s32[192]{0:T(256)S(1)} %compare_select_fusion.2.table, bf16[128,128,128]{2,1,0:T(8,128)(2,1)S(1)} %copy-done, bf16[9,128,128]{2,1,0:T(8,128)(2,1)S(1)} %copy-done.3, bf16[9,128,128]{2,1,0:T(8,128)(2,1)S(1)} %collective-permute-done.3.rest_1_, bf16[9,128,128]{2,1,0:T(8,128)(2,1)S(1)} %collective-permute-done.rest_2_), custom_call_target="tpu_custom_call" | custom-call | flops 400000000 | bytes 11534336 | tf_op jit(solution)/shard_map/early/pallas_call | solution.py:153
  28.3 5.9 %collective-permute-done.4.band = bf16[9,128,128]{2,1,0:T(8,128)(2,1)S(1)} collective-permute-done((bf16[9,128,128]{2,1,0:T(8,128)(2,1)S(1)}, bf16[9,128,128]{2,1,0:T(8,128)(2,1)S(1)}, u32[]{:S(2)}, u32[]{:S(2)}) %collective-permute-start.4) | collective-permute-done | bytes 294944 | tf_op jit(solution)/shard_map/ppermute | solution.py:406
  34.2 1.6 %late.2.mine = bf16[8,128,128]{2,1,0:T(8,128)(2,1)S(1)} custom-call(s32[192]{0:T(256)S(1)} %compare_select_fusion.2.table, bf16[128,128,128]{2,1,0:T(8,128)(2,1)S(1)} %copy-done.1, f32[32,128,128]{2,1,0:T(8,128)S(1)} %early.3.given, bf16[9,128,128]{2,1,0:T(8,128)(2,1)S(1)} %collective-permute-done.4.band), custom_call_target="tpu_custom_call" | custom-call | flops 200000000 | bytes 8388608 | tf_op jit(solution)/shard_map/late/pallas_call | solution.py:190
  35.8 3.5 %collective-permute-start.5 = (bf16[9,128,128]{2,1,0:T(8,128)(2,1)S(1)}, bf16[9,128,128]{2,1,0:T(8,128)(2,1)S(1)}, u32[]{:S(2)}, u32[]{:S(2)}) collective-permute-start(bf16[9,128,128]{2,1,0:T(8,128)(2,1)S(1)} %collective-permute-done.2.rest_2_), channel_id=1, source_target_pairs={{0,4},{4,0},{8,12},{12,8},{1,5},{5,1},{9,13},{13,9},{2,6},{6,2},{1... | collective-permute-start | bytes 884744 | tf_op jit(solution)/shard_map/ppermute | solution.py:406
  39.3 1.5 %collective-permute-start.9 = (bf16[8,128,128]{2,1,0:T(8,128)(2,1)S(1)}, bf16[8,128,128]{2,1,0:T(8,128)(2,1)S(1)}, u32[]{:S(2)}, u32[]{:S(2)}) collective-permute-start(bf16[8,128,128]{2,1,0:T(8,128)(2,1)S(1)} %late.2.mine), channel_id=1, source_target_pairs={{0,2},{1,17},{2,0},{3,19},{16,18},{17,1},{18,16},{19,3},{4,6},{5,2... | collective-permute-start | bytes 786440 | tf_op jit(solution)/shard_map/ppermute | solution.py:416
  40.8 1.5 %collective-permute-start.10 = (bf16[8,128,128]{2,1,0:T(8,128)(2,1)S(1)}, bf16[8,128,128]{2,1,0:T(8,128)(2,1)S(1)}, u32[]{:S(2)}, u32[]{:S(2)}) collective-permute-start(bf16[8,128,128]{2,1,0:T(8,128)(2,1)S(1)} %late.2.mine), channel_id=1, source_target_pairs={{0,16},{1,3},{2,18},{3,1},{16,0},{17,19},{18,2},{19,17},{4,20},{5,... | collective-permute-start | bytes 786440 | tf_op jit(solution)/shard_map/ppermute | solution.py:416
  42.3 2.8 %early.2.given = f32[32,128,128]{2,1,0:T(8,128)S(1)} custom-call(s32[192]{0:T(256)S(1)} %compare_select_fusion.2.table, bf16[128,128,128]{2,1,0:T(8,128)(2,1)S(1)} %copy-done.1, bf16[9,128,128]{2,1,0:T(8,128)(2,1)S(1)} %copy-done.4, bf16[9,128,128]{2,1,0:T(8,128)(2,1)S(1)} %collective-permute-done.1.rest_1_, ...), custom_call_target="tpu_custom_call" | custom-call | flops 400000000 | bytes 11534336 | tf_op jit(solution)/shard_map/early/pallas_call | solution.py:153
  45.1 0.0 copy-start.2
  45.1 1.4 %collective-permute-done.5.band = bf16[9,128,128]{2,1,0:T(8,128)(2,1)S(1)} collective-permute-done((bf16[9,128,128]{2,1,0:T(8,128)(2,1)S(1)}, bf16[9,128,128]{2,1,0:T(8,128)(2,1)S(1)}, u32[]{:S(2)}, u32[]{:S(2)}) %collective-permute-start.5) | collective-permute-done | bytes 294944 | tf_op jit(solution)/shard_map/ppermute | solution.py:406
  46.5 1.6 %late.3.mine = bf16[8,128,128]{2,1,0:T(8,128)(2,1)S(1)} custom-call(s32[192]{0:T(256)S(1)} %compare_select_fusion.2.table, bf16[128,128,128]{2,1,0:T(8,128)(2,1)S(1)} %copy-done.1, f32[32,128,128]{2,1,0:T(8,128)S(1)} %early.2.given, bf16[9,128,128]{2,1,0:T(8,128)(2,1)S(1)} %collective-permute-done.5.band), custom_call_target="tpu_custom_call" | custom-call | flops 200000000 | bytes 8388608 | tf_op jit(solution)/shard_map/late/pallas_call | solution.py:190
  48.1 1.6 %collective-permute-start.7 = (bf16[8,128,128]{2,1,0:T(8,128)(2,1)S(1)}, bf16[8,128,128]{2,1,0:T(8,128)(2,1)S(1)}, u32[]{:S(2)}, u32[]{:S(2)}) collective-permute-start(bf16[8,128,128]{2,1,0:T(8,128)(2,1)S(1)} %late.3.mine), channel_id=1, source_target_pairs={{0,2},{1,17},{2,0},{3,19},{16,18},{17,1},{18,16},{19,3},{4,6},{5,2... | collective-permute-start | bytes 786440 | tf_op jit(solution)/shard_map/ppermute | solution.py:416
  49.6 0.0 collective-permute-done.9.rest_0_.rest_5_
  49.6 0.0 collective-permute-start.12
  49.6 1.5 %collective-permute-start.17 = (bf16[8,128,128]{2,1,0:T(8,128)(2,1)S(1)}, bf16[8,128,128]{2,1,0:T(8,128)(2,1)S(1)}, u32[]{:S(2)}, u32[]{:S(2)}) collective-permute-start(bf16[8,128,128]{2,1,0:T(8,128)(2,1)S(1)} %collective-permute-done.9.rest_0_.rest_5_), channel_id=1, source_target_pairs={{0,16},{1,3},{2,18},{3,1},{16,0},{17,19},{18,2},{19,17},{4,20},{5,... | collective-permute-start | bytes 786440 | tf_op jit(solution)/shard_map/ppermute | solution.py:416
  51.2 0.0 collective-permute-done.10.rest_3_.rest_0_
  51.2 0.0 collective-permute-start.11
  51.2 0.0 collective-permute-done.8.other
  51.2 0.8 collective-permute-start.6
  51.9 4.3 %collective-permute-done.7.rest_0_.rest_5_ = bf16[8,128,128]{2,1,0:T(8,128)(2,1)S(1)} collective-permute-done((bf16[8,128,128]{2,1,0:T(8,128)(2,1)S(1)}, bf16[8,128,128]{2,1,0:T(8,128)(2,1)S(1)}, u32[]{:S(2)}, u32[]{:S(2)}) %collective-permute-start.7) | collective-permute-done | bytes 262176 | tf_op jit(solution)/shard_map/ppermute | solution.py:416
  56.3 1.5 %collective-permute-start.14 = (bf16[8,128,128]{2,1,0:T(8,128)(2,1)S(1)}, bf16[8,128,128]{2,1,0:T(8,128)(2,1)S(1)}, u32[]{:S(2)}, u32[]{:S(2)}) collective-permute-start(bf16[8,128,128]{2,1,0:T(8,128)(2,1)S(1)} %collective-permute-done.7.rest_0_.rest_5_), channel_id=1, source_target_pairs={{0,16},{1,3},{2,18},{3,1},{16,0},{17,19},{18,2},{19,17},{4,20},{5,... | collective-permute-start | bytes 786440 | tf_op jit(solution)/shard_map/ppermute | solution.py:416
  57.8 0.5 collective-permute-start.18
  58.3 0.9 %near.2.rest_8_ = f32[280,128]{1,0:T(8,128)S(1)} custom-call(bf16[280,4096]{1,0:T(8,128)(2,1)S(1)} %bitcast.15, bf16[8,128,128]{2,1,0:T(8,128)(2,1)S(1)} %late.2.mine, bf16[8,128,128]{2,1,0:T(8,128)(2,1)S(1)} %collective-permute-done.8.other, bf16[8,128,128]{2,1,0:T(8,128)(2,1)S(1)} %collective-permute-done.9.rest_0_.rest_5_, ...), custom_call_target="tpu_custom_call" | custom-call | flops 600000000 | bytes 5242880 | tf_op jit(solution)/shard_map/near/pallas_call | solution.py:248
  59.3 1.0 %collective-permute-start.16 = (bf16[8,128,128]{2,1,0:T(8,128)(2,1)S(1)}, bf16[8,128,128]{2,1,0:T(8,128)(2,1)S(1)}, u32[]{:S(2)}, u32[]{:S(2)}) collective-permute-start(bf16[8,128,128]{2,1,0:T(8,128)(2,1)S(1)} %collective-permute-done.6.rest_3_.rest_0_), channel_id=1, source_target_pairs={{0,1},{1,0},{2,3},{3,2},{16,17},{17,16},{18,19},{19,18},{4,5},{5,4... | collective-permute-start | bytes 786440 | tf_op jit(solution)/shard_map/ppermute | solution.py:416
  60.2 0.0 collective-permute-start.13
  60.3 2.4 %collective-permute-done.14.rest_2_.rest_7_ = bf16[8,128,128]{2,1,0:T(8,128)(2,1)S(1)} collective-permute-done((bf16[8,128,128]{2,1,0:T(8,128)(2,1)S(1)}, bf16[8,128,128]{2,1,0:T(8,128)(2,1)S(1)}, u32[]{:S(2)}, u32[]{:S(2)}) %collective-permute-start.14) | collective-permute-done | bytes 262176 | tf_op jit(solution)/shard_map/ppermute | solution.py:416
  62.6 0.1 collective-permute-start.15
  62.8 0.9 %raw.1.rest_9_ = f32[280,128]{1,0:T(8,128)S(1)} custom-call(bf16[280,4096]{1,0:T(8,128)(2,1)S(1)} %bitcast.16, bf16[8,128,128]{2,1,0:T(8,128)(2,1)S(1)} %collective-permute-done.10.rest_3_.rest_0_, bf16[8,128,128]{2,1,0:T(8,128)(2,1)S(1)} %collective-permute-done.12.rest_2_.rest_1_, bf16[8,128,128]{2,1,0:T(8,128)(2,1)S(1)} %collective-permute-done.17.rest_2_.rest_7_, ...), custom_call_target="tpu_custom_call" | custom-call | flops 600000000 | bytes 5242880 | tf_op jit(solution)/shard_map/raw/pallas_call | solution.py:318
  63.7 1.0 %near.3.rest_10_ = f32[280,128]{1,0:T(8,128)S(1)} custom-call(bf16[280,4096]{1,0:T(8,128)(2,1)S(1)} %bitcast.17, bf16[8,128,128]{2,1,0:T(8,128)(2,1)S(1)} %late.3.mine, bf16[8,128,128]{2,1,0:T(8,128)(2,1)S(1)} %collective-permute-done.19.other, bf16[8,128,128]{2,1,0:T(8,128)(2,1)S(1)} %collective-permute-done.7.rest_0_.rest_5_, ...), custom_call_target="tpu_custom_call" | custom-call | flops 600000000 | bytes 5242880 | tf_op jit(solution)/shard_map/near/pallas_call | solution.py:248
  64.7 1.3 %last.1 = (f32[280,128]{1,0:T(8,128)S(1)}, bf16[280,128]{1,0:T(8,128)(2,1)S(1)}, bf16[280,128]{1,0:T(8,128)(2,1)S(1)}, bf16[280,128]{1,0:T(8,128)(2,1)S(1)}) custom-call(bf16[280,4096]{1,0:T(8,128)(2,1)S(1)} %bitcast.18, bf16[8,128,128]{2,1,0:T(8,128)(2,1)S(1)} %collective-permute-done.6.rest_3_.rest_0_, ...), custom_call_target="tpu_custom_call" | custom-call | flops 600000000 | bytes 5242880 | tf_op jit(solution)/shard_map/last/pallas_call | solution.py:364
  66.0 2.7 %collective-permute-start.20 = (bf16[280,128]{1,0:T(8,128)(2,1)S(1)}, bf16[280,128]{1,0:T(8,128)(2,1)S(1)}, u32[]{:S(2)}, u32[]{:S(2)}) collective-permute-start(bf16[280,128]{1,0:T(8,128)(2,1)S(1)} %get-tuple-element.18), channel_id=1, source_target_pairs={{0,4},{4,0},{8,12},{12,8},{1,5},{5,1},{9,13},{13,9},{2,6},{6,2},{1... | collective-permute-start | bytes 215048 | tf_op jit(solution)/shard_map/ppermute | solution.py:406
  68.7 1.1 %collective-permute-start.21 = (bf16[280,128]{1,0:T(8,128)(2,1)S(1)}, bf16[280,128]{1,0:T(8,128)(2,1)S(1)}, u32[]{:S(2)}, u32[]{:S(2)}) collective-permute-start(bf16[280,128]{1,0:T(8,128)(2,1)S(1)} %get-tuple-element.19), channel_id=1, source_target_pairs={{0,8},{4,12},{8,0},{12,4},{1,9},{5,13},{9,1},{13,5},{2,10},{6,14},... | collective-permute-start | bytes 215048 | tf_op jit(solution)/shard_map/ppermute | solution.py:406
  69.8 1.3 %collective-permute-start.22 = (bf16[280,128]{1,0:T(8,128)(2,1)S(1)}, bf16[280,128]{1,0:T(8,128)(2,1)S(1)}, u32[]{:S(2)}, u32[]{:S(2)}) collective-permute-start(bf16[280,128]{1,0:T(8,128)(2,1)S(1)} %get-tuple-element.20), channel_id=1, source_target_pairs={{0,12},{4,8},{8,4},{12,0},{1,13},{5,9},{9,5},{13,1},{2,14},{6,10},... | collective-permute-start | bytes 215048 | tf_op jit(solution)/shard_map/ppermute | solution.py:406
  71.1 0.4 collective-permute-done.20
  71.5 5.3 %collective-permute-done.21 = bf16[280,128]{1,0:T(8,128)(2,1)S(1)} collective-permute-done((bf16[280,128]{1,0:T(8,128)(2,1)S(1)}, bf16[280,128]{1,0:T(8,128)(2,1)S(1)}, u32[]{:S(2)}, u32[]{:S(2)}) %collective-permute-start.21) | collective-permute-done | bytes 71712 | tf_op jit(solution)/shard_map/ppermute | solution.py:406
  76.8 0.7 add_bitcast_fusion
  (31 shorter events, 0.1 us)
Async XLA Ops:
  2.5 13.3 %collective-permute-start = (bf16[9,128,128]{2,1,0:T(8,128)(2,1)}, bf16[9,128,128]{2,1,0:T(8,128)(2,1)S(1)}, u32[]{:S(2)}, u32[]{:S(2)}) collective-permute-start(bf16[9,128,128]{2,1,0:T(8,128)(2,1)} %pack.2.rest_0_), channel_id=1, source_target_pairs={{0,12},{4,8},{8,4},{12,0},{1,13},{5,9},{9,5},{13,1},{2,14},{6,10},... | collective-permute-start | bytes 884744 | tf_op jit(solution)/shard_map/ppermute | solution.py:406
  7.6 15.7 %collective-permute-start.3 = (bf16[9,128,128]{2,1,0:T(8,128)(2,1)}, bf16[9,128,128]{2,1,0:T(8,128)(2,1)S(1)}, u32[]{:S(2)}, u32[]{:S(2)}) collective-permute-start(bf16[9,128,128]{2,1,0:T(8,128)(2,1)} %pack.2.rest_0_), channel_id=1, source_target_pairs={{0,4},{4,0},{8,12},{12,8},{1,5},{5,1},{9,13},{13,9},{2,6},{6,2},{1... | collective-permute-start | bytes 884744 | tf_op jit(solution)/shard_map/ppermute | solution.py:406
  7.6 2.6 %copy-start.7 = (s32[128,1]{0,1:T(1,128)S(1)}, s32[128,1]{0,1:T(1,128)}, u32[]{:S(2)}) copy-start(s32[128,1]{0,1:T(1,128)} %param.9) | copy-start | bytes 1540
  7.6 3.2 %copy-start.5 = (s32[128]{0:T(128)S(1)}, s32[128]{0:T(128)}, u32[]{:S(2)}) copy-start(s32[128]{0:T(128)} %param.8) | copy-start | bytes 1540
  7.6 3.2 %copy-start.6 = (s32[128]{0:T(128)S(1)}, s32[128]{0:T(128)}, u32[]{:S(2)}) copy-start(s32[128]{0:T(128)} %param.10) | copy-start | bytes 1540
  7.6 15.7 %copy-start.3 = (bf16[9,128,128]{2,1,0:T(8,128)(2,1)S(1)}, bf16[9,128,128]{2,1,0:T(8,128)(2,1)}, u32[]{:S(2)}) copy-start(bf16[9,128,128]{2,1,0:T(8,128)(2,1)} %pack.2.rest_0_) | copy-start | bytes 884740
  15.7 20.1 %collective-permute-start.2 = (bf16[9,128,128]{2,1,0:T(8,128)(2,1)}, bf16[9,128,128]{2,1,0:T(8,128)(2,1)S(1)}, u32[]{:S(2)}, u32[]{:S(2)}) collective-permute-start(bf16[9,128,128]{2,1,0:T(8,128)(2,1)} %pack.3.rest_0_), channel_id=1, source_target_pairs={{0,12},{4,8},{8,4},{12,0},{1,13},{5,9},{9,5},{13,1},{2,14},{6,10},... | collective-permute-start | bytes 884744 | tf_op jit(solution)/shard_map/ppermute | solution.py:406
  19.5 14.7 %collective-permute-start.4 = (bf16[9,128,128]{2,1,0:T(8,128)(2,1)S(1)}, bf16[9,128,128]{2,1,0:T(8,128)(2,1)S(1)}, u32[]{:S(2)}, u32[]{:S(2)}) collective-permute-start(bf16[9,128,128]{2,1,0:T(8,128)(2,1)S(1)} %collective-permute-done.rest_2_), channel_id=1, source_target_pairs={{0,4},{4,0},{8,12},{12,8},{1,5},{5,1},{9,13},{13,9},{2,6},{6,2},{1... | collective-permute-start | bytes 884744 | tf_op jit(solution)/shard_map/ppermute | solution.py:406
  23.2 19.1 %collective-permute-start.1 = (bf16[9,128,128]{2,1,0:T(8,128)(2,1)}, bf16[9,128,128]{2,1,0:T(8,128)(2,1)S(1)}, u32[]{:S(2)}, u32[]{:S(2)}) collective-permute-start(bf16[9,128,128]{2,1,0:T(8,128)(2,1)} %pack.3.rest_0_), channel_id=1, source_target_pairs={{0,4},{4,0},{8,12},{12,8},{1,5},{5,1},{9,13},{13,9},{2,6},{6,2},{1... | collective-permute-start | bytes 884744 | tf_op jit(solution)/shard_map/ppermute | solution.py:406
  23.3 2.2 %copy-start = (bf16[128,128,128]{2,1,0:T(8,128)(2,1)S(1)}, bf16[128,128,128]{2,1,0:T(8,128)(2,1)}, u32[]{:S(2)}) copy-start(bf16[128,128,128]{2,1,0:T(8,128)(2,1)} %weights.7) | copy-start | bytes 12582916
  25.5 8.7 %copy-start.1 = (bf16[128,128,128]{2,1,0:T(8,128)(2,1)S(1)}, bf16[128,128,128]{2,1,0:T(8,128)(2,1)}, u32[]{:S(2)}) copy-start(bf16[128,128,128]{2,1,0:T(8,128)(2,1)} %weights.7) | copy-start | bytes 12582916
  28.3 14.0 %copy-start.4 = (bf16[9,128,128]{2,1,0:T(8,128)(2,1)S(1)}, bf16[9,128,128]{2,1,0:T(8,128)(2,1)}, u32[]{:S(2)}) copy-start(bf16[9,128,128]{2,1,0:T(8,128)(2,1)} %pack.3.rest_0_) | copy-start | bytes 884740
  35.8 10.7 %collective-permute-start.5 = (bf16[9,128,128]{2,1,0:T(8,128)(2,1)S(1)}, bf16[9,128,128]{2,1,0:T(8,128)(2,1)S(1)}, u32[]{:S(2)}, u32[]{:S(2)}) collective-permute-start(bf16[9,128,128]{2,1,0:T(8,128)(2,1)S(1)} %collective-permute-done.2.rest_2_), channel_id=1, source_target_pairs={{0,4},{4,0},{8,12},{12,8},{1,5},{5,1},{9,13},{13,9},{2,6},{6,2},{1... | collective-permute-start | bytes 884744 | tf_op jit(solution)/shard_map/ppermute | solution.py:406
  39.3 10.4 %collective-permute-start.9 = (bf16[8,128,128]{2,1,0:T(8,128)(2,1)S(1)}, bf16[8,128,128]{2,1,0:T(8,128)(2,1)S(1)}, u32[]{:S(2)}, u32[]{:S(2)}) collective-permute-start(bf16[8,128,128]{2,1,0:T(8,128)(2,1)S(1)} %late.2.mine), channel_id=1, source_target_pairs={{0,2},{1,17},{2,0},{3,19},{16,18},{17,1},{18,16},{19,3},{4,6},{5,2... | collective-permute-start | bytes 786440 | tf_op jit(solution)/shard_map/ppermute | solution.py:416
  40.8 10.4 %collective-permute-start.10 = (bf16[8,128,128]{2,1,0:T(8,128)(2,1)S(1)}, bf16[8,128,128]{2,1,0:T(8,128)(2,1)S(1)}, u32[]{:S(2)}, u32[]{:S(2)}) collective-permute-start(bf16[8,128,128]{2,1,0:T(8,128)(2,1)S(1)} %late.2.mine), channel_id=1, source_target_pairs={{0,16},{1,3},{2,18},{3,1},{16,0},{17,19},{18,2},{19,17},{4,20},{5,... | collective-permute-start | bytes 786440 | tf_op jit(solution)/shard_map/ppermute | solution.py:416
  42.3 8.9 %collective-permute-start.8 = (bf16[8,128,128]{2,1,0:T(8,128)(2,1)S(1)}, bf16[8,128,128]{2,1,0:T(8,128)(2,1)S(1)}, u32[]{:S(2)}, u32[]{:S(2)}) collective-permute-start(bf16[8,128,128]{2,1,0:T(8,128)(2,1)S(1)} %late.2.mine), channel_id=1, source_target_pairs={{0,1},{1,0},{2,3},{3,2},{16,17},{17,16},{18,19},{19,18},{4,5},{5,4... | collective-permute-start | bytes 786440 | tf_op jit(solution)/shard_map/ppermute | solution.py:416
  45.1 13.2 %copy-start.2 = (bf16[8,35,4096]{2,0,1:T(8,128)(2,1)S(1)}, bf16[8,35,4096]{2,0,1:T(8,128)(2,1)}, u32[]{:S(2)}) copy-start(bf16[8,35,4096]{2,0,1:T(8,128)(2,1)} %param.6) | copy-start | bytes 6881284
  48.1 8.2 %collective-permute-start.7 = (bf16[8,128,128]{2,1,0:T(8,128)(2,1)S(1)}, bf16[8,128,128]{2,1,0:T(8,128)(2,1)S(1)}, u32[]{:S(2)}, u32[]{:S(2)}) collective-permute-start(bf16[8,128,128]{2,1,0:T(8,128)(2,1)S(1)} %late.3.mine), channel_id=1, source_target_pairs={{0,2},{1,17},{2,0},{3,19},{16,18},{17,1},{18,16},{19,3},{4,6},{5,2... | collective-permute-start | bytes 786440 | tf_op jit(solution)/shard_map/ppermute | solution.py:416
  49.6 8.2 %collective-permute-start.12 = (bf16[8,128,128]{2,1,0:T(8,128)(2,1)S(1)}, bf16[8,128,128]{2,1,0:T(8,128)(2,1)S(1)}, u32[]{:S(2)}, u32[]{:S(2)}) collective-permute-start(bf16[8,128,128]{2,1,0:T(8,128)(2,1)S(1)} %collective-permute-done.9.rest_0_.rest_5_), channel_id=1, source_target_pairs={{0,1},{1,0},{2,3},{3,2},{16,17},{17,16},{18,19},{19,18},{4,5},{5,4... | collective-permute-start | bytes 786440 | tf_op jit(solution)/shard_map/ppermute | solution.py:416
  49.6 8.2 %collective-permute-start.17 = (bf16[8,128,128]{2,1,0:T(8,128)(2,1)S(1)}, bf16[8,128,128]{2,1,0:T(8,128)(2,1)S(1)}, u32[]{:S(2)}, u32[]{:S(2)}) collective-permute-start(bf16[8,128,128]{2,1,0:T(8,128)(2,1)S(1)} %collective-permute-done.9.rest_0_.rest_5_), channel_id=1, source_target_pairs={{0,16},{1,3},{2,18},{3,1},{16,0},{17,19},{18,2},{19,17},{4,20},{5,... | collective-permute-start | bytes 786440 | tf_op jit(solution)/shard_map/ppermute | solution.py:416
  51.2 7.2 %collective-permute-start.11 = (bf16[8,128,128]{2,1,0:T(8,128)(2,1)S(1)}, bf16[8,128,128]{2,1,0:T(8,128)(2,1)S(1)}, u32[]{:S(2)}, u32[]{:S(2)}) collective-permute-start(bf16[8,128,128]{2,1,0:T(8,128)(2,1)S(1)} %collective-permute-done.10.rest_3_.rest_0_), channel_id=1, source_target_pairs={{0,1},{1,0},{2,3},{3,2},{16,17},{17,16},{18,19},{19,18},{4,5},{5,4... | collective-permute-start | bytes 786440 | tf_op jit(solution)/shard_map/ppermute | solution.py:416
  51.2 8.1 %collective-permute-start.6 = (bf16[8,128,128]{2,1,0:T(8,128)(2,1)S(1)}, bf16[8,128,128]{2,1,0:T(8,128)(2,1)S(1)}, u32[]{:S(2)}, u32[]{:S(2)}) collective-permute-start(bf16[8,128,128]{2,1,0:T(8,128)(2,1)S(1)} %late.3.mine), channel_id=1, source_target_pairs={{0,16},{1,3},{2,18},{3,1},{16,0},{17,19},{18,2},{19,17},{4,20},{5,... | collective-permute-start | bytes 786440 | tf_op jit(solution)/shard_map/ppermute | solution.py:416
  56.3 6.4 %collective-permute-start.14 = (bf16[8,128,128]{2,1,0:T(8,128)(2,1)S(1)}, bf16[8,128,128]{2,1,0:T(8,128)(2,1)S(1)}, u32[]{:S(2)}, u32[]{:S(2)}) collective-permute-start(bf16[8,128,128]{2,1,0:T(8,128)(2,1)S(1)} %collective-permute-done.7.rest_0_.rest_5_), channel_id=1, source_target_pairs={{0,16},{1,3},{2,18},{3,1},{16,0},{17,19},{18,2},{19,17},{4,20},{5,... | collective-permute-start | bytes 786440 | tf_op jit(solution)/shard_map/ppermute | solution.py:416
  57.8 5.9 %collective-permute-start.19 = (bf16[8,128,128]{2,1,0:T(8,128)(2,1)S(1)}, bf16[8,128,128]{2,1,0:T(8,128)(2,1)S(1)}, u32[]{:S(2)}, u32[]{:S(2)}) collective-permute-start(bf16[8,128,128]{2,1,0:T(8,128)(2,1)S(1)} %late.3.mine), channel_id=1, source_target_pairs={{0,1},{1,0},{2,3},{3,2},{16,17},{17,16},{18,19},{19,18},{4,5},{5,4... | collective-permute-start | bytes 786440 | tf_op jit(solution)/shard_map/ppermute | solution.py:416
  57.8 4.9 %collective-permute-start.18 = (bf16[8,128,128]{2,1,0:T(8,128)(2,1)S(1)}, bf16[8,128,128]{2,1,0:T(8,128)(2,1)S(1)}, u32[]{:S(2)}, u32[]{:S(2)}) collective-permute-start(bf16[8,128,128]{2,1,0:T(8,128)(2,1)S(1)} %collective-permute-done.17.rest_2_.rest_7_), channel_id=1, source_target_pairs={{0,1},{1,0},{2,3},{3,2},{16,17},{17,16},{18,19},{19,18},{4,5},{5,4... | collective-permute-start | bytes 786440 | tf_op jit(solution)/shard_map/ppermute | solution.py:416
  59.3 4.4 %collective-permute-start.16 = (bf16[8,128,128]{2,1,0:T(8,128)(2,1)S(1)}, bf16[8,128,128]{2,1,0:T(8,128)(2,1)S(1)}, u32[]{:S(2)}, u32[]{:S(2)}) collective-permute-start(bf16[8,128,128]{2,1,0:T(8,128)(2,1)S(1)} %collective-permute-done.6.rest_3_.rest_0_), channel_id=1, source_target_pairs={{0,1},{1,0},{2,3},{3,2},{16,17},{17,16},{18,19},{19,18},{4,5},{5,4... | collective-permute-start | bytes 786440 | tf_op jit(solution)/shard_map/ppermute | solution.py:416
  60.2 3.5 %collective-permute-start.13 = (bf16[8,128,128]{2,1,0:T(8,128)(2,1)S(1)}, bf16[8,128,128]{2,1,0:T(8,128)(2,1)S(1)}, u32[]{:S(2)}, u32[]{:S(2)}) collective-permute-start(bf16[8,128,128]{2,1,0:T(8,128)(2,1)S(1)} %collective-permute-done.7.rest_0_.rest_5_), channel_id=1, source_target_pairs={{0,1},{1,0},{2,3},{3,2},{16,17},{17,16},{18,19},{19,18},{4,5},{5,4... | collective-permute-start | bytes 786440 | tf_op jit(solution)/shard_map/ppermute | solution.py:416
  62.6 2.0 %collective-permute-start.15 = (bf16[8,128,128]{2,1,0:T(8,128)(2,1)S(1)}, bf16[8,128,128]{2,1,0:T(8,128)(2,1)S(1)}, u32[]{:S(2)}, u32[]{:S(2)}) collective-permute-start(bf16[8,128,128]{2,1,0:T(8,128)(2,1)S(1)} %collective-permute-done.14.rest_2_.rest_7_), channel_id=1, source_target_pairs={{0,1},{1,0},{2,3},{3,2},{16,17},{17,16},{18,19},{19,18},{4,5},{5,4... | collective-permute-start | bytes 786440 | tf_op jit(solution)/shard_map/ppermute | solution.py:416
  66.0 5.5 %collective-permute-start.20 = (bf16[280,128]{1,0:T(8,128)(2,1)S(1)}, bf16[280,128]{1,0:T(8,128)(2,1)S(1)}, u32[]{:S(2)}, u32[]{:S(2)}) collective-permute-start(bf16[280,128]{1,0:T(8,128)(2,1)S(1)} %get-tuple-element.18), channel_id=1, source_target_pairs={{0,4},{4,0},{8,12},{12,8},{1,5},{5,1},{9,13},{13,9},{2,6},{6,2},{1... | collective-permute-start | bytes 215048 | tf_op jit(solution)/shard_map/ppermute | solution.py:406
  68.7 8.1 %collective-permute-start.21 = (bf16[280,128]{1,0:T(8,128)(2,1)S(1)}, bf16[280,128]{1,0:T(8,128)(2,1)S(1)}, u32[]{:S(2)}, u32[]{:S(2)}) collective-permute-start(bf16[280,128]{1,0:T(8,128)(2,1)S(1)} %get-tuple-element.19), channel_id=1, source_target_pairs={{0,8},{4,12},{8,0},{12,4},{1,9},{5,13},{9,1},{13,5},{2,10},{6,14},... | collective-permute-start | bytes 215048 | tf_op jit(solution)/shard_map/ppermute | solution.py:406
  69.8 7.0 %collective-permute-start.22 = (bf16[280,128]{1,0:T(8,128)(2,1)S(1)}, bf16[280,128]{1,0:T(8,128)(2,1)S(1)}, u32[]{:S(2)}, u32[]{:S(2)}) collective-permute-start(bf16[280,128]{1,0:T(8,128)(2,1)S(1)} %get-tuple-element.20), channel_id=1, source_target_pairs={{0,12},{4,8},{8,4},{12,0},{1,13},{5,9},{9,5},{13,1},{2,14},{6,10},... | collective-permute-start | bytes 215048 | tf_op jit(solution)/shard_map/ppermute | solution.py:406

commit v6 on v5

--- a/solution.py
+++ b/solution.py
@@ -324,6 +324,25 @@
         cost_estimate=cost(*COST_AWAY[chunk]),
         name="raw",
     )(fields, *pieces)
+
+
+def both_kernel(fields, *rest):
+    away, near, outs = rest[:8], rest[8:14], rest[14:]
+    raw_kernel(fields, *away, outs[0])
+    near_kernel(fields, *near, outs[1])
+
+
+def both_scores(fields, away, near):
+    rows = fields.shape[0]
+    return pl.pallas_call(
+        both_kernel,
+        in_specs=[VMEM] * (1 + len(away) + len(near)),
+        out_specs=[VMEM] * 2,
+        out_shape=[jax.ShapeDtypeStruct((rows, LANES), jnp.float32)] * 2,
+        compiler_params=params(20),
+        cost_estimate=cost(*COST_AWAY[1]),
+        name="both",
+    )(fields, *away, *near)
 
 
 def last_kernel(split, fields, *rest):
@@ -516,13 +535,14 @@
             total = after(totals[chunk], TIE_LATE)
             piece = late(table, remap_tiles, total, lasts[chunk])
         near, away, r1, r2, d = gather_plane(piece, {k: [past[n] for n in v if n in past] for k, v in TIE_SWAP.items()})
-        part = near_scores(rows, [after(near[0], TIE_NEAR), *near[1:]], chunk)
-        raw.append(part)
-        if MERGED and chunk == 0:
-            far_part = raw_scores(rows, away, chunk)
-            raw.append(far_part)
-            past = dict(piece=piece, other=near[1], r1=r1, r2=r2, d=d, near=part, away=far_part)
+        if chunk == 0:
+            part = near_scores(rows, near, chunk)
+            raw.append(part)
+            kept = away
+            past = dict(piece=piece, other=near[1], r1=r1, r2=r2, d=d, near=part)
             continue
+        far_part, part = both_scores(rows, kept, near)
+        raw += [far_part, part]
         if MERGED:
             parts = list(last_scores(rows, away, raw, bands == 4))
         else:

time: 77.7 us -> 77.3 us (level)
    pallas_call x2 -> x1, Pallas kernels: 1.89 us -> 0.9 us  [near_scores(): pl.pallas_call(near_kernel, in_specs=[VMEM] * (1 + len(pieces)), out_spec...]
    pallas_call x1, Pallas kernels: 0.92 us -> 1.84 us  [both_scores(): pl.pallas_call(both_kernel, in_specs=[VMEM] * (1 + len(away) + len(near))...]
where the time goes in v6:
time: 77.3 us; the launch traced here: 77.2 us
  starting transfers between devices  29.9 us (39%)
  waiting for transfers between devices  24.7 us (32%)
  Pallas kernels  17.8 us (23%)
  other arithmetic  2.29 us (3%)
  local copies, waits for them, and re-layouts  2.21 us (3%)
    ppermute x9, starting transfers between devices, over_tile(): return lax.ppermute(x, 'tile', [(i, i ^ flip) for i in range(4)])  19.9 us
    ppermute x9, waiting for transfers between devices, over_tile(): return lax.ppermute(x, 'tile', [(i, i ^ flip) for i in range(4)])  17.9 us
    ppermute x14, starting transfers between devices, plane_permute(): return lax.ppermute(x, PLANE, pairs)  10 us
    ppermute x14, waiting for transfers between devices, plane_permute(): return lax.ppermute(x, PLANE, pairs)  6.77 us
    pallas_call x2, Pallas kernels, early(): pl.pallas_call(early_kernel, in_specs=[SMEM, VMEM] + [ANY] * len(bands),...  5.66 us
    pallas_call x2, Pallas kernels, pack(): pl.pallas_call(functools.partial(pack_kernel, parts, chunk), in_specs=[AN...  5.01 us
    pallas_call x2, Pallas kernels, late(): pl.pallas_call(late_kernel, in_specs=[SMEM, VMEM, VMEM, VMEM], out_specs=...  3.11 us
    unnamed x16, local copies, waits for them, and re-layouts  2.21 us
  transfers between devices with their start and end apart: 23, of which 7 were waited for; matrix products, arithmetic and copies ran while one was open for 2% of the time, Pallas kernels for 18%

profile of v6, /device:TPU:0, one launch (start us, length us, event | category | flops | bytes accessed | tf_op | source)
XLA Modules:
  0.0 77.2 jit_solution(12934741861321591737)
XLA Ops:
  0.0 2.5 %pack.2.rest_0_ = bf16[9,128,128]{2,1,0:T(8,128)(2,1)} custom-call(bf16[4608,512]{1,0:T(8,128)(2,1)} %patterns.3), custom_call_target="tpu_custom_call" | custom-call | flops 150000000 | bytes 2411724 | tf_op jit(solution)/shard_map/pack/pallas_call | solution.py:101
  2.5 5.1 %collective-permute-start = (bf16[9,128,128]{2,1,0:T(8,128)(2,1)}, bf16[9,128,128]{2,1,0:T(8,128)(2,1)S(1)}, u32[]{:S(2)}, u32[]{:S(2)}) collective-permute-start(bf16[9,128,128]{2,1,0:T(8,128)(2,1)} %pack.2.rest_0_), channel_id=1, source_target_pairs={{0,12},{4,8},{8,4},{12,0},{1,13},{5,9},{9,5},{13,1},{2,14},{6,10},... | collective-permute-start | bytes 884744 | tf_op jit(solution)/shard_map/ppermute | solution.py:425
  7.6 0.0 collective-permute-start.3
  7.6 2.5 %pack.3.rest_0_ = bf16[9,128,128]{2,1,0:T(8,128)(2,1)} custom-call(bf16[4608,512]{1,0:T(8,128)(2,1)} %patterns.3, bf16[9,128,128]{2,1,0:T(8,128)(2,1)} %pack.2.rest_0_), custom_call_target="tpu_custom_call" | custom-call | flops 150000000 | bytes 2411724 | tf_op jit(solution)/shard_map/pack/pallas_call | solution.py:101
  10.2 0.6 fusion
  10.9 0.2 convert_reduce_fusion
  11.0 4.7 %collective-permute-done.rest_2_ = bf16[9,128,128]{2,1,0:T(8,128)(2,1)S(1)} collective-permute-done((bf16[9,128,128]{2,1,0:T(8,128)(2,1)}, bf16[9,128,128]{2,1,0:T(8,128)(2,1)S(1)}, u32[]{:S(2)}, u32[]{:S(2)}) %collective-permute-start) | collective-permute-done | bytes 294944 | tf_op jit(solution)/shard_map/ppermute | solution.py:425
  15.7 3.8 %collective-permute-start.2 = (bf16[9,128,128]{2,1,0:T(8,128)(2,1)}, bf16[9,128,128]{2,1,0:T(8,128)(2,1)S(1)}, u32[]{:S(2)}, u32[]{:S(2)}) collective-permute-start(bf16[9,128,128]{2,1,0:T(8,128)(2,1)} %pack.3.rest_0_), channel_id=1, source_target_pairs={{0,12},{4,8},{8,4},{12,0},{1,13},{5,9},{9,5},{13,1},{2,14},{6,10},... | collective-permute-start | bytes 884744 | tf_op jit(solution)/shard_map/ppermute | solution.py:425
  19.5 2.9 %collective-permute-start.4 = (bf16[9,128,128]{2,1,0:T(8,128)(2,1)S(1)}, bf16[9,128,128]{2,1,0:T(8,128)(2,1)S(1)}, u32[]{:S(2)}, u32[]{:S(2)}) collective-permute-start(bf16[9,128,128]{2,1,0:T(8,128)(2,1)S(1)} %collective-permute-done.rest_2_), channel_id=1, source_target_pairs={{0,4},{4,0},{8,12},{12,8},{1,5},{5,1},{9,13},{13,9},{2,6},{6,2},{1... | collective-permute-start | bytes 884744 | tf_op jit(solution)/shard_map/ppermute | solution.py:425
  22.4 0.1 select_reduce_fusion
  22.5 0.7 compare_select_fusion.2.table
  23.2 0.1 collective-permute-start.1
  23.3 0.0 collective-permute-done.3.rest_1_
  23.3 0.0 copy-start
  23.3 2.2 %copy-done = bf16[128,128,128]{2,1,0:T(8,128)(2,1)S(1)} copy-done((bf16[128,128,128]{2,1,0:T(8,128)(2,1)S(1)}, bf16[128,128,128]{2,1,0:T(8,128)(2,1)}, u32[]{:S(2)}) %copy-start) | copy-done | bytes 4194328
  25.5 2.8 %early.3.given = f32[32,128,128]{2,1,0:T(8,128)S(1)} custom-call(s32[192]{0:T(256)S(1)} %compare_select_fusion.2.table, bf16[128,128,128]{2,1,0:T(8,128)(2,1)S(1)} %copy-done, bf16[9,128,128]{2,1,0:T(8,128)(2,1)S(1)} %copy-done.3, bf16[9,128,128]{2,1,0:T(8,128)(2,1)S(1)} %collective-permute-done.3.rest_1_, bf16[9,128,128]{2,1,0:T(8,128)(2,1)S(1)} %collective-permute-done.rest_2_), custom_call_target="tpu_custom_call" | custom-call | flops 400000000 | bytes 11534336 | tf_op jit(solution)/shard_map/early/pallas_call | solution.py:153
  28.3 5.9 %collective-permute-done.4.band = bf16[9,128,128]{2,1,0:T(8,128)(2,1)S(1)} collective-permute-done((bf16[9,128,128]{2,1,0:T(8,128)(2,1)S(1)}, bf16[9,128,128]{2,1,0:T(8,128)(2,1)S(1)}, u32[]{:S(2)}, u32[]{:S(2)}) %collective-permute-start.4) | collective-permute-done | bytes 294944 | tf_op jit(solution)/shard_map/ppermute | solution.py:425
  34.2 1.6 %late.2.mine = bf16[8,128,128]{2,1,0:T(8,128)(2,1)S(1)} custom-call(s32[192]{0:T(256)S(1)} %compare_select_fusion.2.table, bf16[128,128,128]{2,1,0:T(8,128)(2,1)S(1)} %copy-done.1, f32[32,128,128]{2,1,0:T(8,128)S(1)} %early.3.given, bf16[9,128,128]{2,1,0:T(8,128)(2,1)S(1)} %collective-permute-done.4.band), custom_call_target="tpu_custom_call" | custom-call | flops 200000000 | bytes 8388608 | tf_op jit(solution)/shard_map/late/pallas_call | solution.py:190
  35.8 0.0 collective-permute-done.2.rest_2_
  35.8 3.2 %collective-permute-start.5 = (bf16[9,128,128]{2,1,0:T(8,128)(2,1)S(1)}, bf16[9,128,128]{2,1,0:T(8,128)(2,1)S(1)}, u32[]{:S(2)}, u32[]{:S(2)}) collective-permute-start(bf16[9,128,128]{2,1,0:T(8,128)(2,1)S(1)} %collective-permute-done.2.rest_2_), channel_id=1, source_target_pairs={{0,4},{4,0},{8,12},{12,8},{1,5},{5,1},{9,13},{13,9},{2,6},{6,2},{1... | collective-permute-start | bytes 884744 | tf_op jit(solution)/shard_map/ppermute | solution.py:425
  39.0 1.5 %collective-permute-start.9 = (bf16[8,128,128]{2,1,0:T(8,128)(2,1)S(1)}, bf16[8,128,128]{2,1,0:T(8,128)(2,1)S(1)}, u32[]{:S(2)}, u32[]{:S(2)}) collective-permute-start(bf16[8,128,128]{2,1,0:T(8,128)(2,1)S(1)} %late.2.mine), channel_id=1, source_target_pairs={{0,2},{1,17},{2,0},{3,19},{16,18},{17,1},{18,16},{19,3},{4,6},{5,2... | collective-permute-start | bytes 786440 | tf_op jit(solution)/shard_map/ppermute | solution.py:435
  40.5 1.5 %collective-permute-start.10 = (bf16[8,128,128]{2,1,0:T(8,128)(2,1)S(1)}, bf16[8,128,128]{2,1,0:T(8,128)(2,1)S(1)}, u32[]{:S(2)}, u32[]{:S(2)}) collective-permute-start(bf16[8,128,128]{2,1,0:T(8,128)(2,1)S(1)} %late.2.mine), channel_id=1, source_target_pairs={{0,16},{1,3},{2,18},{3,1},{16,0},{17,19},{18,2},{19,17},{4,20},{5,... | collective-permute-start | bytes 786440 | tf_op jit(solution)/shard_map/ppermute | solution.py:435
  42.0 0.0 collective-permute-start.8
  42.0 0.0 collective-permute-done.1.rest_1_
  42.0 2.8 %early.2.given = f32[32,128,128]{2,1,0:T(8,128)S(1)} custom-call(s32[192]{0:T(256)S(1)} %compare_select_fusion.2.table, bf16[128,128,128]{2,1,0:T(8,128)(2,1)S(1)} %copy-done.1, bf16[9,128,128]{2,1,0:T(8,128)(2,1)S(1)} %copy-done.4, bf16[9,128,128]{2,1,0:T(8,128)(2,1)S(1)} %collective-permute-done.1.rest_1_, ...), custom_call_target="tpu_custom_call" | custom-call | flops 400000000 | bytes 11534336 | tf_op jit(solution)/shard_map/early/pallas_call | solution.py:153
  44.8 0.0 copy-start.2
  44.9 1.7 %collective-permute-done.5.band = bf16[9,128,128]{2,1,0:T(8,128)(2,1)S(1)} collective-permute-done((bf16[9,128,128]{2,1,0:T(8,128)(2,1)S(1)}, bf16[9,128,128]{2,1,0:T(8,128)(2,1)S(1)}, u32[]{:S(2)}, u32[]{:S(2)}) %collective-permute-start.5) | collective-permute-done | bytes 294944 | tf_op jit(solution)/shard_map/ppermute | solution.py:425
  46.5 1.6 %late.3.rest_8_ = bf16[8,128,128]{2,1,0:T(8,128)(2,1)S(1)} custom-call(s32[192]{0:T(256)S(1)} %compare_select_fusion.2.table, bf16[128,128,128]{2,1,0:T(8,128)(2,1)S(1)} %copy-done.1, f32[32,128,128]{2,1,0:T(8,128)S(1)} %early.2.given, bf16[9,128,128]{2,1,0:T(8,128)(2,1)S(1)} %collective-permute-done.5.band), custom_call_target="tpu_custom_call" | custom-call | flops 200000000 | bytes 8388608 | tf_op jit(solution)/shard_map/late/pallas_call | solution.py:190
  48.1 1.6 %collective-permute-start.7 = (bf16[8,128,128]{2,1,0:T(8,128)(2,1)S(1)}, bf16[8,128,128]{2,1,0:T(8,128)(2,1)S(1)}, u32[]{:S(2)}, u32[]{:S(2)}) collective-permute-start(bf16[8,128,128]{2,1,0:T(8,128)(2,1)S(1)} %late.3.rest_8_), channel_id=1, source_target_pairs={{0,2},{1,17},{2,0},{3,19},{16,18},{17,1},{18,16},{19,3},{4,6},{5,2... | collective-permute-start | bytes 786440 | tf_op jit(solution)/shard_map/ppermute | solution.py:435
  49.6 0.0 collective-permute-done.9.rest_0_.rest_5_
  49.6 1.5 %collective-permute-start.17 = (bf16[8,128,128]{2,1,0:T(8,128)(2,1)S(1)}, bf16[8,128,128]{2,1,0:T(8,128)(2,1)S(1)}, u32[]{:S(2)}, u32[]{:S(2)}) collective-permute-start(bf16[8,128,128]{2,1,0:T(8,128)(2,1)S(1)} %collective-permute-done.9.rest_0_.rest_5_), channel_id=1, source_target_pairs={{0,16},{1,3},{2,18},{3,1},{16,0},{17,19},{18,2},{19,17},{4,20},{5,... | collective-permute-start | bytes 786440 | tf_op jit(solution)/shard_map/ppermute | solution.py:435
  51.2 0.8 collective-permute-start.6
  51.9 4.3 %collective-permute-done.7.rest_10_.rest_5_ = bf16[8,128,128]{2,1,0:T(8,128)(2,1)S(1)} collective-permute-done((bf16[8,128,128]{2,1,0:T(8,128)(2,1)S(1)}, bf16[8,128,128]{2,1,0:T(8,128)(2,1)S(1)}, u32[]{:S(2)}, u32[]{:S(2)}) %collective-permute-start.7) | collective-permute-done | bytes 262176 | tf_op jit(solution)/shard_map/ppermute | solution.py:435
  56.3 1.5 %collective-permute-start.14 = (bf16[8,128,128]{2,1,0:T(8,128)(2,1)S(1)}, bf16[8,128,128]{2,1,0:T(8,128)(2,1)S(1)}, u32[]{:S(2)}, u32[]{:S(2)}) collective-permute-start(bf16[8,128,128]{2,1,0:T(8,128)(2,1)S(1)} %collective-permute-done.7.rest_10_.rest_5_), channel_id=1, source_target_pairs={{0,16},{1,3},{2,18},{3,1},{16,0},{17,19},{18,2},{19,17},{4,20},{5,... | collective-permute-start | bytes 786440 | tf_op jit(solution)/shard_map/ppermute | solution.py:435
  57.8 0.5 collective-permute-start.18
  58.3 0.9 %near.1.rest_8_ = f32[280,128]{1,0:T(8,128)S(1)} custom-call(bf16[280,4096]{1,0:T(8,128)(2,1)S(1)} %bitcast.15, bf16[8,128,128]{2,1,0:T(8,128)(2,1)S(1)} %late.2.mine, bf16[8,128,128]{2,1,0:T(8,128)(2,1)S(1)} %collective-permute-done.8.other, bf16[8,128,128]{2,1,0:T(8,128)(2,1)S(1)} %collective-permute-done.9.rest_0_.rest_5_, ...), custom_call_target="tpu_custom_call" | custom-call | flops 600000000 | bytes 5242880 | tf_op jit(solution)/shard_map/near/pallas_call | solution.py:248
  59.2 1.0 %collective-permute-start.16 = (bf16[8,128,128]{2,1,0:T(8,128)(2,1)S(1)}, bf16[8,128,128]{2,1,0:T(8,128)(2,1)S(1)}, u32[]{:S(2)}, u32[]{:S(2)}) collective-permute-start(bf16[8,128,128]{2,1,0:T(8,128)(2,1)S(1)} %collective-permute-done.6.rest_13_.rest_0_), channel_id=1, source_target_pairs={{0,1},{1,0},{2,3},{3,2},{16,17},{17,16},{18,19},{19,18},{4,5},{5,4... | collective-permute-start | bytes 786440 | tf_op jit(solution)/shard_map/ppermute | solution.py:435
  60.2 0.0 collective-permute-start.13
  60.2 2.4 %collective-permute-done.14.rest_2_.rest_7_ = bf16[8,128,128]{2,1,0:T(8,128)(2,1)S(1)} collective-permute-done((bf16[8,128,128]{2,1,0:T(8,128)(2,1)S(1)}, bf16[8,128,128]{2,1,0:T(8,128)(2,1)S(1)}, u32[]{:S(2)}, u32[]{:S(2)}) %collective-permute-start.14) | collective-permute-done | bytes 262176 | tf_op jit(solution)/shard_map/ppermute | solution.py:435
  62.6 0.1 collective-permute-start.15
  62.8 1.8 %both.1 = (f32[280,128]{1,0:T(8,128)S(1)}, f32[280,128]{1,0:T(8,128)S(1)}) custom-call(bf16[280,4096]{1,0:T(8,128)(2,1)S(1)} %bitcast.16, bf16[8,128,128]{2,1,0:T(8,128)(2,1)S(1)} %collective-permute-done.10.rest_3_.rest_0_, bf16[8,128,128]{2,1,0:T(8,128)(2,1)S(1)} %collective-permute-done.12.rest_2_.rest_1_, ...), custom_call_target="tpu_custom_call" | custom-call | flops 600000000 | bytes 5242880 | tf_op jit(solution)/shard_map/both/pallas_call | solution.py:337
  64.6 1.3 %last.1 = (f32[280,128]{1,0:T(8,128)S(1)}, bf16[280,128]{1,0:T(8,128)(2,1)S(1)}, bf16[280,128]{1,0:T(8,128)(2,1)S(1)}, bf16[280,128]{1,0:T(8,128)(2,1)S(1)}) custom-call(bf16[280,4096]{1,0:T(8,128)(2,1)S(1)} %bitcast.17, bf16[8,128,128]{2,1,0:T(8,128)(2,1)S(1)} %collective-permute-done.6.rest_13_.rest_0_, ...), custom_call_target="tpu_custom_call" | custom-call | flops 600000000 | bytes 5242880 | tf_op jit(solution)/shard_map/last/pallas_call | solution.py:383
  65.9 2.5 %collective-permute-start.20 = (bf16[280,128]{1,0:T(8,128)(2,1)S(1)}, bf16[280,128]{1,0:T(8,128)(2,1)S(1)}, u32[]{:S(2)}, u32[]{:S(2)}) collective-permute-start(bf16[280,128]{1,0:T(8,128)(2,1)S(1)} %get-tuple-element.22), channel_id=1, source_target_pairs={{0,4},{4,0},{8,12},{12,8},{1,5},{5,1},{9,13},{13,9},{2,6},{6,2},{1... | collective-permute-start | bytes 215048 | tf_op jit(solution)/shard_map/ppermute | solution.py:425
  68.4 0.5 collective-permute-start.21
  68.9 2.0 %collective-permute-start.22 = (bf16[280,128]{1,0:T(8,128)(2,1)S(1)}, bf16[280,128]{1,0:T(8,128)(2,1)S(1)}, u32[]{:S(2)}, u32[]{:S(2)}) collective-permute-start(bf16[280,128]{1,0:T(8,128)(2,1)S(1)} %get-tuple-element.24), channel_id=1, source_target_pairs={{0,12},{4,8},{8,4},{12,0},{1,13},{5,9},{9,5},{13,1},{2,14},{6,10},... | collective-permute-start | bytes 215048 | tf_op jit(solution)/shard_map/ppermute | solution.py:425
  70.8 0.3 collective-permute-done.20
  71.2 5.3 %collective-permute-done.21 = bf16[280,128]{1,0:T(8,128)(2,1)S(1)} collective-permute-done((bf16[280,128]{1,0:T(8,128)(2,1)S(1)}, bf16[280,128]{1,0:T(8,128)(2,1)S(1)}, u32[]{:S(2)}, u32[]{:S(2)}) %collective-permute-start.21) | collective-permute-done | bytes 71712 | tf_op jit(solution)/shard_map/ppermute | solution.py:425
  76.5 0.7 add_bitcast_fusion
  (30 shorter events, 0.1 us)
Async XLA Ops:
  2.5 13.3 %collective-permute-start = (bf16[9,128,128]{2,1,0:T(8,128)(2,1)}, bf16[9,128,128]{2,1,0:T(8,128)(2,1)S(1)}, u32[]{:S(2)}, u32[]{:S(2)}) collective-permute-start(bf16[9,128,128]{2,1,0:T(8,128)(2,1)} %pack.2.rest_0_), channel_id=1, source_target_pairs={{0,12},{4,8},{8,4},{12,0},{1,13},{5,9},{9,5},{13,1},{2,14},{6,10},... | collective-permute-start | bytes 884744 | tf_op jit(solution)/shard_map/ppermute | solution.py:425
  7.6 15.7 %collective-permute-start.3 = (bf16[9,128,128]{2,1,0:T(8,128)(2,1)}, bf16[9,128,128]{2,1,0:T(8,128)(2,1)S(1)}, u32[]{:S(2)}, u32[]{:S(2)}) collective-permute-start(bf16[9,128,128]{2,1,0:T(8,128)(2,1)} %pack.2.rest_0_), channel_id=1, source_target_pairs={{0,4},{4,0},{8,12},{12,8},{1,5},{5,1},{9,13},{13,9},{2,6},{6,2},{1... | collective-permute-start | bytes 884744 | tf_op jit(solution)/shard_map/ppermute | solution.py:425
  7.6 2.6 %copy-start.7 = (s32[128,1]{0,1:T(1,128)S(1)}, s32[128,1]{0,1:T(1,128)}, u32[]{:S(2)}) copy-start(s32[128,1]{0,1:T(1,128)} %param.9) | copy-start | bytes 1540
  7.6 3.2 %copy-start.5 = (s32[128]{0:T(128)S(1)}, s32[128]{0:T(128)}, u32[]{:S(2)}) copy-start(s32[128]{0:T(128)} %param.8) | copy-start | bytes 1540
  7.6 3.2 %copy-start.6 = (s32[128]{0:T(128)S(1)}, s32[128]{0:T(128)}, u32[]{:S(2)}) copy-start(s32[128]{0:T(128)} %param.10) | copy-start | bytes 1540
  7.6 15.7 %copy-start.3 = (bf16[9,128,128]{2,1,0:T(8,128)(2,1)S(1)}, bf16[9,128,128]{2,1,0:T(8,128)(2,1)}, u32[]{:S(2)}) copy-start(bf16[9,128,128]{2,1,0:T(8,128)(2,1)} %pack.2.rest_0_) | copy-start | bytes 884740
  15.7 20.1 %collective-permute-start.2 = (bf16[9,128,128]{2,1,0:T(8,128)(2,1)}, bf16[9,128,128]{2,1,0:T(8,128)(2,1)S(1)}, u32[]{:S(2)}, u32[]{:S(2)}) collective-permute-start(bf16[9,128,128]{2,1,0:T(8,128)(2,1)} %pack.3.rest_0_), channel_id=1, source_target_pairs={{0,12},{4,8},{8,4},{12,0},{1,13},{5,9},{9,5},{13,1},{2,14},{6,10},... | collective-permute-start | bytes 884744 | tf_op jit(solution)/shard_map/ppermute | solution.py:425
  19.5 14.7 %collective-permute-start.4 = (bf16[9,128,128]{2,1,0:T(8,128)(2,1)S(1)}, bf16[9,128,128]{2,1,0:T(8,128)(2,1)S(1)}, u32[]{:S(2)}, u32[]{:S(2)}) collective-permute-start(bf16[9,128,128]{2,1,0:T(8,128)(2,1)S(1)} %collective-permute-done.rest_2_), channel_id=1, source_target_pairs={{0,4},{4,0},{8,12},{12,8},{1,5},{5,1},{9,13},{13,9},{2,6},{6,2},{1... | collective-permute-start | bytes 884744 | tf_op jit(solution)/shard_map/ppermute | solution.py:425
  23.2 18.8 %collective-permute-start.1 = (bf16[9,128,128]{2,1,0:T(8,128)(2,1)}, bf16[9,128,128]{2,1,0:T(8,128)(2,1)S(1)}, u32[]{:S(2)}, u32[]{:S(2)}) collective-permute-start(bf16[9,128,128]{2,1,0:T(8,128)(2,1)} %pack.3.rest_0_), channel_id=1, source_target_pairs={{0,4},{4,0},{8,12},{12,8},{1,5},{5,1},{9,13},{13,9},{2,6},{6,2},{1... | collective-permute-start | bytes 884744 | tf_op jit(solution)/shard_map/ppermute | solution.py:425
  23.3 2.2 %copy-start = (bf16[128,128,128]{2,1,0:T(8,128)(2,1)S(1)}, bf16[128,128,128]{2,1,0:T(8,128)(2,1)}, u32[]{:S(2)}) copy-start(bf16[128,128,128]{2,1,0:T(8,128)(2,1)} %weights.7) | copy-start | bytes 12582916
  25.5 8.7 %copy-start.1 = (bf16[128,128,128]{2,1,0:T(8,128)(2,1)S(1)}, bf16[128,128,128]{2,1,0:T(8,128)(2,1)}, u32[]{:S(2)}) copy-start(bf16[128,128,128]{2,1,0:T(8,128)(2,1)} %weights.7) | copy-start | bytes 12582916
  28.3 13.7 %copy-start.4 = (bf16[9,128,128]{2,1,0:T(8,128)(2,1)S(1)}, bf16[9,128,128]{2,1,0:T(8,128)(2,1)}, u32[]{:S(2)}) copy-start(bf16[9,128,128]{2,1,0:T(8,128)(2,1)} %pack.3.rest_0_) | copy-start | bytes 884740
  35.8 10.7 %collective-permute-start.5 = (bf16[9,128,128]{2,1,0:T(8,128)(2,1)S(1)}, bf16[9,128,128]{2,1,0:T(8,128)(2,1)S(1)}, u32[]{:S(2)}, u32[]{:S(2)}) collective-permute-start(bf16[9,128,128]{2,1,0:T(8,128)(2,1)S(1)} %collective-permute-done.2.rest_2_), channel_id=1, source_target_pairs={{0,4},{4,0},{8,12},{12,8},{1,5},{5,1},{9,13},{13,9},{2,6},{6,2},{1... | collective-permute-start | bytes 884744 | tf_op jit(solution)/shard_map/ppermute | solution.py:425
  39.0 10.7 %collective-permute-start.9 = (bf16[8,128,128]{2,1,0:T(8,128)(2,1)S(1)}, bf16[8,128,128]{2,1,0:T(8,128)(2,1)S(1)}, u32[]{:S(2)}, u32[]{:S(2)}) collective-permute-start(bf16[8,128,128]{2,1,0:T(8,128)(2,1)S(1)} %late.2.mine), channel_id=1, source_target_pairs={{0,2},{1,17},{2,0},{3,19},{16,18},{17,1},{18,16},{19,3},{4,6},{5,2... | collective-permute-start | bytes 786440 | tf_op jit(solution)/shard_map/ppermute | solution.py:435
  40.5 10.7 %collective-permute-start.10 = (bf16[8,128,128]{2,1,0:T(8,128)(2,1)S(1)}, bf16[8,128,128]{2,1,0:T(8,128)(2,1)S(1)}, u32[]{:S(2)}, u32[]{:S(2)}) collective-permute-start(bf16[8,128,128]{2,1,0:T(8,128)(2,1)S(1)} %late.2.mine), channel_id=1, source_target_pairs={{0,16},{1,3},{2,18},{3,1},{16,0},{17,19},{18,2},{19,17},{4,20},{5,... | collective-permute-start | bytes 786440 | tf_op jit(solution)/shard_map/ppermute | solution.py:435
  42.0 9.2 %collective-permute-start.8 = (bf16[8,128,128]{2,1,0:T(8,128)(2,1)S(1)}, bf16[8,128,128]{2,1,0:T(8,128)(2,1)S(1)}, u32[]{:S(2)}, u32[]{:S(2)}) collective-permute-start(bf16[8,128,128]{2,1,0:T(8,128)(2,1)S(1)} %late.2.mine), channel_id=1, source_target_pairs={{0,1},{1,0},{2,3},{3,2},{16,17},{17,16},{18,19},{19,18},{4,5},{5,4... | collective-permute-start | bytes 786440 | tf_op jit(solution)/shard_map/ppermute | solution.py:435
  44.8 13.5 %copy-start.2 = (bf16[8,35,4096]{2,0,1:T(8,128)(2,1)S(1)}, bf16[8,35,4096]{2,0,1:T(8,128)(2,1)}, u32[]{:S(2)}) copy-start(bf16[8,35,4096]{2,0,1:T(8,128)(2,1)} %param.6) | copy-start | bytes 6881284
  48.1 8.2 %collective-permute-start.7 = (bf16[8,128,128]{2,1,0:T(8,128)(2,1)S(1)}, bf16[8,128,128]{2,1,0:T(8,128)(2,1)S(1)}, u32[]{:S(2)}, u32[]{:S(2)}) collective-permute-start(bf16[8,128,128]{2,1,0:T(8,128)(2,1)S(1)} %late.3.rest_8_), channel_id=1, source_target_pairs={{0,2},{1,17},{2,0},{3,19},{16,18},{17,1},{18,16},{19,3},{4,6},{5,2... | collective-permute-start | bytes 786440 | tf_op jit(solution)/shard_map/ppermute | solution.py:435
  49.6 8.2 %collective-permute-start.12 = (bf16[8,128,128]{2,1,0:T(8,128)(2,1)S(1)}, bf16[8,128,128]{2,1,0:T(8,128)(2,1)S(1)}, u32[]{:S(2)}, u32[]{:S(2)}) collective-permute-start(bf16[8,128,128]{2,1,0:T(8,128)(2,1)S(1)} %collective-permute-done.9.rest_0_.rest_5_), channel_id=1, source_target_pairs={{0,1},{1,0},{2,3},{3,2},{16,17},{17,16},{18,19},{19,18},{4,5},{5,4... | collective-permute-start | bytes 786440 | tf_op jit(solution)/shard_map/ppermute | solution.py:435
  49.6 8.2 %collective-permute-start.17 = (bf16[8,128,128]{2,1,0:T(8,128)(2,1)S(1)}, bf16[8,128,128]{2,1,0:T(8,128)(2,1)S(1)}, u32[]{:S(2)}, u32[]{:S(2)}) collective-permute-start(bf16[8,128,128]{2,1,0:T(8,128)(2,1)S(1)} %collective-permute-done.9.rest_0_.rest_5_), channel_id=1, source_target_pairs={{0,16},{1,3},{2,18},{3,1},{16,0},{17,19},{18,2},{19,17},{4,20},{5,... | collective-permute-start | bytes 786440 | tf_op jit(solution)/shard_map/ppermute | solution.py:435
  51.2 7.2 %collective-permute-start.11 = (bf16[8,128,128]{2,1,0:T(8,128)(2,1)S(1)}, bf16[8,128,128]{2,1,0:T(8,128)(2,1)S(1)}, u32[]{:S(2)}, u32[]{:S(2)}) collective-permute-start(bf16[8,128,128]{2,1,0:T(8,128)(2,1)S(1)} %collective-permute-done.10.rest_3_.rest_0_), channel_id=1, source_target_pairs={{0,1},{1,0},{2,3},{3,2},{16,17},{17,16},{18,19},{19,18},{4,5},{5,4... | collective-permute-start | bytes 786440 | tf_op jit(solution)/shard_map/ppermute | solution.py:435
  51.2 8.1 %collective-permute-start.6 = (bf16[8,128,128]{2,1,0:T(8,128)(2,1)S(1)}, bf16[8,128,128]{2,1,0:T(8,128)(2,1)S(1)}, u32[]{:S(2)}, u32[]{:S(2)}) collective-permute-start(bf16[8,128,128]{2,1,0:T(8,128)(2,1)S(1)} %late.3.rest_8_), channel_id=1, source_target_pairs={{0,16},{1,3},{2,18},{3,1},{16,0},{17,19},{18,2},{19,17},{4,20},{5,... | collective-permute-start | bytes 786440 | tf_op jit(solution)/shard_map/ppermute | solution.py:435
  56.3 6.4 %collective-permute-start.14 = (bf16[8,128,128]{2,1,0:T(8,128)(2,1)S(1)}, bf16[8,128,128]{2,1,0:T(8,128)(2,1)S(1)}, u32[]{:S(2)}, u32[]{:S(2)}) collective-permute-start(bf16[8,128,128]{2,1,0:T(8,128)(2,1)S(1)} %collective-permute-done.7.rest_10_.rest_5_), channel_id=1, source_target_pairs={{0,16},{1,3},{2,18},{3,1},{16,0},{17,19},{18,2},{19,17},{4,20},{5,... | collective-permute-start | bytes 786440 | tf_op jit(solution)/shard_map/ppermute | solution.py:435
  57.8 5.0 %collective-permute-start.19 = (bf16[8,128,128]{2,1,0:T(8,128)(2,1)S(1)}, bf16[8,128,128]{2,1,0:T(8,128)(2,1)S(1)}, u32[]{:S(2)}, u32[]{:S(2)}) collective-permute-start(bf16[8,128,128]{2,1,0:T(8,128)(2,1)S(1)} %late.3.rest_8_), channel_id=1, source_target_pairs={{0,1},{1,0},{2,3},{3,2},{16,17},{17,16},{18,19},{19,18},{4,5},{5,4... | collective-permute-start | bytes 786440 | tf_op jit(solution)/shard_map/ppermute | solution.py:435
  57.8 5.0 %collective-permute-start.18 = (bf16[8,128,128]{2,1,0:T(8,128)(2,1)S(1)}, bf16[8,128,128]{2,1,0:T(8,128)(2,1)S(1)}, u32[]{:S(2)}, u32[]{:S(2)}) collective-permute-start(bf16[8,128,128]{2,1,0:T(8,128)(2,1)S(1)} %collective-permute-done.17.rest_2_.rest_7_), channel_id=1, source_target_pairs={{0,1},{1,0},{2,3},{3,2},{16,17},{17,16},{18,19},{19,18},{4,5},{5,4... | collective-permute-start | bytes 786440 | tf_op jit(solution)/shard_map/ppermute | solution.py:435
  59.2 3.5 %collective-permute-start.16 = (bf16[8,128,128]{2,1,0:T(8,128)(2,1)S(1)}, bf16[8,128,128]{2,1,0:T(8,128)(2,1)S(1)}, u32[]{:S(2)}, u32[]{:S(2)}) collective-permute-start(bf16[8,128,128]{2,1,0:T(8,128)(2,1)S(1)} %collective-permute-done.6.rest_13_.rest_0_), channel_id=1, source_target_pairs={{0,1},{1,0},{2,3},{3,2},{16,17},{17,16},{18,19},{19,18},{4,5},{5,4... | collective-permute-start | bytes 786440 | tf_op jit(solution)/shard_map/ppermute | solution.py:435
  60.2 2.5 %collective-permute-start.13 = (bf16[8,128,128]{2,1,0:T(8,128)(2,1)S(1)}, bf16[8,128,128]{2,1,0:T(8,128)(2,1)S(1)}, u32[]{:S(2)}, u32[]{:S(2)}) collective-permute-start(bf16[8,128,128]{2,1,0:T(8,128)(2,1)S(1)} %collective-permute-done.7.rest_10_.rest_5_), channel_id=1, source_target_pairs={{0,1},{1,0},{2,3},{3,2},{16,17},{17,16},{18,19},{19,18},{4,5},{5,4... | collective-permute-start | bytes 786440 | tf_op jit(solution)/shard_map/ppermute | solution.py:435
  62.6 2.0 %collective-permute-start.15 = (bf16[8,128,128]{2,1,0:T(8,128)(2,1)S(1)}, bf16[8,128,128]{2,1,0:T(8,128)(2,1)S(1)}, u32[]{:S(2)}, u32[]{:S(2)}) collective-permute-start(bf16[8,128,128]{2,1,0:T(8,128)(2,1)S(1)} %collective-permute-done.14.rest_2_.rest_7_), channel_id=1, source_target_pairs={{0,1},{1,0},{2,3},{3,2},{16,17},{17,16},{18,19},{19,18},{4,5},{5,4... | collective-permute-start | bytes 786440 | tf_op jit(solution)/shard_map/ppermute | solution.py:435
  65.9 5.2 %collective-permute-start.20 = (bf16[280,128]{1,0:T(8,128)(2,1)S(1)}, bf16[280,128]{1,0:T(8,128)(2,1)S(1)}, u32[]{:S(2)}, u32[]{:S(2)}) collective-permute-start(bf16[280,128]{1,0:T(8,128)(2,1)S(1)} %get-tuple-element.22), channel_id=1, source_target_pairs={{0,4},{4,0},{8,12},{12,8},{1,5},{5,1},{9,13},{13,9},{2,6},{6,2},{1... | collective-permute-start | bytes 215048 | tf_op jit(solution)/shard_map/ppermute | solution.py:425
  68.4 8.1 %collective-permute-start.21 = (bf16[280,128]{1,0:T(8,128)(2,1)S(1)}, bf16[280,128]{1,0:T(8,128)(2,1)S(1)}, u32[]{:S(2)}, u32[]{:S(2)}) collective-permute-start(bf16[280,128]{1,0:T(8,128)(2,1)S(1)} %get-tuple-element.23), channel_id=1, source_target_pairs={{0,8},{4,12},{8,0},{12,4},{1,9},{5,13},{9,1},{13,5},{2,10},{6,14},... | collective-permute-start | bytes 215048 | tf_op jit(solution)/shard_map/ppermute | solution.py:425
  68.9 7.6 %collective-permute-start.22 = (bf16[280,128]{1,0:T(8,128)(2,1)S(1)}, bf16[280,128]{1,0:T(8,128)(2,1)S(1)}, u32[]{:S(2)}, u32[]{:S(2)}) collective-permute-start(bf16[280,128]{1,0:T(8,128)(2,1)S(1)} %get-tuple-element.24), channel_id=1, source_target_pairs={{0,12},{4,8},{8,4},{12,0},{1,13},{5,9},{9,5},{13,1},{2,14},{6,10},... | collective-permute-start | bytes 215048 | tf_op jit(solution)/shard_map/ppermute | solution.py:425
